TPU v7x, 256 devices: a whole 4x4x8 slice. The times are simulated.
256 devices in a mesh: gx: 8 (over y, core), gy: 32 (over z, x).
Axes of the slice: x: 4, y: 4, z: 8, core: 2. Of those that a mesh axis runs over, the one named last changes fastest.
Arguments:
- displacement: float32 [3, 64, 256, 128], P(None, 'gx', 'gy'), may hold values from -0.12 to 0.12
- velocity: float32 [3, 64, 256, 128], P(None, 'gx', 'gy'), may hold values from -4 to 4
- intact: int32 [61, 64, 256, 128], P(None, 'gx', 'gy'), may hold values 0 or 1
- material: int32 [64, 256, 128], P('gx', 'gy'), may hold values from 0 to 7
- bulk_modulus: float32 [8], replicated, may hold values from 80 to 800
- shear_modulus: float32 [8], replicated, may hold values from 40 to 400
- density: float32 [8], replicated, may hold values from 1 to 4
Outputs:
- new_displacement: float32 [3, 64, 256, 128], P(None, 'gx', 'gy')
- new_velocity: float32 [3, 64, 256, 128], P(None, 'gx', 'gy')
- last_force: float32 [3, 64, 256, 128], P(None, 'gx', 'gy')
Inputs may be any that keep to these rules, and one draw needn't show every extreme that they name: intact[k, i] refers to the bond from node i to node i + e_k.
All inputs are finite; a program needn't handle non-finite values. No bound on the sum of `intact` on one device may be relied on, other than what follows from the above.
Results may differ from a plain program's by a relative error of at most 0.00002.
Values sent between devices are 32-bit elements; how exact they have to be, the bound alone decides.
No kernel may reach another device: no remote copies, remote signals or barrier semaphores. Data moves between devices by JAX's collectives and lax.ppermute only.
A program may use at most 64 MiB of HBM per device.

v0:
```python
import math

import jax
import jax.numpy as jnp
from jax import lax
from jax.sharding import PartitionSpec as P

STEPS = 2


time_step = 0.02


def extended_2(shard, sides, width):
    for axis, dim in sides:
        size, length = (lax.axis_size(axis), shard.shape[dim])
        up = [(i, (i + 1) % size) for i in range(size - 1)]
        down = [(j, i) for i, j in up]
        last = lax.slice_in_dim(shard, length - width, length, axis=dim)
        first = lax.slice_in_dim(shard, 0, width, axis=dim)
        before = lax.ppermute(last, axis, up)
        after = lax.ppermute(first, axis, down)
        shard = jnp.concatenate([before, shard, after], axis=dim)
    return shard


def passed_along(block, axis, distance):
    devices = range(lax.axis_size(axis))
    route = [(i - distance, i) for i in devices if i - distance in devices]
    return lax.ppermute(block, axis, route)


def half_offsets():
    result = []
    for along_x in range(-3, 4):
        for along_y in range(-3, 4):
            for along_z in range(-3, 4):
                if along_x * along_x + along_y * along_y + along_z * along_z <= 9 and (
                    along_x,
                    along_y,
                    along_z,
                ) > (0, 0, 0):
                    result.append((along_x, along_y, along_z))
    return result


def weighted_volume(offsets):
    return 2.0 * sum(
        (
            math.sqrt(float(offset[0] * offset[0] + offset[1] * offset[1] + offset[2] * offset[2]))
            for offset in offsets
        )
    )


def shift_depth(values, offset):
    if offset == 0:
        return values
    tile_depth = values.shape[-1]
    zeros_block = jnp.zeros(values.shape[:-1] + (abs(offset),), values.dtype)
    if offset > 0:
        return jnp.concatenate([values[..., offset:], zeros_block], -1)
    return jnp.concatenate([zeros_block, values[..., : tile_depth + offset]], -1)


def depth_inside(tile_depth, offset):
    positions = jnp.arange(tile_depth, dtype=jnp.int32) + offset
    return ((positions >= 0) & (positions < tile_depth)).astype(jnp.float32)


def extend_upper(side_extended, upper_rows, dimension):
    return jnp.concatenate([jnp.zeros_like(upper_rows), side_extended, upper_rows], dimension)


def fold_axis(halved, dimension, margin, interior):
    region = interior + 2 * margin - 6
    middle = lax.slice_in_dim(halved, 6, 6 + region, axis=dimension)
    low_part = lax.slice_in_dim(halved, 0, margin, axis=dimension)
    high_part = lax.slice_in_dim(
        halved, halved.shape[dimension] - margin, halved.shape[dimension], axis=dimension
    )
    low_padding = [(0, 0)] * halved.ndim
    low_padding[dimension] = (0, region - margin)
    high_padding = [(0, 0)] * halved.ndim
    high_padding[dimension] = (region - margin, 0)
    return middle + jnp.pad(low_part, low_padding) + jnp.pad(high_part, high_padding)


def fold_plane(halved, dimension, margin, tile_rows, tile_columns):
    return fold_axis(
        fold_axis(halved, dimension, margin, tile_rows), dimension + 1, margin, tile_columns
    )


def class_lookup(lookup_table, classes):
    class_numbers = jnp.arange(lookup_table.shape[0], dtype=jnp.int32)[:, None, None, None]
    return jnp.sum(
        jnp.where(classes[None] == class_numbers, lookup_table[:, None, None, None], 0.0), 0
    )


def plane_inside(tile_rows, tile_columns):
    row_position = lax.axis_index("gx") * tile_rows + jnp.arange(-3, tile_rows + 3, dtype=jnp.int32)
    column_position = lax.axis_index("gy") * tile_columns + jnp.arange(
        -3, tile_columns + 3, dtype=jnp.int32
    )
    row_inside = (row_position >= 0) & (row_position < tile_rows * lax.axis_size("gx"))
    column_inside = (column_position >= 0) & (column_position < tile_columns * lax.axis_size("gy"))
    return (row_inside[:, None] & column_inside[None, :]).astype(jnp.float32)


def tile_view(extended, offset, tile_rows, tile_columns):
    window = extended[
        ...,
        3 + offset[0] : 3 + offset[0] + tile_rows,
        3 + offset[1] : 3 + offset[1] + tile_columns,
        :,
    ]
    return shift_depth(window, offset[2])


def place_back(contribution, offset):
    sliding = shift_depth(contribution, -offset[2])
    leading = [(0, 0)] * (contribution.ndim - 3)
    return jnp.pad(
        sliding, leading + [(3 + offset[0], 3 - offset[0]), (3 + offset[1], 3 - offset[1]), (0, 0)]
    )


def bond_weight(flags, inside_plane, offset, tile_rows, tile_columns, tile_depth):
    plane = inside_plane[
        3 + offset[0] : 3 + offset[0] + tile_rows, 3 + offset[1] : 3 + offset[1] + tile_columns
    ]
    return (
        flags.astype(jnp.float32)
        * plane[:, :, None]
        * depth_inside(tile_depth, offset[2])[None, None, :]
    )


def bond_state(displacement_wide, own_motion, offset, tile_rows, tile_columns):
    partner = tile_view(displacement_wide, offset, tile_rows, tile_columns)
    radius = math.sqrt(float(offset[0] * offset[0] + offset[1] * offset[1] + offset[2] * offset[2]))
    components = [offset[number] + partner[number] - own_motion[number] for number in range(3)]
    length = jnp.sqrt(
        components[0] * components[0]
        + components[1] * components[1]
        + components[2] * components[2]
    )
    return (components, length, length - radius, radius)


def strain_partial(displacement_wide, intact, inside_plane, tile_rows, tile_columns, tile_depth):
    own_motion = displacement_wide[:, 3 : 3 + tile_rows, 3 : 3 + tile_columns, :]
    own_sum = jnp.zeros((tile_rows, tile_columns, tile_depth), jnp.float32)
    spread = jnp.zeros((tile_rows + 6, tile_columns + 6, tile_depth), jnp.float32)
    for bond_index, offset in enumerate(half_offsets()):
        components, length, stretch, radius = bond_state(
            displacement_wide, own_motion, offset, tile_rows, tile_columns
        )
        contribution = (
            bond_weight(
                intact[bond_index], inside_plane, offset, tile_rows, tile_columns, tile_depth
            )
            * stretch
        )
        own_sum = own_sum + contribution
        spread = spread + place_back(contribution, offset)
    return spread + jnp.pad(own_sum, ((3, 3), (3, 3), (0, 0)))


def force_partial(
    displacement_wide,
    dilatation_wide,
    bulk_wide,
    shear_wide,
    intact,
    inside_plane,
    volume,
    tile_rows,
    tile_columns,
    tile_depth,
):
    own_motion = displacement_wide[:, 3 : 3 + tile_rows, 3 : 3 + tile_columns, :]
    pressure_wide = bulk_wide * dilatation_wide
    twisting_wide = shear_wide * dilatation_wide
    own_pressure = pressure_wide[3 : 3 + tile_rows, 3 : 3 + tile_columns, :]
    own_twisting = twisting_wide[3 : 3 + tile_rows, 3 : 3 + tile_columns, :]
    own_shear = shear_wide[3 : 3 + tile_rows, 3 : 3 + tile_columns, :]
    own_force = jnp.zeros((3, tile_rows, tile_columns, tile_depth), jnp.float32)
    spread = jnp.zeros((3, tile_rows + 6, tile_columns + 6, tile_depth), jnp.float32)
    for bond_index, offset in enumerate(half_offsets()):
        components, length, stretch, radius = bond_state(
            displacement_wide, own_motion, offset, tile_rows, tile_columns
        )
        weight = bond_weight(
            intact[bond_index], inside_plane, offset, tile_rows, tile_columns, tile_depth
        )
        tension = (
            weight
            / radius
            * (
                3.0
                * radius
                / volume
                * (own_pressure + tile_view(pressure_wide, offset, tile_rows, tile_columns))
                + 15.0
                / volume
                * (
                    (own_shear + tile_view(shear_wide, offset, tile_rows, tile_columns)) * stretch
                    - radius
                    / 3.0
                    * (own_twisting + tile_view(twisting_wide, offset, tile_rows, tile_columns))
                )
            )
        )
        vector = jnp.stack([tension * component / length for component in components])
        own_force = own_force + vector
        spread = spread - place_back(vector, offset)
    return spread + jnp.pad(own_force, ((0, 0), (3, 3), (3, 3), (0, 0)))


def return_force(pushed, tile_rows, tile_columns):
    halved = extended_2(pushed, (("gx", 1), ("gy", 2)), 3)
    return fold_plane(halved, 1, 3, tile_rows, tile_columns)


def on_device(displacement, velocity, intact, material, bulk_modulus, shear_modulus, density):
    tile_rows, tile_columns, tile_depth = material.shape
    volume = weighted_volume(half_offsets())
    classes_side = extended_2(material, (("gy", 1),), 3)
    classes_next = passed_along(classes_side[:3], "gx", -1)
    classes_wide = extend_upper(classes_side, classes_next, 0)
    bulk_wide = class_lookup(bulk_modulus, classes_wide)
    shear_wide = class_lookup(shear_modulus, classes_wide)
    inertia_wide = class_lookup(density, classes_wide)
    inertia_tile = inertia_wide[3 : 3 + tile_rows, 3 : 3 + tile_columns, :]
    inside_plane = plane_inside(tile_rows, tile_columns)
    forces = jnp.zeros(displacement.shape, jnp.float32)
    for counter in range(STEPS):
        motion_side = extended_2(displacement, (("gy", 2),), 3)
        motion_next = passed_along(motion_side[:, :3], "gx", -1)
        displacement_wide = extend_upper(motion_side, motion_next, 1)
        partial_value = strain_partial(
            displacement_wide, intact, inside_plane, tile_rows, tile_columns, tile_depth
        )
        returned = extended_2(partial_value, (("gx", 0), ("gy", 1)), 3)
        dilatation = 3.0 / volume * fold_plane(returned, 0, 3, tile_rows, tile_columns)
        strain_side = extended_2(dilatation, (("gy", 1),), 3)
        strain_next = passed_along(strain_side[:3], "gx", -1)
        dilatation_wide = extend_upper(strain_side, strain_next, 0)
        pushed = force_partial(
            displacement_wide,
            dilatation_wide,
            bulk_wide,
            shear_wide,
            intact,
            inside_plane,
            volume,
            tile_rows,
            tile_columns,
            tile_depth,
        )
        forces = return_force(pushed, tile_rows, tile_columns)
        velocity = velocity + time_step * forces / inertia_tile
        displacement = displacement + time_step * velocity
    return (displacement, velocity, forces)


def solution(mesh):
    return jax.shard_map(
        on_device,
        mesh=mesh,
        in_specs=(
            P(None, "gx", "gy", None),
            P(None, "gx", "gy", None),
            P(None, "gx", "gy", None),
            P("gx", "gy", None),
            P(),
            P(),
            P(),
        ),
        out_specs=(P(None, "gx", "gy", None), P(None, "gx", "gy", None), P(None, "gx", "gy", None)),
        check_vma=False,
    )
```

profile of v0, /device:TPU:102, one launch (start us, length us, event | category | flops | bytes accessed | tf_op | source)
XLA Modules:
  0.0 198.9 jit_solution(13608460969834300098)
XLA Ops:
  1.5 4.9 %collective-permute-start = (s32[8,3,128]{2,1,0:T(4,128)S(1)}, s32[8,3,128]{2,1,0:T(4,128)S(1)}, u32[]{:S(2)}, u32[]{:S(2)}) collective-permute-start(s32[8,3,128]{2,1,0:T(4,128)S(1)} %get-tuple-element.1322), channel_id=1, source_target_pairs={{0,1},{1,2},{2,3},{3,4},{4,5},{5,6},{6,7},{7,8},{8,9},{9,10},{10,1... | collective-permute-start | bytes 36872 | tf_op jit(solution)/shard_map/ppermute | solution.py:21
  6.4 1.9 collective-permute-start.1
  9.4 7.2 %collective-permute-start.4 = (f32[3,8,3,128]{3,2,1,0:T(4,128)S(1)}, f32[3,8,3,128]{3,2,1,0:T(4,128)S(1)}, u32[]{:S(2)}, u32[]{:S(2)}) collective-permute-start(f32[3,8,3,128]{3,2,1,0:T(4,128)S(1)} %get-tuple-element.1311), channel_id=1, source_target_pairs={{0,1},{1,2},{2,3},{3,4},{4,5},{5,6},{6,7},{7,8},{8,9},{9,10},{10,1... | collective-permute-start | bytes 110600 | tf_op jit(solution)/shard_map/ppermute | solution.py:21
  16.6 1.9 collective-permute-start.3
  28.7 2.2 %collective-permute-done.5 = f32[3,3,14,128]{3,2,1,0:T(8,128)S(1)} collective-permute-done((f32[3,3,14,128]{3,2,1,0:T(8,128)S(1)}, f32[3,3,14,128]{3,2,1,0:T(8,128)S(1)}, u32[]{:S(2)}, u32[]{:S(2)}) %collective-permute-start.5) | collective-permute-done | bytes 64544 | tf_op jit(solution)/shard_map/ppermute | solution.py:30
  32.8 2.2 %add_add_fusion.3 = (f32[8,8,128]{2,1,0:T(8,128)S(1)}, f32[8,8,128]{2,1,0:T(8,128)S(1)}, f32[8,8,128]{2,1,0:T(8,128)S(1)}, f32[8,8,128]{2,1,0:T(8,128)S(1)}, f32...) fusion(f32[128]{0:T(128)S(1)} %get-tuple-element.1341, ...), kind=kLoop, calls=%fused_computation.2729 | loop fusion | flops 8142848 | bytes 12077312 | tf_op jit(solution)/shard_map/add | solution.py:167
  37.4 4.9 %collective-permute-start.6 = (f32[3,14,128]{2,1,0:T(8,128)S(1)}, f32[3,14,128]{2,1,0:T(8,128)S(1)}, u32[]{:S(2)}, u32[]{:S(2)}) collective-permute-start(f32[3,14,128]{2,1,0:T(8,128)S(1)} %get-tuple-element.1121), channel_id=1, source_target_pairs={{0,32},{32,64},{64,96},{96,128},{128,160},{160,192},{192,224},{1,3... | collective-permute-start | bytes 64520 | tf_op jit(solution)/shard_map/ppermute | solution.py:21
  45.4 7.2 %collective-permute-start.8 = (f32[20,3,128]{2,1,0:T(4,128)S(1)}, f32[20,3,128]{2,1,0:T(4,128)S(1)}, u32[]{:S(2)}, u32[]{:S(2)}) collective-permute-start(f32[20,3,128]{2,1,0:T(4,128)S(1)} %get-tuple-element.876), channel_id=1, source_target_pairs={{0,1},{1,2},{2,3},{3,4},{4,5},{5,6},{6,7},{7,8},{8,9},{9,10},{10,1... | collective-permute-start | bytes 92168 | tf_op jit(solution)/shard_map/ppermute | solution.py:21
  52.6 1.9 collective-permute-start.9
  54.7 7.1 %collective-permute-done.9 = f32[20,3,128]{2,1,0:T(4,128)S(1)} collective-permute-done((f32[20,3,128]{2,1,0:T(4,128)S(1)}, f32[20,3,128]{2,1,0:T(4,128)S(1)}, u32[]{:S(2)}, u32[]{:S(2)}) %collective-permute-start.9) | collective-permute-done | bytes 30752 | tf_op jit(solution)/shard_map/ppermute | solution.py:22
  62.1 1.9 collective-permute-start.10
  64.0 3.9 %collective-permute-start.11 = (f32[8,3,128]{2,1,0:T(4,128)S(1)}, f32[8,3,128]{2,1,0:T(4,128)S(1)}, u32[]{:S(2)}, u32[]{:S(2)}) collective-permute-start(f32[8,3,128]{2,1,0:T(4,128)S(1)} %get-tuple-element.1321), channel_id=1, source_target_pairs={{1,0},{2,1},{3,2},{4,3},{5,4},{6,5},{7,6},{8,7},{9,8},{10,9},{11,1... | collective-permute-start | bytes 36872 | tf_op jit(solution)/shard_map/ppermute | solution.py:22
  68.1 4.9 %collective-permute-done.11 = f32[8,3,128]{2,1,0:T(4,128)S(1)} collective-permute-done((f32[8,3,128]{2,1,0:T(4,128)S(1)}, f32[8,3,128]{2,1,0:T(4,128)S(1)}, u32[]{:S(2)}, u32[]{:S(2)}) %collective-permute-start.11) | collective-permute-done | bytes 12320 | tf_op jit(solution)/shard_map/ppermute | solution.py:22
  89.6 4.4 %collective-permute-start.13 = (f32[3,3,14,128]{3,2,1,0:T(8,128)S(1)}, f32[3,3,14,128]{3,2,1,0:T(8,128)S(1)}, u32[]{:S(2)}, u32[]{:S(2)}) collective-permute-start(f32[3,3,14,128]{3,2,1,0:T(8,128)S(1)} %get-tuple-element.598), channel_id=1, source_target_pairs={{0,32},{32,64},{64,96},{96,128},{128,160},{160,192},{192,224},{1,3... | collective-permute-start | bytes 193544 | tf_op jit(solution)/shard_map/ppermute | solution.py:21
  97.4 1.9 collective-permute-start.15
  99.3 3.9 %collective-permute-start.16 = (f32[3,20,3,128]{3,2,1,0:T(4,128)S(1)}, f32[3,20,3,128]{3,2,1,0:T(4,128)S(1)}, u32[]{:S(2)}, u32[]{:S(2)}) collective-permute-start(f32[3,20,3,128]{3,2,1,0:T(4,128)S(1)} %get-tuple-element.505), channel_id=1, source_target_pairs={{1,0},{2,1},{3,2},{4,3},{5,4},{6,5},{7,6},{8,7},{9,8},{10,9},{11,1... | collective-permute-start | bytes 276488 | tf_op jit(solution)/shard_map/ppermute | solution.py:22
  104.1 5.2 %collective-permute-done.16 = f32[3,20,3,128]{3,2,1,0:T(4,128)S(1)} collective-permute-done((f32[3,20,3,128]{3,2,1,0:T(4,128)S(1)}, f32[3,20,3,128]{3,2,1,0:T(4,128)S(1)}, u32[]{:S(2)}, u32[]{:S(2)}) %collective-permute-start.16) | collective-permute-done | bytes 92192 | tf_op jit(solution)/shard_map/ppermute | solution.py:22
  109.8 1.9 collective-permute-start.18
  111.7 3.9 %collective-permute-start.17 = (f32[3,8,3,128]{3,2,1,0:T(4,128)S(1)}, f32[3,8,3,128]{3,2,1,0:T(4,128)S(1)}, u32[]{:S(2)}, u32[]{:S(2)}) collective-permute-start(f32[3,8,3,128]{3,2,1,0:T(4,128)S(1)} %get-tuple-element.1310), channel_id=1, source_target_pairs={{1,0},{2,1},{3,2},{4,3},{5,4},{6,5},{7,6},{8,7},{9,8},{10,9},{11,1... | collective-permute-start | bytes 110600 | tf_op jit(solution)/shard_map/ppermute | solution.py:22
  116.0 5.2 %collective-permute-done.17 = f32[3,8,3,128]{3,2,1,0:T(4,128)S(1)} collective-permute-done((f32[3,8,3,128]{3,2,1,0:T(4,128)S(1)}, f32[3,8,3,128]{3,2,1,0:T(4,128)S(1)}, u32[]{:S(2)}, u32[]{:S(2)}) %collective-permute-start.17) | collective-permute-done | bytes 36896 | tf_op jit(solution)/shard_map/ppermute | solution.py:22
  125.1 3.0 %add_add_fusion.2 = (f32[8,8,128]{2,1,0:T(8,128)S(1)}, f32[8,8,128]{2,1,0:T(8,128)S(1)}, f32[8,8,128]{2,1,0:T(8,128)S(1)}, f32[8,8,128]{2,1,0:T(8,128)S(1)}, f32...) fusion(f32[128]{0:T(128)S(1)} %get-tuple-element.1341, ...), kind=kLoop, calls=%fused_computation.2390 | loop fusion | flops 8216576 | bytes 12073984 | tf_op jit(solution)/shard_map/add | solution.py:167
  130.4 5.7 %collective-permute-start.20 = (f32[3,14,128]{2,1,0:T(8,128)S(1)}, f32[3,14,128]{2,1,0:T(8,128)S(1)}, u32[]{:S(2)}, u32[]{:S(2)}) collective-permute-start(f32[3,14,128]{2,1,0:T(8,128)S(1)} %get-tuple-element.981), channel_id=1, source_target_pairs={{0,32},{32,64},{64,96},{96,128},{128,160},{160,192},{192,224},{1,3... | collective-permute-start | bytes 64520 | tf_op jit(solution)/shard_map/ppermute | solution.py:21
  139.2 1.9 collective-permute-start.22
  141.1 3.9 %collective-permute-start.23 = (f32[20,3,128]{2,1,0:T(4,128)S(1)}, f32[20,3,128]{2,1,0:T(4,128)S(1)}, u32[]{:S(2)}, u32[]{:S(2)}) collective-permute-start(f32[20,3,128]{2,1,0:T(4,128)S(1)} %get-tuple-element.875), channel_id=1, source_target_pairs={{1,0},{2,1},{3,2},{4,3},{5,4},{6,5},{7,6},{8,7},{9,8},{10,9},{11,1... | collective-permute-start | bytes 92168 | tf_op jit(solution)/shard_map/ppermute | solution.py:22
  145.1 5.2 %collective-permute-done.23 = f32[20,3,128]{2,1,0:T(4,128)S(1)} collective-permute-done((f32[20,3,128]{2,1,0:T(4,128)S(1)}, f32[20,3,128]{2,1,0:T(4,128)S(1)}, u32[]{:S(2)}, u32[]{:S(2)}) %collective-permute-start.23) | collective-permute-done | bytes 30752 | tf_op jit(solution)/shard_map/ppermute | solution.py:22
  150.6 1.9 collective-permute-start.24
  152.5 3.9 %collective-permute-start.25 = (f32[8,3,128]{2,1,0:T(4,128)S(1)}, f32[8,3,128]{2,1,0:T(4,128)S(1)}, u32[]{:S(2)}, u32[]{:S(2)}) collective-permute-start(f32[8,3,128]{2,1,0:T(4,128)S(1)} %get-tuple-element.1319), channel_id=1, source_target_pairs={{1,0},{2,1},{3,2},{4,3},{5,4},{6,5},{7,6},{8,7},{9,8},{10,9},{11,1... | collective-permute-start | bytes 36872 | tf_op jit(solution)/shard_map/ppermute | solution.py:22
  156.4 5.1 %collective-permute-done.25 = f32[8,3,128]{2,1,0:T(4,128)S(1)} collective-permute-done((f32[8,3,128]{2,1,0:T(4,128)S(1)}, f32[8,3,128]{2,1,0:T(4,128)S(1)}, u32[]{:S(2)}, u32[]{:S(2)}) %collective-permute-start.25) | collective-permute-done | bytes 12320 | tf_op jit(solution)/shard_map/ppermute | solution.py:22
  178.4 4.2 %collective-permute-start.27 = (f32[3,3,14,128]{3,2,1,0:T(8,128)S(1)}, f32[3,3,14,128]{3,2,1,0:T(8,128)S(1)}, u32[]{:S(2)}, u32[]{:S(2)}) collective-permute-start(f32[3,3,14,128]{3,2,1,0:T(8,128)S(1)} %get-tuple-element.596), channel_id=1, source_target_pairs={{0,32},{32,64},{64,96},{96,128},{128,160},{160,192},{192,224},{1,3... | collective-permute-start | bytes 193544 | tf_op jit(solution)/shard_map/ppermute | solution.py:21
  185.8 1.9 collective-permute-start.29
  187.7 3.9 %collective-permute-start.30 = (f32[3,20,3,128]{3,2,1,0:T(4,128)S(1)}, f32[3,20,3,128]{3,2,1,0:T(4,128)S(1)}, u32[]{:S(2)}, u32[]{:S(2)}) collective-permute-start(f32[3,20,3,128]{3,2,1,0:T(4,128)S(1)} %get-tuple-element.503), channel_id=1, source_target_pairs={{1,0},{2,1},{3,2},{4,3},{5,4},{6,5},{7,6},{8,7},{9,8},{10,9},{11,1... | collective-permute-start | bytes 276488 | tf_op jit(solution)/shard_map/ppermute | solution.py:22
  192.6 5.2 %collective-permute-done.30 = f32[3,20,3,128]{3,2,1,0:T(4,128)S(1)} collective-permute-done((f32[3,20,3,128]{3,2,1,0:T(4,128)S(1)}, f32[3,20,3,128]{3,2,1,0:T(4,128)S(1)}, u32[]{:S(2)}, u32[]{:S(2)}) %collective-permute-start.30) | collective-permute-done | bytes 92192 | tf_op jit(solution)/shard_map/ppermute | solution.py:22
  (476 shorter events, 70.7 us)
Async XLA Ops:
  0.6 26.4 %copy-start = (f32[3,8,8,128]{3,2,1,0:T(8,128)S(1)}, f32[3,8,8,128]{3,2,1,0:T(8,128)}, u32[]{:S(2)}) copy-start(f32[3,8,8,128]{3,2,1,0:T(8,128)} %param.7) | copy-start | bytes 294916
  1.5 18.1 %collective-permute-start = (s32[8,3,128]{2,1,0:T(4,128)S(1)}, s32[8,3,128]{2,1,0:T(4,128)S(1)}, u32[]{:S(2)}, u32[]{:S(2)}) collective-permute-start(s32[8,3,128]{2,1,0:T(4,128)S(1)} %get-tuple-element.1322), channel_id=1, source_target_pairs={{0,1},{1,2},{2,3},{3,4},{4,5},{5,6},{6,7},{7,8},{8,9},{9,10},{10,1... | collective-permute-start | bytes 36872 | tf_op jit(solution)/shard_map/ppermute | solution.py:21
  6.4 13.2 %collective-permute-start.1 = (s32[8,3,128]{2,1,0:T(4,128)S(1)}, s32[8,3,128]{2,1,0:T(4,128)S(1)}, u32[]{:S(2)}, u32[]{:S(2)}) collective-permute-start(s32[8,3,128]{2,1,0:T(4,128)S(1)} %get-tuple-element.1323), channel_id=1, source_target_pairs={{1,0},{2,1},{3,2},{4,3},{5,4},{6,5},{7,6},{8,7},{9,8},{10,9},{11,1... | collective-permute-start | bytes 36872 | tf_op jit(solution)/shard_map/ppermute | solution.py:22
  9.4 17.7 %collective-permute-start.4 = (f32[3,8,3,128]{3,2,1,0:T(4,128)S(1)}, f32[3,8,3,128]{3,2,1,0:T(4,128)S(1)}, u32[]{:S(2)}, u32[]{:S(2)}) collective-permute-start(f32[3,8,3,128]{3,2,1,0:T(4,128)S(1)} %get-tuple-element.1311), channel_id=1, source_target_pairs={{0,1},{1,2},{2,3},{3,4},{4,5},{5,6},{6,7},{7,8},{8,9},{9,10},{10,1... | collective-permute-start | bytes 110600 | tf_op jit(solution)/shard_map/ppermute | solution.py:21
  16.6 10.4 %collective-permute-start.3 = (f32[3,8,3,128]{3,2,1,0:T(4,128)S(1)}, f32[3,8,3,128]{3,2,1,0:T(4,128)S(1)}, u32[]{:S(2)}, u32[]{:S(2)}) collective-permute-start(f32[3,8,3,128]{3,2,1,0:T(4,128)S(1)} %get-tuple-element.1312), channel_id=1, source_target_pairs={{1,0},{2,1},{3,2},{4,3},{5,4},{6,5},{7,6},{8,7},{9,8},{10,9},{11,1... | collective-permute-start | bytes 110600 | tf_op jit(solution)/shard_map/ppermute | solution.py:22
  20.4 4.3 %collective-permute-start.2 = (s32[3,14,128]{2,1,0:T(8,128)S(1)}, s32[3,14,128]{2,1,0:T(8,128)S(1)}, u32[]{:S(2)}, u32[]{:S(2)}) collective-permute-start(s32[3,14,128]{2,1,0:T(8,128)S(1)} %pad_add_fusion.140), channel_id=1, source_target_pairs={{32,0},{64,32},{96,64},{128,96},{160,128},{192,160},{224,192},{33,... | collective-permute-start | bytes 64520 | tf_op jit(solution)/shard_map/ppermute | solution.py:30
  27.1 3.8 %collective-permute-start.5 = (f32[3,3,14,128]{3,2,1,0:T(8,128)S(1)}, f32[3,3,14,128]{3,2,1,0:T(8,128)S(1)}, u32[]{:S(2)}, u32[]{:S(2)}) collective-permute-start(f32[3,3,14,128]{3,2,1,0:T(8,128)S(1)} %pad_maximum_fusion.138), channel_id=1, source_target_pairs={{32,0},{64,32},{96,64},{128,96},{160,128},{192,160},{224,192},{33,... | collective-permute-start | bytes 193544 | tf_op jit(solution)/shard_map/ppermute | solution.py:30
  37.4 6.4 %collective-permute-start.6 = (f32[3,14,128]{2,1,0:T(8,128)S(1)}, f32[3,14,128]{2,1,0:T(8,128)S(1)}, u32[]{:S(2)}, u32[]{:S(2)}) collective-permute-start(f32[3,14,128]{2,1,0:T(8,128)S(1)} %get-tuple-element.1121), channel_id=1, source_target_pairs={{0,32},{32,64},{64,96},{96,128},{128,160},{160,192},{192,224},{1,3... | collective-permute-start | bytes 64520 | tf_op jit(solution)/shard_map/ppermute | solution.py:21
  42.3 3.1 %collective-permute-start.7 = (f32[3,14,128]{2,1,0:T(8,128)S(1)}, f32[3,14,128]{2,1,0:T(8,128)S(1)}, u32[]{:S(2)}, u32[]{:S(2)}) collective-permute-start(f32[3,14,128]{2,1,0:T(8,128)S(1)} %get-tuple-element.1122), channel_id=1, source_target_pairs={{32,0},{64,32},{96,64},{128,96},{160,128},{192,160},{224,192},{33,... | collective-permute-start | bytes 64520 | tf_op jit(solution)/shard_map/ppermute | solution.py:22
  45.4 9.3 %collective-permute-start.8 = (f32[20,3,128]{2,1,0:T(4,128)S(1)}, f32[20,3,128]{2,1,0:T(4,128)S(1)}, u32[]{:S(2)}, u32[]{:S(2)}) collective-permute-start(f32[20,3,128]{2,1,0:T(4,128)S(1)} %get-tuple-element.876), channel_id=1, source_target_pairs={{0,1},{1,2},{2,3},{3,4},{4,5},{5,6},{6,7},{7,8},{8,9},{9,10},{10,1... | collective-permute-start | bytes 92168 | tf_op jit(solution)/shard_map/ppermute | solution.py:21
  52.6 9.2 %collective-permute-start.9 = (f32[20,3,128]{2,1,0:T(4,128)S(1)}, f32[20,3,128]{2,1,0:T(4,128)S(1)}, u32[]{:S(2)}, u32[]{:S(2)}) collective-permute-start(f32[20,3,128]{2,1,0:T(4,128)S(1)} %get-tuple-element.877), channel_id=1, source_target_pairs={{1,0},{2,1},{3,2},{4,3},{5,4},{6,5},{7,6},{8,7},{9,8},{10,9},{11,1... | collective-permute-start | bytes 92168 | tf_op jit(solution)/shard_map/ppermute | solution.py:22
  62.1 6.0 %collective-permute-start.10 = (f32[8,3,128]{2,1,0:T(4,128)S(1)}, f32[8,3,128]{2,1,0:T(4,128)S(1)}, u32[]{:S(2)}, u32[]{:S(2)}) collective-permute-start(f32[8,3,128]{2,1,0:T(4,128)S(1)} %get-tuple-element.1320), channel_id=1, source_target_pairs={{0,1},{1,2},{2,3},{3,4},{4,5},{5,6},{6,7},{7,8},{8,9},{9,10},{10,1... | collective-permute-start | bytes 36872 | tf_op jit(solution)/shard_map/ppermute | solution.py:21
  64.0 9.0 %collective-permute-start.11 = (f32[8,3,128]{2,1,0:T(4,128)S(1)}, f32[8,3,128]{2,1,0:T(4,128)S(1)}, u32[]{:S(2)}, u32[]{:S(2)}) collective-permute-start(f32[8,3,128]{2,1,0:T(4,128)S(1)} %get-tuple-element.1321), channel_id=1, source_target_pairs={{1,0},{2,1},{3,2},{4,3},{5,4},{6,5},{7,6},{8,7},{9,8},{10,9},{11,1... | collective-permute-start | bytes 36872 | tf_op jit(solution)/shard_map/ppermute | solution.py:22
  73.0 3.1 %collective-permute-start.12 = (f32[3,14,128]{2,1,0:T(8,128)S(1)}, f32[3,14,128]{2,1,0:T(8,128)S(1)}, u32[]{:S(2)}, u32[]{:S(2)}) collective-permute-start(f32[3,14,128]{2,1,0:T(8,128)S(1)} %pad_maximum_fusion.149), channel_id=1, source_target_pairs={{32,0},{64,32},{96,64},{128,96},{160,128},{192,160},{224,192},{33,... | collective-permute-start | bytes 64520 | tf_op jit(solution)/shard_map/ppermute | solution.py:30
  89.6 5.9 %collective-permute-start.13 = (f32[3,3,14,128]{3,2,1,0:T(8,128)S(1)}, f32[3,3,14,128]{3,2,1,0:T(8,128)S(1)}, u32[]{:S(2)}, u32[]{:S(2)}) collective-permute-start(f32[3,3,14,128]{3,2,1,0:T(8,128)S(1)} %get-tuple-element.598), channel_id=1, source_target_pairs={{0,32},{32,64},{64,96},{96,128},{128,160},{160,192},{192,224},{1,3... | collective-permute-start | bytes 193544 | tf_op jit(solution)/shard_map/ppermute | solution.py:21
  94.0 3.3 %collective-permute-start.14 = (f32[3,3,14,128]{3,2,1,0:T(8,128)S(1)}, f32[3,3,14,128]{3,2,1,0:T(8,128)S(1)}, u32[]{:S(2)}, u32[]{:S(2)}) collective-permute-start(f32[3,3,14,128]{3,2,1,0:T(8,128)S(1)} %get-tuple-element.599), channel_id=1, source_target_pairs={{32,0},{64,32},{96,64},{128,96},{160,128},{192,160},{224,192},{33,... | collective-permute-start | bytes 193544 | tf_op jit(solution)/shard_map/ppermute | solution.py:22
  97.4 6.8 %collective-permute-start.15 = (f32[3,20,3,128]{3,2,1,0:T(4,128)S(1)}, f32[3,20,3,128]{3,2,1,0:T(4,128)S(1)}, u32[]{:S(2)}, u32[]{:S(2)}) collective-permute-start(f32[3,20,3,128]{3,2,1,0:T(4,128)S(1)} %get-tuple-element.504), channel_id=1, source_target_pairs={{0,1},{1,2},{2,3},{3,4},{4,5},{5,6},{6,7},{7,8},{8,9},{9,10},{10,1... | collective-permute-start | bytes 276488 | tf_op jit(solution)/shard_map/ppermute | solution.py:21
  99.3 10.1 %collective-permute-start.16 = (f32[3,20,3,128]{3,2,1,0:T(4,128)S(1)}, f32[3,20,3,128]{3,2,1,0:T(4,128)S(1)}, u32[]{:S(2)}, u32[]{:S(2)}) collective-permute-start(f32[3,20,3,128]{3,2,1,0:T(4,128)S(1)} %get-tuple-element.505), channel_id=1, source_target_pairs={{1,0},{2,1},{3,2},{4,3},{5,4},{6,5},{7,6},{8,7},{9,8},{10,9},{11,1... | collective-permute-start | bytes 276488 | tf_op jit(solution)/shard_map/ppermute | solution.py:22
  109.8 6.2 %collective-permute-start.18 = (f32[3,8,3,128]{3,2,1,0:T(4,128)S(1)}, f32[3,8,3,128]{3,2,1,0:T(4,128)S(1)}, u32[]{:S(2)}, u32[]{:S(2)}) collective-permute-start(f32[3,8,3,128]{3,2,1,0:T(4,128)S(1)} %get-tuple-element.1309), channel_id=1, source_target_pairs={{0,1},{1,2},{2,3},{3,4},{4,5},{5,6},{6,7},{7,8},{8,9},{9,10},{10,1... | collective-permute-start | bytes 110600 | tf_op jit(solution)/shard_map/ppermute | solution.py:21
  111.7 9.5 %collective-permute-start.17 = (f32[3,8,3,128]{3,2,1,0:T(4,128)S(1)}, f32[3,8,3,128]{3,2,1,0:T(4,128)S(1)}, u32[]{:S(2)}, u32[]{:S(2)}) collective-permute-start(f32[3,8,3,128]{3,2,1,0:T(4,128)S(1)} %get-tuple-element.1310), channel_id=1, source_target_pairs={{1,0},{2,1},{3,2},{4,3},{5,4},{6,5},{7,6},{8,7},{9,8},{10,9},{11,1... | collective-permute-start | bytes 110600 | tf_op jit(solution)/shard_map/ppermute | solution.py:22
  121.2 3.2 %collective-permute-start.19 = (f32[3,3,14,128]{3,2,1,0:T(8,128)S(1)}, f32[3,3,14,128]{3,2,1,0:T(8,128)S(1)}, u32[]{:S(2)}, u32[]{:S(2)}) collective-permute-start(f32[3,3,14,128]{3,2,1,0:T(8,128)S(1)} %pad_maximum_fusion.136), channel_id=1, source_target_pairs={{32,0},{64,32},{96,64},{128,96},{160,128},{192,160},{224,192},{33,... | collective-permute-start | bytes 193544 | tf_op jit(solution)/shard_map/ppermute | solution.py:30
  130.4 7.0 %collective-permute-start.20 = (f32[3,14,128]{2,1,0:T(8,128)S(1)}, f32[3,14,128]{2,1,0:T(8,128)S(1)}, u32[]{:S(2)}, u32[]{:S(2)}) collective-permute-start(f32[3,14,128]{2,1,0:T(8,128)S(1)} %get-tuple-element.981), channel_id=1, source_target_pairs={{0,32},{32,64},{64,96},{96,128},{128,160},{160,192},{192,224},{1,3... | collective-permute-start | bytes 64520 | tf_op jit(solution)/shard_map/ppermute | solution.py:21
  136.1 3.1 %collective-permute-start.21 = (f32[3,14,128]{2,1,0:T(8,128)S(1)}, f32[3,14,128]{2,1,0:T(8,128)S(1)}, u32[]{:S(2)}, u32[]{:S(2)}) collective-permute-start(f32[3,14,128]{2,1,0:T(8,128)S(1)} %get-tuple-element.982), channel_id=1, source_target_pairs={{32,0},{64,32},{96,64},{128,96},{160,128},{192,160},{224,192},{33,... | collective-permute-start | bytes 64520 | tf_op jit(solution)/shard_map/ppermute | solution.py:22
  139.2 5.9 %collective-permute-start.22 = (f32[20,3,128]{2,1,0:T(4,128)S(1)}, f32[20,3,128]{2,1,0:T(4,128)S(1)}, u32[]{:S(2)}, u32[]{:S(2)}) collective-permute-start(f32[20,3,128]{2,1,0:T(4,128)S(1)} %get-tuple-element.874), channel_id=1, source_target_pairs={{0,1},{1,2},{2,3},{3,4},{4,5},{5,6},{6,7},{7,8},{8,9},{9,10},{10,1... | collective-permute-start | bytes 92168 | tf_op jit(solution)/shard_map/ppermute | solution.py:21
  141.1 9.2 %collective-permute-start.23 = (f32[20,3,128]{2,1,0:T(4,128)S(1)}, f32[20,3,128]{2,1,0:T(4,128)S(1)}, u32[]{:S(2)}, u32[]{:S(2)}) collective-permute-start(f32[20,3,128]{2,1,0:T(4,128)S(1)} %get-tuple-element.875), channel_id=1, source_target_pairs={{1,0},{2,1},{3,2},{4,3},{5,4},{6,5},{7,6},{8,7},{9,8},{10,9},{11,1... | collective-permute-start | bytes 92168 | tf_op jit(solution)/shard_map/ppermute | solution.py:22
  150.6 5.9 %collective-permute-start.24 = (f32[8,3,128]{2,1,0:T(4,128)S(1)}, f32[8,3,128]{2,1,0:T(4,128)S(1)}, u32[]{:S(2)}, u32[]{:S(2)}) collective-permute-start(f32[8,3,128]{2,1,0:T(4,128)S(1)} %get-tuple-element.1318), channel_id=1, source_target_pairs={{0,1},{1,2},{2,3},{3,4},{4,5},{5,6},{6,7},{7,8},{8,9},{9,10},{10,1... | collective-permute-start | bytes 36872 | tf_op jit(solution)/shard_map/ppermute | solution.py:21
  152.5 9.1 %collective-permute-start.25 = (f32[8,3,128]{2,1,0:T(4,128)S(1)}, f32[8,3,128]{2,1,0:T(4,128)S(1)}, u32[]{:S(2)}, u32[]{:S(2)}) collective-permute-start(f32[8,3,128]{2,1,0:T(4,128)S(1)} %get-tuple-element.1319), channel_id=1, source_target_pairs={{1,0},{2,1},{3,2},{4,3},{5,4},{6,5},{7,6},{8,7},{9,8},{10,9},{11,1... | collective-permute-start | bytes 36872 | tf_op jit(solution)/shard_map/ppermute | solution.py:22
  161.6 3.1 %collective-permute-start.26 = (f32[3,14,128]{2,1,0:T(8,128)S(1)}, f32[3,14,128]{2,1,0:T(8,128)S(1)}, u32[]{:S(2)}, u32[]{:S(2)}) collective-permute-start(f32[3,14,128]{2,1,0:T(8,128)S(1)} %pad_maximum_fusion.147), channel_id=1, source_target_pairs={{32,0},{64,32},{96,64},{128,96},{160,128},{192,160},{224,192},{33,... | collective-permute-start | bytes 64520 | tf_op jit(solution)/shard_map/ppermute | solution.py:30
  178.4 5.5 %collective-permute-start.27 = (f32[3,3,14,128]{3,2,1,0:T(8,128)S(1)}, f32[3,3,14,128]{3,2,1,0:T(8,128)S(1)}, u32[]{:S(2)}, u32[]{:S(2)}) collective-permute-start(f32[3,3,14,128]{3,2,1,0:T(8,128)S(1)} %get-tuple-element.596), channel_id=1, source_target_pairs={{0,32},{32,64},{64,96},{96,128},{128,160},{160,192},{192,224},{1,3... | collective-permute-start | bytes 193544 | tf_op jit(solution)/shard_map/ppermute | solution.py:21
  182.6 3.2 %collective-permute-start.28 = (f32[3,3,14,128]{3,2,1,0:T(8,128)S(1)}, f32[3,3,14,128]{3,2,1,0:T(8,128)S(1)}, u32[]{:S(2)}, u32[]{:S(2)}) collective-permute-start(f32[3,3,14,128]{3,2,1,0:T(8,128)S(1)} %get-tuple-element.597), channel_id=1, source_target_pairs={{32,0},{64,32},{96,64},{128,96},{160,128},{192,160},{224,192},{33,... | collective-permute-start | bytes 193544 | tf_op jit(solution)/shard_map/ppermute | solution.py:22
  185.8 6.8 %collective-permute-start.29 = (f32[3,20,3,128]{3,2,1,0:T(4,128)S(1)}, f32[3,20,3,128]{3,2,1,0:T(4,128)S(1)}, u32[]{:S(2)}, u32[]{:S(2)}) collective-permute-start(f32[3,20,3,128]{3,2,1,0:T(4,128)S(1)} %get-tuple-element.502), channel_id=1, source_target_pairs={{0,1},{1,2},{2,3},{3,4},{4,5},{5,6},{6,7},{7,8},{8,9},{9,10},{10,1... | collective-permute-start | bytes 276488 | tf_op jit(solution)/shard_map/ppermute | solution.py:21
  187.7 10.1 %collective-permute-start.30 = (f32[3,20,3,128]{3,2,1,0:T(4,128)S(1)}, f32[3,20,3,128]{3,2,1,0:T(4,128)S(1)}, u32[]{:S(2)}, u32[]{:S(2)}) collective-permute-start(f32[3,20,3,128]{3,2,1,0:T(4,128)S(1)} %get-tuple-element.503), channel_id=1, source_target_pairs={{1,0},{2,1},{3,2},{4,3},{5,4},{6,5},{7,6},{8,7},{9,8},{10,9},{11,1... | collective-permute-start | bytes 276488 | tf_op jit(solution)/shard_map/ppermute | solution.py:22
  (3 other events, 41.8 us)
where the time goes:
time: 202 us; the launch traced here: 199 us
  starting transfers between devices  91.6 us (45%)
  waiting for transfers between devices  54.1 us (27%)
  other arithmetic  31.3 us (15%)
  local copies, waits for them, and re-layouts  18.8 us (9%)
  between operations  3.19 us (2%)
    ppermute x13, starting transfers between devices, extended_2(): before = lax.ppermute(last, axis, up)  50.1 us
    ppermute x13, waiting for transfers between devices, extended_2(): after = lax.ppermute(first, axis, down)  45.2 us
    ppermute x13, starting transfers between devices, extended_2(): after = lax.ppermute(first, axis, down)  34.6 us
    another operation x250, other arithmetic, force_partial(): jnp.stack([tension * component / length for component in components])  14.5 us
    slice x113, local copies, waits for them, and re-layouts, shift_depth(): return jnp.concatenate([values[..., offset:], zeros_block], -1)  13.7 us
    ppermute x5, starting transfers between devices, passed_along(): return lax.ppermute(block, axis, route)  6.85 us
    ppermute x5, waiting for transfers between devices, passed_along(): return lax.ppermute(block, axis, route)  6.71 us
    add x2, other arithmetic, strain_partial(): own_sum = own_sum + contribution  5.15 us
  transfers between devices with their start and end apart: 31, of which 18 were waited for; matrix products, arithmetic and copies ran while one was open for 5% of the time, Pallas kernels for 0%

commit v1 on v0

v1 whole, which is shorter than its diff:
```python
import functools
import math

import jax
import jax.numpy as jnp
from jax import lax
from jax.experimental import pallas as pl
from jax.experimental.pallas import tpu as pltpu
from jax.sharding import PartitionSpec as P

STEPS = 2
TIME_STEP = 0.02
F32 = jnp.float32
CLASSES = 8

OFFSETS = [
    (a, b, c)
    for a in range(-3, 4)
    for b in range(-3, 4)
    for c in range(-3, 4)
    if a * a + b * b + c * c <= 9 and (a, b, c) > (0, 0, 0)
]
INDEX = {offset: k for k, offset in enumerate(OFFSETS)}
VOLUME = 2.0 * sum(math.sqrt(float(a * a + b * b + c * c)) for a, b, c in OFFSETS)


def directed(b):
    return [
        (a, c)
        for a in range(-3, 4)
        for c in range(-3, 4)
        if 0 < a * a + b * b + c * c <= 9
    ]


FLAG_BASE, _row = [], 0
for _a, _b, _c in OFFSETS:
    FLAG_BASE.append(_row)
    _row += 8 * (8 + _a)
FLAG_ROWS = _row

X_FLAG, _row = {}, 96
for _k, (_a, _b, _c) in enumerate(OFFSETS):
    if _a:
        X_FLAG[_k] = _row
        _row += 8 * _a
X_UP_ROWS, X_DOWN_ROWS = _row, 96

Y_SUM, Y_MATERIAL, Y_FLAGS = 144, 168, 216
Y_UP_FLAG, Y_DOWN_FLAG, _up, _down = {}, {}, Y_FLAGS, Y_FLAGS
for _k, (_a, _b, _c) in enumerate(OFFSETS):
    if _b > 0:
        Y_UP_FLAG[_k] = _up
        _up += _b * (8 + _a)
    elif _b < 0:
        Y_DOWN_FLAG[_k] = _down
        _down += -_b * (8 + _a)
Y_UP_ROWS, Y_DOWN_ROWS = -(-_up // 8) * 8, -(-_down // 8) * 8


def rows(start, count=8):
    return pl.ds(start, count)


def copy_rows(target, to, source, at, count):
    done = 0
    while done < count:
        size = min(8, count - done)
        target[rows(to + done, size), :] = source[rows(at + done, size), :]
        done += size


def roll(value, shift):
    return value if shift % 128 == 0 else pltpu.roll(value, shift % 128, 1)


def pack_first(u, material, intact, up, down):
    for n in range(3):
        up[24 * n : 24 * n + 24, :] = u[64 * n + 40 : 64 * n + 64, :]
        down[24 * n : 24 * n + 24, :] = u[64 * n : 64 * n + 24, :]
    up[72:96, :] = material[40:64, :].astype(F32)
    down[72:96, :] = material[0:24, :].astype(F32)
    for k, base in X_FLAG.items():
        a = OFFSETS[k][0]
        up[base : base + 8 * a, :] = intact[64 * k + 64 - 8 * a : 64 * k + 64, :].astype(F32)


def widen(target, base, own, own_base, below, above, at):
    for x in range(-3, 11):
        if x < 0:
            tile = below[at + 8 * (x + 3) : at + 8 * (x + 3) + 8, :]
        elif x < 8:
            tile = own[own_base + 8 * x : own_base + 8 * x + 8, :].astype(F32)
        else:
            tile = above[at + 8 * (x - 8) : at + 8 * (x - 8) + 8, :]
        target[pl.ds(base + x + 3, 8, stride=16), :] = tile
    for x in (14, 15):
        target[pl.ds(base + x, 8, stride=16), :] = jnp.zeros((8, 128), F32)


def shifted_row(field, fields, c, column):
    return ((c + 3) * fields + field) * 224 + (column + 3) * 16


def store_shifts(target, field, fields, column, half, tile, along_z):
    for c in range(-3, 4):
        value = roll(tile, -c)
        if along_z and c:
            value = value + float(c)
        target[rows(shifted_row(field, fields, c, column) + 8 * half), :] = value


def pair_geometry(shifts, fields, column, a, c, own_x, own_y, own_z):
    at = 3 + a
    x = shifts[rows(shifted_row(0, fields, c, column) + at), :] - own_x
    y = shifts[rows(shifted_row(1, fields, c, column) + at), :] - own_y
    z = shifts[rows(shifted_row(2, fields, c, column) + at), :] - own_z
    return x, y, z, x * x + y * y + z * z


def band_sum(flags, incoming, shifts, sums):
    def column_sum(y, carry):
        own = [shifts[rows(shifted_row(n, 3, 0, y) + 3), :] for n in range(3)]
        total = jnp.zeros((8, 128), F32)
        own_x = {a: own[0] - float(a) for a in range(-3, 4)}
        for b in range(-3, 4):
            own_y = own[1] - float(b)
            part = None
            for a, c in directed(b):
                _, _, _, square = pair_geometry(shifts, 3, y + b, a, c, own_x[a], own_y, own[2])
                length = square * lax.rsqrt(square)
                stretch = length - math.sqrt(float(a * a + b * b + c * c))
                if (a, b, c) > (0, 0, 0):
                    flag = flags[rows(FLAG_BASE[INDEX[a, b, c]] + y * (8 + a) + a), :]
                else:
                    flag = incoming[rows((INDEX[-a, -b, -c] * 14 + y + b + 3) * 8), :]
                part = flag * stretch if part is None else part + flag * stretch
            if b:
                inside = jnp.logical_and(y + b >= 0, y + b < 8)
                part = jnp.where(inside, part, 0.0)
            total = total + part
        sums[rows(8 * y), :] = total
        return carry

    lax.fori_loop(0, 8, column_sum, 0)


def own_shifts(wide, shifts):
    def column(y, carry):
        for n in range(3):
            for half in range(2):
                tile = wide[rows(128 * n + 16 * y + 8 * half), :]
                store_shifts(shifts, n, 3, y, half, tile, n == 2)
        return carry

    lax.fori_loop(0, 8, column, 0)


def pack_y(wide, sums, up, down):
    for n in range(3):
        up[48 * n : 48 * n + 48, :] = wide[128 * n + 80 : 128 * n + 128, :]
        down[48 * n : 48 * n + 48, :] = wide[128 * n : 128 * n + 48, :]
    up[Y_SUM : Y_SUM + 24, :] = sums[40:64, :]
    down[Y_SUM : Y_SUM + 24, :] = sums[0:24, :]


def band_first(
    place, u, material, intact, below, above, wide, wide_material, flags, incoming, sums, up, down, shifts
):
    last_x = jnp.where(place[0] == 1, 0.0, 1.0)
    zero = place[3]
    for n in range(3):
        widen(wide, 128 * n, u, 64 * n, below, above, 24 * n)
    widen(wide_material, 0, material, 0, below, above, 72)
    own_shifts(wide, shifts)
    lane = lax.broadcasted_iota(jnp.int32, (8, 128), 1)
    column = lax.broadcasted_iota(jnp.int32, (8, 128), 0)
    first_column = jnp.where(place[1] == 1, 0, -8)
    last_column = jnp.where(place[2] == 1, 8, 16)
    for b in range(-3, 4):
        in_y = jnp.logical_and(column + b >= first_column, column + b < last_column)
        for c in range(-3, 4):
            inside = jnp.logical_and(in_y, jnp.logical_and(lane + c >= 0, lane + c < 128))
            valid = jnp.where(inside, 1.0, 0.0).astype(F32)
            leaving = valid * last_x
            for a in range(4):
                k = INDEX.get((a, b, c))
                if k is None:
                    continue
                step = 8 + a
                for x in range(8):
                    tile = intact[64 * k + 8 * x : 64 * k + 8 * x + 8, :].astype(F32)
                    tile = tile * (leaving if x + a >= 8 else valid)
                    flags[pl.ds(FLAG_BASE[k] + a + x, 8, stride=step), :] = tile
                for t in range(a):
                    tile = below[X_FLAG[k] + 8 * t : X_FLAG[k] + 8 * t + 8, :] * valid
                    flags[pl.ds(FLAG_BASE[k] + t, 8, stride=step), :] = tile

    def turn(y, carry):
        for k, (a, b, c) in enumerate(OFFSETS):
            tile = flags[rows(FLAG_BASE[k] + y * (8 + a)), :]
            incoming[rows((k * 14 + y + 3) * 8), :] = roll(tile, c)
        return carry

    lax.fori_loop(0, 8, turn, 0)
    band_sum(flags, incoming, shifts, sums)
    pack_y(wide, sums, up, down)
    up[Y_MATERIAL : Y_MATERIAL + 48, :] = wide_material[80:128, :]
    down[Y_MATERIAL : Y_MATERIAL + 48, :] = wide_material[0:48, :]
    for k, (a, b, c) in enumerate(OFFSETS):
        if b > 0:
            copy_rows(up, zero + Y_UP_FLAG[k], flags, zero + FLAG_BASE[k] + (8 - b) * (8 + a), b * (8 + a))
        elif b < 0:
            copy_rows(down, zero + Y_DOWN_FLAG[k], flags, zero + FLAG_BASE[k], -b * (8 + a))


def band_next(u, below, above, flags, incoming, wide, sums, up, down, shifts):
    for n in range(3):
        widen(wide, 128 * n, u, 64 * n, below, above, 24 * n)
    own_shifts(wide, shifts)
    band_sum(flags, incoming, shifts, sums)
    pack_y(wide, sums, up, down)


def wide_tile(wide, before, after, field, column, half):
    if column < 0:
        return before[rows(48 * field + 16 * (column + 3) + 8 * half), :]
    if column < 8:
        return wide[rows(128 * field + 16 * column + 8 * half), :]
    return after[rows(48 * field + 16 * (column - 8) + 8 * half), :]


def strip_theta(first, place, wide, flags, incoming, sums, before, after, before_flags, after_flags, *rest):
    if first:
        theta, up, down, all_incoming, shifts = rest
        own_incoming, incoming = incoming, all_incoming

        def keep(k, carry):
            copy_rows(incoming, (k * 14 + 3) * 8, own_incoming, (k * 14 + 3) * 8, 64)
            return carry

        lax.fori_loop(0, len(OFFSETS), keep, 0)
        zero = place[3]
        for k, (a, b, c) in enumerate(OFFSETS):
            for n in range(abs(b)):
                if b > 0:
                    tile = before_flags[rows(zero + Y_UP_FLAG[k] + n * (8 + a)), :]
                    incoming[rows((k * 14 + 3 - b + n) * 8), :] = roll(tile, c)
                else:
                    tile = after_flags[rows(zero + Y_DOWN_FLAG[k] + n * (8 + a)), :]
                    incoming[rows((k * 14 + 11 + n) * 8), :] = roll(tile, c)
    else:
        theta, up, down, shifts = rest
        zero = place[3]
    for column in (-3, -2, -1, 0, 1, 2, 5, 6, 7, 8, 9, 10):
        for n in range(3):
            for half in range(2):
                tile = wide_tile(wide, before, after, n, column, half)
                store_shifts(shifts, n, 3, column, half, tile, n == 2)
    for column in range(-3, 11):
        if column < 0:
            total = before[rows(Y_SUM + 8 * (column + 3)), :]
            partners = range(-column, 4)
        elif column < 8:
            total = sums[rows(8 * column), :]
            partners = [b for b in range(-3, 4) if not 0 <= column + b < 8]
        else:
            total = after[rows(Y_SUM + 8 * (column - 8)), :]
            partners = range(-3, 8 - column)
        own = [shifts[rows(zero + shifted_row(n, 3, 0, column) + 3), :] for n in range(3)] if len(partners) else None
        for b in partners:
            own_y = own[1] - float(b)
            for a, c in directed(b):
                own_x = own[0] - float(a)
                _, _, _, square = pair_geometry(shifts, 3, zero * 0 + column + b, a, c, own_x, own_y, own[2])
                length = square * lax.rsqrt(square)
                stretch = length - math.sqrt(float(a * a + b * b + c * c))
                if (a, b, c) > (0, 0, 0):
                    k = INDEX[a, b, c]
                    if column < 0:
                        flag = before_flags[rows(zero + Y_UP_FLAG[k] + (column + b) * (8 + a) + a), :]
                    elif column < 8:
                        flag = flags[rows(zero + FLAG_BASE[k] + column * (8 + a) + a), :]
                    else:
                        flag = after_flags[rows(zero + Y_DOWN_FLAG[k] + (column - 8) * (8 + a) + a), :]
                else:
                    flag = incoming[rows((INDEX[-a, -b, -c] * 14 + column + b + 3) * 8), :]
                total = total + flag * stretch
        theta[rows(8 * (column + 3)), :] = total
        up[rows(zero + 3 * (column + 3), 3), :] = theta[rows(zero + 8 * (column + 3) + 5, 3), :]
        down[rows(zero + 3 * (column + 3), 3), :] = theta[rows(zero + 8 * (column + 3), 3), :]


def pick(numbers, values):
    result = jnp.full(numbers.shape, values[CLASSES - 1], F32)
    for n in range(CLASSES - 1):
        result = jnp.where(numbers == float(n), values[n], result)
    return result


def advance(last, place, bulk, shear, density, u, v, wide, before, after, wide_material, before_material, after_material,
            theta, below, above, flags, incoming, *rest):
    if last:
        new_u, new_v, force, shifts, wide_theta = rest
    else:
        new_u, new_v, up, down, shifts, wide_theta = rest
        force = None
    zero = place[3]
    twist = [shear[n] * (15.0 / VOLUME) for n in range(CLASSES)]
    press = [(bulk[n] * 3.0 - shear[n] * 5.0) * (3.0 / (VOLUME * VOLUME)) for n in range(CLASSES)]
    inertia = [density[n] for n in range(CLASSES)]
    for column in range(-3, 11):
        at = 16 * (column + 3)
        wide_theta[rows(zero + at + 3), :] = theta[8 * (column + 3) : 8 * (column + 3) + 8, :]
        wide_theta[rows(zero + at, 3), :] = below[rows(zero + 3 * (column + 3), 3), :]
        wide_theta[rows(zero + at + 11, 3), :] = above[rows(zero + 3 * (column + 3), 3), :]
        wide_theta[rows(zero + at + 14, 2), :] = jnp.zeros((2, 128), F32)
        for half in range(2):
            for n in range(3):
                tile = wide_tile(wide, before, after, n, column, half)
                store_shifts(shifts, n, 5, column, half, tile, n == 2)
            if column < 0:
                number = before_material[rows(Y_MATERIAL + 16 * (column + 3) + 8 * half), :]
            elif column < 8:
                number = wide_material[rows(16 * column + 8 * half), :]
            else:
                number = after_material[rows(Y_MATERIAL + 16 * (column - 8) + 8 * half), :]
            twisting = pick(number, twist)
            pressing = pick(number, press) * wide_theta[rows(at + 8 * half), :] - twisting
            store_shifts(shifts, 3, 5, column, half, pressing, False)
            store_shifts(shifts, 4, 5, column, half, twisting, False)

    def column_force(y, carry):
        own = [shifts[rows(shifted_row(n, 5, 0, y) + 3), :] for n in range(5)]
        own_x = {a: own[0] - float(a) for a in range(-3, 4)}
        total = [jnp.zeros((8, 128), F32) for _ in range(3)]
        for b in range(-3, 4):
            own_y = own[1] - float(b)
            for a, c in directed(b):
                *vector, square = pair_geometry(shifts, 5, y + b, a, c, own_x[a], own_y, own[2])
                inverse = lax.rsqrt(square)
                pressing = shifts[rows(shifted_row(3, 5, c, y + b) + 3 + a), :] + own[3]
                twisting = shifts[rows(shifted_row(4, 5, c, y + b) + 3 + a), :] + own[4]
                if (a, b, c) > (0, 0, 0):
                    flag = flags[rows(FLAG_BASE[INDEX[a, b, c]] + y * (8 + a) + a), :]
                else:
                    flag = incoming[rows((INDEX[-a, -b, -c] * 14 + y + b + 3) * 8), :]
                size = flag * (pressing * inverse + twisting * (1.0 / math.sqrt(float(a * a + b * b + c * c))))
                total = [t + size * w for t, w in zip(total, vector)]
        number = wide_material[rows(16 * y + 3), :]
        mass = pick(number, inertia)
        for n in range(3):
            at = pl.ds(64 * n + y, 8, stride=8)
            speed = v[at, :] + TIME_STEP * total[n] / mass
            new_v[at, :] = speed
            new_u[at, :] = u[at, :] + TIME_STEP * speed
            if last:
                force[at, :] = total[n]
        return carry

    lax.fori_loop(0, 8, column_force, 0)
    if not last:
        for n in range(3):
            up[24 * n : 24 * n + 24, :] = new_u[64 * n + 40 : 64 * n + 64, :]
            down[24 * n : 24 * n + 24, :] = new_u[64 * n : 64 * n + 24, :]


VMEM = pl.BlockSpec(memory_space=pltpu.VMEM)
SMEM = pl.BlockSpec(memory_space=pltpu.SMEM)


def call(body, outputs, scratch, scalars, *arguments, flops=0):
    shapes = [jax.ShapeDtypeStruct((n, 128), F32) for n in outputs]
    traffic = 512 * sum(outputs) + sum(4 * x.size for x in arguments)
    return pl.pallas_call(
        body,
        out_shape=shapes,
        in_specs=[SMEM] * scalars + [VMEM] * (len(arguments) - scalars),
        out_specs=[VMEM] * len(shapes),
        scratch_shapes=[pltpu.VMEM((n, 128), F32) for n in scratch],
        compiler_params=pltpu.CompilerParams(vmem_limit_bytes=24 << 20),
        cost_estimate=pl.CostEstimate(flops=flops, bytes_accessed=traffic, transcendentals=0),
    )(*arguments)


def both_ways(up, down, axis):
    size = lax.axis_size(axis)
    route = [(i, i + 1) for i in range(size - 1)]
    from_below = lax.ppermute(up, axis, route)
    from_above = lax.ppermute(down, axis, [(j, i) for i, j in route])
    return from_below, from_above


def on_device(displacement, velocity, intact, material, bulk_modulus, shear_modulus, density):
    shape = displacement.shape
    u, v = displacement.reshape(192, 128), velocity.reshape(192, 128)
    flags_in = intact.reshape(len(OFFSETS) * 64, 128)
    material = material.reshape(64, 128)
    gx, gy = lax.axis_index("gx"), lax.axis_index("gy")
    place = jnp.stack(
        [gx == lax.axis_size("gx") - 1, gy == 0, gy == lax.axis_size("gy") - 1, gy < 0]
    ).astype(jnp.int32)
    tables = (bulk_modulus, shear_modulus, density)
    all_rows = len(OFFSETS) * 14 * 8
    up, down = call(pack_first, [X_UP_ROWS, X_DOWN_ROWS], [], 0, u, material, flags_in)
    below, above = both_ways(up, down, "gx")
    wide, wide_material, flags, incoming, sums, up, down = call(
        band_first,
        [384, 128, FLAG_ROWS, all_rows, 64, Y_UP_ROWS, Y_DOWN_ROWS],
        [7 * 3 * 224],
        1, place, u, material, flags_in, below, above,
    )
    before, after = both_ways(up, down, "gy")
    first_before, first_after = before, after
    for step in range(STEPS):
        if step:
            below, above = both_ways(up, down, "gx")
            wide, sums, up, down = call(
                band_next, [384, 64, Y_FLAGS, Y_FLAGS], [7 * 3 * 224], 0, u, below, above, flags, incoming
            )
            before, after = both_ways(up, down, "gy")
        outputs = [112, 48, 48] + ([] if step else [all_rows])
        theta, up, down, *more = call(
            functools.partial(strip_theta, step == 0), outputs, [7 * 3 * 224],
            1, place, wide, flags, incoming, sums, before, after, first_before, first_after,
        )
        if not step:
            incoming = more[0]
        below, above = both_ways(up, down, "gx")
        last = step == STEPS - 1
        u, v, *more = call(
            functools.partial(advance, last), [192, 192] + ([192] if last else [72, 72]), [7 * 5 * 224, 224],
            4, place, *tables, u, v, wide, before, after, wide_material, first_before, first_after,
            theta, below, above, flags, incoming,
        )
        if last:
            force = more[0]
        else:
            up, down = more
    return u.reshape(shape), v.reshape(shape), force.reshape(shape)


def solution(mesh):
    return jax.shard_map(
        on_device,
        mesh=mesh,
        in_specs=(
            P(None, "gx", "gy", None),
            P(None, "gx", "gy", None),
            P(None, "gx", "gy", None),
            P("gx", "gy", None),
            P(),
            P(),
            P(),
        ),
        out_specs=(P(None, "gx", "gy", None), P(None, "gx", "gy", None), P(None, "gx", "gy", None)),
        check_vma=False,
    )
```

time: 202 us -> 90.4 us (0.45)
  the two profiles are of different devices: /device:TPU:102 before, /device:TPU:103 now
where the time goes in v1:
time: 90.4 us; the launch traced here: 89.7 us
  starting transfers between devices  35.1 us (39%)
  waiting for transfers between devices  27.4 us (30%)
  Pallas kernels  21.5 us (24%)
  local copies, waits for them, and re-layouts  4.88 us (5%)
    ppermute x6, waiting for transfers between devices, both_ways(): from_above = lax.ppermute(down, axis, [(j, i) for i, j in route])  27.2 us
    ppermute x6, starting transfers between devices, both_ways(): from_below = lax.ppermute(up, axis, route)  21.6 us
    pallas_call x7, Pallas kernels, call(): pl.pallas_call(body, out_shape=shapes, in_specs=[SMEM] * scalars + [VMEM]...  21.5 us
    ppermute x6, starting transfers between devices, both_ways(): from_above = lax.ppermute(down, axis, [(j, i) for i, j in route])  13.4 us
    unnamed x22, local copies, waits for them, and re-layouts  4.88 us
  transfers between devices with their start and end apart: 12, of which 7 were waited for; matrix products, arithmetic and copies ran while one was open for 0% of the time, Pallas kernels for 0%

profile of v1, /device:TPU:103, one launch (start us, length us, event | category | flops | bytes accessed | tf_op | source)
XLA Modules:
  0.0 89.7 jit_solution(5676798603661418691)
XLA Ops:
  0.6 1.5 %copy-done = s32[61,8,8,128]{3,2,1,0:T(8,128)S(1)} copy-done((s32[61,8,8,128]{3,2,1,0:T(8,128)S(1)}, s32[61,8,8,128]{3,2,1,0:T(8,128)}, u32[]{:S(2)}) %copy-start) | copy-done | bytes 1998872
  2.2 0.9 copy-done.2
  3.1 0.8 copy-done.5
  3.9 3.9 %collective-permute-start = (f32[656,128]{1,0:T(8,128)S(1)}, f32[656,128]{1,0:T(8,128)S(1)}, u32[]{:S(2)}, u32[]{:S(2)}) collective-permute-start(f32[656,128]{1,0:T(8,128)S(1)} %get-tuple-element.30), channel_id=1, source_target_pairs={{0,32},{32,64},{64,96},{96,128},{128,160},{160,192},{192,224},{1,3... | collective-permute-start | bytes 1007624 | tf_op jit(solution)/shard_map/ppermute | solution.py:389
  7.8 1.9 %collective-permute-start.1 = (f32[96,128]{1,0:T(8,128)S(1)}, f32[96,128]{1,0:T(8,128)S(1)}, u32[]{:S(2)}, u32[]{:S(2)}) collective-permute-start(f32[96,128]{1,0:T(8,128)S(1)} %get-tuple-element.31), channel_id=1, source_target_pairs={{32,0},{64,32},{96,64},{128,96},{160,128},{192,160},{224,192},{33,... | collective-permute-start | bytes 147464 | tf_op jit(solution)/shard_map/ppermute | solution.py:390
  9.7 0.1 add_convert_fusion.place
  9.8 3.4 %collective-permute-done.1.above = f32[96,128]{1,0:T(8,128)S(1)} collective-permute-done((f32[96,128]{1,0:T(8,128)S(1)}, f32[96,128]{1,0:T(8,128)S(1)}, u32[]{:S(2)}, u32[]{:S(2)}) %collective-permute-start.1) | collective-permute-done | bytes 49184 | tf_op jit(solution)/shard_map/ppermute | solution.py:390
  13.2 0.9 copy-done.3
  14.1 0.8 copy-done.6
  14.9 4.6 %shard_map.95 = (f32[384,128]{1,0:T(8,128)S(1)}, f32[128,128]{1,0:T(8,128)S(1)}, f32[4464,128]{1,0:T(8,128)S(1)}, f32[6832,128]{1,0:T(8,128)S(1)}, f32[64,128]{1...) custom-call(s32[4]{0:T(128)S(1)} %add_convert_fusion.place, f32[192,128]{1,0:T(8,128)S(1)} %bitcast.14, ...), custom_call_target="tpu_custom_call" | custom-call | bytes 9142288 | tf_op jit(solution)/shard_map/pallas_call | solution.py:375
  19.5 4.7 %collective-permute-start.2 = (f32[608,128]{1,0:T(8,128)S(1)}, f32[608,128]{1,0:T(8,128)S(1)}, u32[]{:S(2)}, u32[]{:S(2)}) collective-permute-start(f32[608,128]{1,0:T(8,128)S(1)} %get-tuple-element.33), channel_id=1, source_target_pairs={{0,1},{1,2},{2,3},{3,4},{4,5},{5,6},{6,7},{7,8},{8,9},{9,10},{10,1... | collective-permute-start | bytes 933896 | tf_op jit(solution)/shard_map/ppermute | solution.py:389
  24.1 1.9 %collective-permute-start.3 = (f32[464,128]{1,0:T(8,128)S(1)}, f32[464,128]{1,0:T(8,128)S(1)}, u32[]{:S(2)}, u32[]{:S(2)}) collective-permute-start(f32[464,128]{1,0:T(8,128)S(1)} %get-tuple-element.34), channel_id=1, source_target_pairs={{1,0},{2,1},{3,2},{4,3},{5,4},{6,5},{7,6},{8,7},{9,8},{10,9},{11,1... | collective-permute-start | bytes 712712 | tf_op jit(solution)/shard_map/ppermute | solution.py:390
  26.1 9.3 %collective-permute-done.3.after.after_flags.after_material = f32[464,128]{1,0:T(8,128)S(1)} collective-permute-done((f32[464,128]{1,0:T(8,128)S(1)}, f32[464,128]{1,0:T(8,128)S(1)}, u32[]{:S(2)}, u32[]{:S(2)}) %collective-permute-start.3) | collective-permute-done | bytes 237600 | tf_op jit(solution)/shard_map/ppermute | solution.py:390
  35.3 0.0 copy-start.9
  35.4 2.0 %shard_map.96 = (f32[112,128]{1,0:T(8,128)S(1)}, f32[48,128]{1,0:T(8,128)S(1)}, f32[48,128]{1,0:T(8,128)S(1)}, f32[6832,128]{1,0:T(8,128)S(1)}) custom-call(s32[4]{0:T(128)S(1)} %add_convert_fusion.place, f32[384,128]{1,0:T(8,128)S(1)} %get-tuple-element.32.wide, f32[4464,128]{1,0:T(8,128)S(1)} %get-tuple-element.36.flags, ...), custom_call_target="tpu_custom_call" | custom-call | bytes 10715152 | tf_op jit(solution)/shard_map/pallas_call | solution.py:375
  37.4 5.3 %collective-permute-start.4 = (f32[48,128]{1,0:T(8,128)S(1)}, f32[48,128]{1,0:T(8,128)S(1)}, u32[]{:S(2)}, u32[]{:S(2)}) collective-permute-start(f32[48,128]{1,0:T(8,128)S(1)} %get-tuple-element.40), channel_id=1, source_target_pairs={{0,32},{32,64},{64,96},{96,128},{128,160},{160,192},{192,224},{1,3... | collective-permute-start | bytes 73736 | tf_op jit(solution)/shard_map/ppermute | solution.py:389
  42.7 1.9 %collective-permute-start.5 = (f32[48,128]{1,0:T(8,128)S(1)}, f32[48,128]{1,0:T(8,128)S(1)}, u32[]{:S(2)}, u32[]{:S(2)}) collective-permute-start(f32[48,128]{1,0:T(8,128)S(1)} %get-tuple-element.41), channel_id=1, source_target_pairs={{32,0},{64,32},{96,64},{128,96},{160,128},{192,160},{224,192},{33,... | collective-permute-start | bytes 73736 | tf_op jit(solution)/shard_map/ppermute | solution.py:390
  44.6 3.2 %collective-permute-done.5.above = f32[48,128]{1,0:T(8,128)S(1)} collective-permute-done((f32[48,128]{1,0:T(8,128)S(1)}, f32[48,128]{1,0:T(8,128)S(1)}, u32[]{:S(2)}, u32[]{:S(2)}) %collective-permute-start.5) | collective-permute-done | bytes 24608 | tf_op jit(solution)/shard_map/ppermute | solution.py:390
  47.9 4.9 %shard_map.97 = (f32[192,128]{1,0:T(8,128)S(1)}, f32[192,128]{1,0:T(8,128)S(1)}, f32[72,128]{1,0:T(8,128)S(1)}, f32[72,128]{1,0:T(8,128)S(1)}) custom-call(s32[4]{0:T(128)S(1)} %add_convert_fusion.place, f32[8]{0:T(128)S(1)} %copy-done.8, f32[8]{0:T(128)S(1)} %copy-done.9, f32[8]{0:T(128)S(1)} %copy-done.10, f32[192,128]{1,0:T(8,128)S(1)} %bitcast.15, ...), custom_call_target="tpu_custom_call" | custom-call | bytes 7716976 | tf_op jit(solution)/shard_map/pallas_call | solution.py:375
  52.7 1.9 %collective-permute-start.6 = (f32[72,128]{1,0:T(8,128)S(1)}, f32[72,128]{1,0:T(8,128)S(1)}, u32[]{:S(2)}, u32[]{:S(2)}) collective-permute-start(f32[72,128]{1,0:T(8,128)S(1)} %get-tuple-element.45), channel_id=1, source_target_pairs={{0,32},{32,64},{64,96},{96,128},{128,160},{160,192},{192,224},{1,3... | collective-permute-start | bytes 110600 | tf_op jit(solution)/shard_map/ppermute | solution.py:389
  54.7 2.4 %collective-permute-start.7 = (f32[72,128]{1,0:T(8,128)S(1)}, f32[72,128]{1,0:T(8,128)S(1)}, u32[]{:S(2)}, u32[]{:S(2)}) collective-permute-start(f32[72,128]{1,0:T(8,128)S(1)} %get-tuple-element.46), channel_id=1, source_target_pairs={{32,0},{64,32},{96,64},{128,96},{160,128},{192,160},{224,192},{33,... | collective-permute-start | bytes 110600 | tf_op jit(solution)/shard_map/ppermute | solution.py:390
  57.1 2.9 %collective-permute-done.7.above = f32[72,128]{1,0:T(8,128)S(1)} collective-permute-done((f32[72,128]{1,0:T(8,128)S(1)}, f32[72,128]{1,0:T(8,128)S(1)}, u32[]{:S(2)}, u32[]{:S(2)}) %collective-permute-start.7) | collective-permute-done | bytes 36896 | tf_op jit(solution)/shard_map/ppermute | solution.py:390
  59.9 2.8 %shard_map.98 = (f32[384,128]{1,0:T(8,128)S(1)}, f32[64,128]{1,0:T(8,128)S(1)}, f32[216,128]{1,0:T(8,128)S(1)}, f32[216,128]{1,0:T(8,128)S(1)}) custom-call(f32[192,128]{1,0:T(8,128)S(1)} %get-tuple-element.43.u, f32[72,128]{1,0:T(8,128)S(1)} %collective-permute-done.6.below, f32[72,128]{1,0:T(8,128)S(1)} %collective-permute-done.7.above, ...), custom_call_target="tpu_custom_call" | custom-call | bytes 6406144 | tf_op jit(solution)/shard_map/pallas_call | solution.py:375
  62.8 1.9 %collective-permute-start.8 = (f32[216,128]{1,0:T(8,128)S(1)}, f32[216,128]{1,0:T(8,128)S(1)}, u32[]{:S(2)}, u32[]{:S(2)}) collective-permute-start(f32[216,128]{1,0:T(8,128)S(1)} %get-tuple-element.48), channel_id=1, source_target_pairs={{0,1},{1,2},{2,3},{3,4},{4,5},{5,6},{6,7},{7,8},{8,9},{9,10},{10,1... | collective-permute-start | bytes 331784 | tf_op jit(solution)/shard_map/ppermute | solution.py:389
  64.7 3.4 %collective-permute-start.9 = (f32[216,128]{1,0:T(8,128)S(1)}, f32[216,128]{1,0:T(8,128)S(1)}, u32[]{:S(2)}, u32[]{:S(2)}) collective-permute-start(f32[216,128]{1,0:T(8,128)S(1)} %get-tuple-element.49), channel_id=1, source_target_pairs={{1,0},{2,1},{3,2},{4,3},{5,4},{6,5},{7,6},{8,7},{9,8},{10,9},{11,1... | collective-permute-start | bytes 331784 | tf_op jit(solution)/shard_map/ppermute | solution.py:390
  68.1 0.2 collective-permute-done.8.before
  68.3 5.2 %collective-permute-done.9.after = f32[216,128]{1,0:T(8,128)S(1)} collective-permute-done((f32[216,128]{1,0:T(8,128)S(1)}, f32[216,128]{1,0:T(8,128)S(1)}, u32[]{:S(2)}, u32[]{:S(2)}) %collective-permute-start.9) | collective-permute-done | bytes 110624 | tf_op jit(solution)/shard_map/ppermute | solution.py:390
  73.5 1.6 %shard_map.99 = (f32[112,128]{1,0:T(8,128)S(1)}, f32[48,128]{1,0:T(8,128)S(1)}, f32[48,128]{1,0:T(8,128)S(1)}) custom-call(s32[4]{0:T(128)S(1)} %add_convert_fusion.place, f32[384,128]{1,0:T(8,128)S(1)} %get-tuple-element.47.wide, f32[4464,128]{1,0:T(8,128)S(1)} %get-tuple-element.36.flags, f32[6832,128]{1,0:T(8,128)S(1)} %get-tuple-element.42.incoming, ...), custom_call_target="tpu_custom_call" | custom-call | bytes 6889488 | tf_op jit(solution)/shard_map/pallas_call | solution.py:375
  75.1 3.9 %collective-permute-start.10 = (f32[48,128]{1,0:T(8,128)S(1)}, f32[48,128]{1,0:T(8,128)S(1)}, u32[]{:S(2)}, u32[]{:S(2)}) collective-permute-start(f32[48,128]{1,0:T(8,128)S(1)} %get-tuple-element.52), channel_id=1, source_target_pairs={{0,32},{32,64},{64,96},{96,128},{128,160},{160,192},{192,224},{1,3... | collective-permute-start | bytes 73736 | tf_op jit(solution)/shard_map/ppermute | solution.py:389
  79.0 1.9 %collective-permute-start.11 = (f32[48,128]{1,0:T(8,128)S(1)}, f32[48,128]{1,0:T(8,128)S(1)}, u32[]{:S(2)}, u32[]{:S(2)}) collective-permute-start(f32[48,128]{1,0:T(8,128)S(1)} %get-tuple-element.53), channel_id=1, source_target_pairs={{32,0},{64,32},{96,64},{128,96},{160,128},{192,160},{224,192},{33,... | collective-permute-start | bytes 73736 | tf_op jit(solution)/shard_map/ppermute | solution.py:390
  81.0 3.2 %collective-permute-done.11.above = f32[48,128]{1,0:T(8,128)S(1)} collective-permute-done((f32[48,128]{1,0:T(8,128)S(1)}, f32[48,128]{1,0:T(8,128)S(1)}, u32[]{:S(2)}, u32[]{:S(2)}) %collective-permute-start.11) | collective-permute-done | bytes 24608 | tf_op jit(solution)/shard_map/ppermute | solution.py:390
  84.2 5.6 %shard_map.100 = (f32[192,128]{1,0:T(8,128)}, f32[192,128]{1,0:T(8,128)}, f32[192,128]{1,0:T(8,128)}) custom-call(s32[4]{0:T(128)S(1)} %add_convert_fusion.place, f32[8]{0:T(128)S(1)} %copy-done.8, f32[8]{0:T(128)S(1)} %copy-done.9, f32[8]{0:T(128)S(1)} %copy-done.10, f32[192,128]{1,0:T(8,128)S(1)} %get-tuple-element.43.u, ...), custom_call_target="tpu_custom_call" | custom-call | bytes 7413872 | tf_op jit(solution)/shard_map/pallas_call | solution.py:375
  (22 shorter events, 0.1 us)
Async XLA Ops:
  0.6 1.6 %copy-start = (s32[61,8,8,128]{3,2,1,0:T(8,128)S(1)}, s32[61,8,8,128]{3,2,1,0:T(8,128)}, u32[]{:S(2)}) copy-start(s32[61,8,8,128]{3,2,1,0:T(8,128)} %param.9) | copy-start | bytes 5996548
  2.2 0.9 copy-start.2
  3.1 0.8 copy-start.5
  3.8 9.4 %copy-start.1 = (s32[61,8,8,128]{3,2,1,0:T(8,128)S(1)}, s32[61,8,8,128]{3,2,1,0:T(8,128)}, u32[]{:S(2)}) copy-start(s32[61,8,8,128]{3,2,1,0:T(8,128)} %param.9) | copy-start | bytes 5996548
  3.9 9.3 %collective-permute-start = (f32[656,128]{1,0:T(8,128)S(1)}, f32[656,128]{1,0:T(8,128)S(1)}, u32[]{:S(2)}, u32[]{:S(2)}) collective-permute-start(f32[656,128]{1,0:T(8,128)S(1)} %get-tuple-element.30), channel_id=1, source_target_pairs={{0,32},{32,64},{64,96},{96,128},{128,160},{160,192},{192,224},{1,3... | collective-permute-start | bytes 1007624 | tf_op jit(solution)/shard_map/ppermute | solution.py:389
  7.8 5.4 %collective-permute-start.1 = (f32[96,128]{1,0:T(8,128)S(1)}, f32[96,128]{1,0:T(8,128)S(1)}, u32[]{:S(2)}, u32[]{:S(2)}) collective-permute-start(f32[96,128]{1,0:T(8,128)S(1)} %get-tuple-element.31), channel_id=1, source_target_pairs={{32,0},{64,32},{96,64},{128,96},{160,128},{192,160},{224,192},{33,... | collective-permute-start | bytes 147464 | tf_op jit(solution)/shard_map/ppermute | solution.py:390
  13.2 0.9 copy-start.3
  14.1 0.8 copy-start.6
  19.5 15.9 %collective-permute-start.2 = (f32[608,128]{1,0:T(8,128)S(1)}, f32[608,128]{1,0:T(8,128)S(1)}, u32[]{:S(2)}, u32[]{:S(2)}) collective-permute-start(f32[608,128]{1,0:T(8,128)S(1)} %get-tuple-element.33), channel_id=1, source_target_pairs={{0,1},{1,2},{2,3},{3,4},{4,5},{5,6},{6,7},{7,8},{8,9},{9,10},{10,1... | collective-permute-start | bytes 933896 | tf_op jit(solution)/shard_map/ppermute | solution.py:389
  24.1 11.2 %collective-permute-start.3 = (f32[464,128]{1,0:T(8,128)S(1)}, f32[464,128]{1,0:T(8,128)S(1)}, u32[]{:S(2)}, u32[]{:S(2)}) collective-permute-start(f32[464,128]{1,0:T(8,128)S(1)} %get-tuple-element.34), channel_id=1, source_target_pairs={{1,0},{2,1},{3,2},{4,3},{5,4},{6,5},{7,6},{8,7},{9,8},{10,9},{11,1... | collective-permute-start | bytes 712712 | tf_op jit(solution)/shard_map/ppermute | solution.py:390
  35.3 12.5 %copy-start.4 = (f32[3,8,8,128]{3,2,1,0:T(8,128)S(1)}, f32[3,8,8,128]{3,2,1,0:T(8,128)}, u32[]{:S(2)}) copy-start(f32[3,8,8,128]{3,2,1,0:T(8,128)} %param.7) | copy-start | bytes 294916
  35.3 12.5 %copy-start.7 = (f32[3,8,8,128]{3,2,1,0:T(8,128)S(1)}, f32[3,8,8,128]{3,2,1,0:T(8,128)}, u32[]{:S(2)}) copy-start(f32[3,8,8,128]{3,2,1,0:T(8,128)} %param.8) | copy-start | bytes 294916
  35.3 12.5 %copy-start.8 = (f32[8]{0:T(128)S(1)}, f32[8]{0:T(128)}, u32[]{:S(2)}) copy-start(f32[8]{0:T(128)} %bulk.3) | copy-start | bytes 100
  35.3 12.5 %copy-start.9 = (f32[8]{0:T(128)S(1)}, f32[8]{0:T(128)}, u32[]{:S(2)}) copy-start(f32[8]{0:T(128)} %shear.3) | copy-start | bytes 100
  35.4 12.5 %copy-start.10 = (f32[8]{0:T(128)S(1)}, f32[8]{0:T(128)}, u32[]{:S(2)}) copy-start(f32[8]{0:T(128)} %density.3) | copy-start | bytes 100
  37.4 7.2 %collective-permute-start.4 = (f32[48,128]{1,0:T(8,128)S(1)}, f32[48,128]{1,0:T(8,128)S(1)}, u32[]{:S(2)}, u32[]{:S(2)}) collective-permute-start(f32[48,128]{1,0:T(8,128)S(1)} %get-tuple-element.40), channel_id=1, source_target_pairs={{0,32},{32,64},{64,96},{96,128},{128,160},{160,192},{192,224},{1,3... | collective-permute-start | bytes 73736 | tf_op jit(solution)/shard_map/ppermute | solution.py:389
  42.7 5.1 %collective-permute-start.5 = (f32[48,128]{1,0:T(8,128)S(1)}, f32[48,128]{1,0:T(8,128)S(1)}, u32[]{:S(2)}, u32[]{:S(2)}) collective-permute-start(f32[48,128]{1,0:T(8,128)S(1)} %get-tuple-element.41), channel_id=1, source_target_pairs={{32,0},{64,32},{96,64},{128,96},{160,128},{192,160},{224,192},{33,... | collective-permute-start | bytes 73736 | tf_op jit(solution)/shard_map/ppermute | solution.py:390
  52.7 4.3 %collective-permute-start.6 = (f32[72,128]{1,0:T(8,128)S(1)}, f32[72,128]{1,0:T(8,128)S(1)}, u32[]{:S(2)}, u32[]{:S(2)}) collective-permute-start(f32[72,128]{1,0:T(8,128)S(1)} %get-tuple-element.45), channel_id=1, source_target_pairs={{0,32},{32,64},{64,96},{96,128},{128,160},{160,192},{192,224},{1,3... | collective-permute-start | bytes 110600 | tf_op jit(solution)/shard_map/ppermute | solution.py:389
  54.7 5.3 %collective-permute-start.7 = (f32[72,128]{1,0:T(8,128)S(1)}, f32[72,128]{1,0:T(8,128)S(1)}, u32[]{:S(2)}, u32[]{:S(2)}) collective-permute-start(f32[72,128]{1,0:T(8,128)S(1)} %get-tuple-element.46), channel_id=1, source_target_pairs={{32,0},{64,32},{96,64},{128,96},{160,128},{192,160},{224,192},{33,... | collective-permute-start | bytes 110600 | tf_op jit(solution)/shard_map/ppermute | solution.py:390
  62.8 5.5 %collective-permute-start.8 = (f32[216,128]{1,0:T(8,128)S(1)}, f32[216,128]{1,0:T(8,128)S(1)}, u32[]{:S(2)}, u32[]{:S(2)}) collective-permute-start(f32[216,128]{1,0:T(8,128)S(1)} %get-tuple-element.48), channel_id=1, source_target_pairs={{0,1},{1,2},{2,3},{3,4},{4,5},{5,6},{6,7},{7,8},{8,9},{9,10},{10,1... | collective-permute-start | bytes 331784 | tf_op jit(solution)/shard_map/ppermute | solution.py:389
  64.7 8.8 %collective-permute-start.9 = (f32[216,128]{1,0:T(8,128)S(1)}, f32[216,128]{1,0:T(8,128)S(1)}, u32[]{:S(2)}, u32[]{:S(2)}) collective-permute-start(f32[216,128]{1,0:T(8,128)S(1)} %get-tuple-element.49), channel_id=1, source_target_pairs={{1,0},{2,1},{3,2},{4,3},{5,4},{6,5},{7,6},{8,7},{9,8},{10,9},{11,1... | collective-permute-start | bytes 331784 | tf_op jit(solution)/shard_map/ppermute | solution.py:390
  75.1 5.8 %collective-permute-start.10 = (f32[48,128]{1,0:T(8,128)S(1)}, f32[48,128]{1,0:T(8,128)S(1)}, u32[]{:S(2)}, u32[]{:S(2)}) collective-permute-start(f32[48,128]{1,0:T(8,128)S(1)} %get-tuple-element.52), channel_id=1, source_target_pairs={{0,32},{32,64},{64,96},{96,128},{128,160},{160,192},{192,224},{1,3... | collective-permute-start | bytes 73736 | tf_op jit(solution)/shard_map/ppermute | solution.py:389
  79.0 5.1 %collective-permute-start.11 = (f32[48,128]{1,0:T(8,128)S(1)}, f32[48,128]{1,0:T(8,128)S(1)}, u32[]{:S(2)}, u32[]{:S(2)}) collective-permute-start(f32[48,128]{1,0:T(8,128)S(1)} %get-tuple-element.53), channel_id=1, source_target_pairs={{32,0},{64,32},{96,64},{128,96},{160,128},{192,160},{224,192},{33,... | collective-permute-start | bytes 73736 | tf_op jit(solution)/shard_map/ppermute | solution.py:390

commit v2 on v1

--- a/solution.py
+++ b/solution.py
@@ -74,15 +74,58 @@
     return value if shift % 128 == 0 else pltpu.roll(value, shift % 128, 1)
 
 
-def pack_first(u, material, intact, up, down):
+def place_messages(even, up, down, far, near):
+    near[...] = jnp.where(even, up[...], down[...])
+    far[...] = jnp.where(even, down[...], up[...])
+
+
+def take_messages(even, first, last, far, near, below, above):
+    size = above.shape[0]
+    below[...] = jnp.where(first, 0.0, jnp.where(even, far[...], near[...]))
+    above[...] = jnp.where(last, 0.0, jnp.where(even, near[0:size, :], far[0:size, :]))
+
+
+def place_along_x(place, *blocks):
+    place_messages(place[4] == 1, *blocks)
+
+
+def place_along_y(place, *blocks):
+    place_messages(place[6] == 1, *blocks)
+
+
+def take_along_x(place, *blocks):
+    take_messages(place[4] == 1, place[5] == 1, place[0] == 1, *blocks)
+
+
+def take_along_y(place, *blocks):
+    take_messages(place[6] == 1, place[1] == 1, place[2] == 1, *blocks)
+
+
+def pack_first(place, u_in, material_in, intact_in, near, far, u, material, material_copy, ones, twos, threes, up, down, done):
+    parts = [
+        pltpu.make_async_copy(u_in, u, done.at[0]),
+        pltpu.make_async_copy(material_in, material_copy, done.at[1]),
+    ]
+    for a, block in ((1, ones), (2, twos), (3, threes)):
+        first = min(k for k in X_FLAG if OFFSETS[k][0] == a)
+        source = intact_in.at[pl.ds(first, block.shape[0]), pl.ds(64 - 8 * a, 8 * a), :]
+        parts.append(pltpu.make_async_copy(source, block, done.at[1 + a]))
+    for part in parts:
+        part.start()
+    for part in parts:
+        part.wait()
     for n in range(3):
         up[24 * n : 24 * n + 24, :] = u[64 * n + 40 : 64 * n + 64, :]
         down[24 * n : 24 * n + 24, :] = u[64 * n : 64 * n + 24, :]
-    up[72:96, :] = material[40:64, :].astype(F32)
-    down[72:96, :] = material[0:24, :].astype(F32)
-    for k, base in X_FLAG.items():
-        a = OFFSETS[k][0]
-        up[base : base + 8 * a, :] = intact[64 * k + 64 - 8 * a : 64 * k + 64, :].astype(F32)
+    material[...] = material_copy[...].astype(F32)
+    up[72:96, :] = material_copy[40:64, :].astype(F32)
+    down[72:96, :] = material_copy[0:24, :].astype(F32)
+    at = 96
+    for block in (ones, twos, threes):
+        size = block.shape[0] * block.shape[1]
+        up[at : at + size, :] = block[...].astype(F32).reshape(size, 128)
+        at += size
+    place_along_x(place, up, down, near, far)
 
 
 def widen(target, base, own, own_base, below, above, at):
@@ -90,7 +133,7 @@
         if x < 0:
             tile = below[at + 8 * (x + 3) : at + 8 * (x + 3) + 8, :]
         elif x < 8:
-            tile = own[own_base + 8 * x : own_base + 8 * x + 8, :].astype(F32)
+            tile = own[own_base + 8 * x : own_base + 8 * x + 8, :]
         else:
             tile = above[at + 8 * (x - 8) : at + 8 * (x - 8) + 8, :]
         target[pl.ds(base + x + 3, 8, stride=16), :] = tile
@@ -164,37 +207,30 @@
     down[Y_SUM : Y_SUM + 24, :] = sums[0:24, :]
 
 
-def band_first(
-    place, u, material, intact, below, above, wide, wide_material, flags, incoming, sums, up, down, shifts
-):
-    last_x = jnp.where(place[0] == 1, 0.0, 1.0)
-    zero = place[3]
-    for n in range(3):
-        widen(wide, 128 * n, u, 64 * n, below, above, 24 * n)
-    widen(wide_material, 0, material, 0, below, above, 72)
-    own_shifts(wide, shifts)
+def validity(place, b, c):
     lane = lax.broadcasted_iota(jnp.int32, (8, 128), 1)
     column = lax.broadcasted_iota(jnp.int32, (8, 128), 0)
     first_column = jnp.where(place[1] == 1, 0, -8)
     last_column = jnp.where(place[2] == 1, 8, 16)
+    in_y = jnp.logical_and(column + b >= first_column, column + b < last_column)
+    inside = jnp.logical_and(in_y, jnp.logical_and(lane + c >= 0, lane + c < 128))
+    return jnp.where(inside, 1.0, 0.0).astype(F32)
+
+
+def prepare_flags(place, intact, flags, incoming):
+    last_x = jnp.where(place[0] == 1, 0.0, 1.0)
     for b in range(-3, 4):
-        in_y = jnp.logical_and(column + b >= first_column, column + b < last_column)
         for c in range(-3, 4):
-            inside = jnp.logical_and(in_y, jnp.logical_and(lane + c >= 0, lane + c < 128))
-            valid = jnp.where(inside, 1.0, 0.0).astype(F32)
+            valid = validity(place, b, c)
             leaving = valid * last_x
             for a in range(4):
                 k = INDEX.get((a, b, c))
                 if k is None:
                     continue
-                step = 8 + a
                 for x in range(8):
                     tile = intact[64 * k + 8 * x : 64 * k + 8 * x + 8, :].astype(F32)
                     tile = tile * (leaving if x + a >= 8 else valid)
-                    flags[pl.ds(FLAG_BASE[k] + a + x, 8, stride=step), :] = tile
-                for t in range(a):
-                    tile = below[X_FLAG[k] + 8 * t : X_FLAG[k] + 8 * t + 8, :] * valid
-                    flags[pl.ds(FLAG_BASE[k] + t, 8, stride=step), :] = tile
+                    flags[pl.ds(FLAG_BASE[k] + a + x, 8, stride=8 + a), :] = tile
 
     def turn(y, carry):
         for k, (a, b, c) in enumerate(OFFSETS):
@@ -203,6 +239,25 @@
         return carry
 
     lax.fori_loop(0, 8, turn, 0)
+
+
+def band_first(
+    place, u, material, near, far, own_flags, own_incoming,
+    wide, wide_material, sums, near_y, far_y, flags, incoming, shifts, below, above, up, down,
+):
+    zero = place[3]
+    take_along_x(place, near, far, below, above)
+    for k, base in X_FLAG.items():
+        a, b, c = OFFSETS[k]
+        valid = validity(place, b, c)
+        for t in range(a):
+            tile = below[base + 8 * t : base + 8 * t + 8, :] * valid
+            flags[pl.ds(FLAG_BASE[k] + t, 8, stride=8 + a), :] = tile
+            incoming[pl.ds((k * 14 + 3) * 8 + t, 8, stride=8), :] = roll(tile, c)
+    for n in range(3):
+        widen(wide, 128 * n, u, 64 * n, below, above, 24 * n)
+    widen(wide_material, 0, material, 0, below, above, 72)
+    own_shifts(wide, shifts)
     band_sum(flags, incoming, shifts, sums)
     pack_y(wide, sums, up, down)
     up[Y_MATERIAL : Y_MATERIAL + 48, :] = wide_material[80:128, :]
@@ -212,14 +267,19 @@
             copy_rows(up, zero + Y_UP_FLAG[k], flags, zero + FLAG_BASE[k] + (8 - b) * (8 + a), b * (8 + a))
         elif b < 0:
             copy_rows(down, zero + Y_DOWN_FLAG[k], flags, zero + FLAG_BASE[k], -b * (8 + a))
-
-
-def band_next(u, below, above, flags, incoming, wide, sums, up, down, shifts):
+    place_along_y(place, up, down, near_y, far_y)
+
+
+def band_next(
+    place, u, near, far, flags, incoming, wide, sums, near_y, far_y, shifts, below, above, up, down
+):
+    take_along_x(place, near, far, below, above)
     for n in range(3):
         widen(wide, 128 * n, u, 64 * n, below, above, 24 * n)
     own_shifts(wide, shifts)
     band_sum(flags, incoming, shifts, sums)
     pack_y(wide, sums, up, down)
+    place_along_y(place, up, down, near_y, far_y)
 
 
 def wide_tile(wide, before, after, field, column, half):
@@ -230,9 +290,14 @@
     return after[rows(48 * field + 16 * (column - 8) + 8 * half), :]
 
 
-def strip_theta(first, place, wide, flags, incoming, sums, before, after, before_flags, after_flags, *rest):
+def strip_theta(first, place, wide, flags, incoming, sums, near, far, *rest):
+    if not first:
+        before_flags, after_flags, *rest = rest
+    theta, near_x, far_x, before, after, *rest = rest
+    take_along_y(place, near, far, before, after)
     if first:
-        theta, up, down, all_incoming, shifts = rest
+        all_incoming, shifts, up, down = rest
+        before_flags, after_flags = before, after
         own_incoming, incoming = incoming, all_incoming
 
         def keep(k, carry):
@@ -250,13 +315,15 @@
                     tile = after_flags[rows(zero + Y_DOWN_FLAG[k] + n * (8 + a)), :]
                     incoming[rows((k * 14 + 11 + n) * 8), :] = roll(tile, c)
     else:
-        theta, up, down, shifts = rest
+        shifts, up, down = rest
         zero = place[3]
     for column in (-3, -2, -1, 0, 1, 2, 5, 6, 7, 8, 9, 10):
         for n in range(3):
             for half in range(2):
                 tile = wide_tile(wide, before, after, n, column, half)
                 store_shifts(shifts, n, 3, column, half, tile, n == 2)
+    for block in (up, down):
+        block[40:48, :] = jnp.zeros((8, 128), F32)
     for column in range(-3, 11):
         if column < 0:
             total = before[rows(Y_SUM + 8 * (column + 3)), :]
@@ -289,6 +356,7 @@
         theta[rows(8 * (column + 3)), :] = total
         up[rows(zero + 3 * (column + 3), 3), :] = theta[rows(zero + 8 * (column + 3) + 5, 3), :]
         down[rows(zero + 3 * (column + 3), 3), :] = theta[rows(zero + 8 * (column + 3), 3), :]
+    place_along_x(place, up, down, near_x, far_x)
 
 
 def pick(numbers, values):
@@ -299,13 +367,14 @@
 
 
 def advance(last, place, bulk, shear, density, u, v, wide, before, after, wide_material, before_material, after_material,
-            theta, below, above, flags, incoming, *rest):
+            theta, near, far, flags, incoming, *rest):
     if last:
-        new_u, new_v, force, shifts, wide_theta = rest
+        new_u, new_v, force, shifts, wide_theta, below, above = rest
     else:
-        new_u, new_v, up, down, shifts, wide_theta = rest
+        new_u, new_v, near_x, far_x, shifts, wide_theta, below, above, up, down = rest
         force = None
     zero = place[3]
+    take_along_x(place, near, far, below, above)
     twist = [shear[n] * (15.0 / VOLUME) for n in range(CLASSES)]
     press = [(bulk[n] * 3.0 - shear[n] * 5.0) * (3.0 / (VOLUME * VOLUME)) for n in range(CLASSES)]
     inertia = [density[n] for n in range(CLASSES)]
@@ -363,80 +432,113 @@
         for n in range(3):
             up[24 * n : 24 * n + 24, :] = new_u[64 * n + 40 : 64 * n + 64, :]
             down[24 * n : 24 * n + 24, :] = new_u[64 * n : 64 * n + 24, :]
+        place_along_x(place, up, down, near_x, far_x)
 
 
 VMEM = pl.BlockSpec(memory_space=pltpu.VMEM)
 SMEM = pl.BlockSpec(memory_space=pltpu.SMEM)
-
-
-def call(body, outputs, scratch, scalars, *arguments, flops=0):
+IN_HBM = pl.BlockSpec(memory_space=pltpu.HBM)
+
+
+def call(body, outputs, scratch, scalars, *arguments, flops=0, aliases={}, place=VMEM, limit=24):
     shapes = [jax.ShapeDtypeStruct((n, 128), F32) for n in outputs]
     traffic = 512 * sum(outputs) + sum(4 * x.size for x in arguments)
     return pl.pallas_call(
         body,
         out_shape=shapes,
-        in_specs=[SMEM] * scalars + [VMEM] * (len(arguments) - scalars),
+        in_specs=[SMEM] * scalars + [place] * (len(arguments) - scalars),
         out_specs=[VMEM] * len(shapes),
-        scratch_shapes=[pltpu.VMEM((n, 128), F32) for n in scratch],
-        compiler_params=pltpu.CompilerParams(vmem_limit_bytes=24 << 20),
+        scratch_shapes=[pltpu.VMEM((n, 128), F32) if isinstance(n, int) else n for n in scratch],
+        input_output_aliases=aliases,
+        compiler_params=pltpu.CompilerParams(vmem_limit_bytes=limit << 20),
         cost_estimate=pl.CostEstimate(flops=flops, bytes_accessed=traffic, transcendentals=0),
     )(*arguments)
 
 
-def both_ways(up, down, axis):
-    size = lax.axis_size(axis)
-    route = [(i, i + 1) for i in range(size - 1)]
-    from_below = lax.ppermute(up, axis, route)
-    from_above = lax.ppermute(down, axis, [(j, i) for i, j in route])
-    return from_below, from_above
+def swap_pairs(far, near, axis):
+    sizes = {name: lax.axis_size(name) for name in ("gx", "gy")}
+    other = "gy" if axis == "gx" else "gx"
+    size = sizes[axis]
+
+    def device(along, across):
+        at = {axis: along, other: across}
+        return at["gx"] * sizes["gy"] + at["gy"]
+
+    swaps = []
+    for start in (0, 1):
+        pairs = []
+        for across in range(sizes[other]):
+            for along in range(size):
+                partner = along + 1 if (along - start) % 2 == 0 else along - 1
+                inside = 0 <= partner < size
+                target = device(partner, across) if inside else device(along, across ^ 1)
+                pairs.append((device(along, across), target))
+        swaps.append(pairs)
+    far = lax.ppermute(far, ("gx", "gy"), swaps[1])
+    near = lax.ppermute(near, ("gx", "gy"), swaps[0])
+    return far, near
 
 
 def on_device(displacement, velocity, intact, material, bulk_modulus, shear_modulus, density):
     shape = displacement.shape
+    bonds = len(OFFSETS)
     u, v = displacement.reshape(192, 128), velocity.reshape(192, 128)
-    flags_in = intact.reshape(len(OFFSETS) * 64, 128)
     material = material.reshape(64, 128)
     gx, gy = lax.axis_index("gx"), lax.axis_index("gy")
     place = jnp.stack(
-        [gx == lax.axis_size("gx") - 1, gy == 0, gy == lax.axis_size("gy") - 1, gy < 0]
+        [gx == lax.axis_size("gx") - 1, gy == 0, gy == lax.axis_size("gy") - 1, gy < 0, gx % 2 == 0, gx == 0, gy % 2 == 0]
     ).astype(jnp.int32)
     tables = (bulk_modulus, shear_modulus, density)
-    all_rows = len(OFFSETS) * 14 * 8
-    up, down = call(pack_first, [X_UP_ROWS, X_DOWN_ROWS], [], 0, u, material, flags_in)
-    below, above = both_ways(up, down, "gx")
-    wide, wide_material, flags, incoming, sums, up, down = call(
+    all_rows = bonds * 14 * 8
+    counts = [sum(offset[0] == a for offset in OFFSETS) for a in (1, 2, 3)]
+    blocks = [pltpu.VMEM((count, 8 * a, 128), jnp.int32) for a, count in zip((1, 2, 3), counts)]
+    far, near, u, material = call(
+        pack_first, [X_UP_ROWS, X_UP_ROWS, 192, 64],
+        [pltpu.VMEM((64, 128), jnp.int32), *blocks, X_UP_ROWS, X_UP_ROWS, pltpu.SemaphoreType.DMA((5,))],
+        1, place, u, material, intact.reshape(bonds, 64, 128), place=IN_HBM,
+    )
+    flags, incoming = call(
+        prepare_flags, [FLAG_ROWS, all_rows], [], 1, place, intact.reshape(bonds * 64, 128), flops=bonds * 8192 * 4
+    )
+    far, near = swap_pairs(far, near, "gx")
+    wide, wide_material, sums, far, near, flags, incoming = call(
         band_first,
-        [384, 128, FLAG_ROWS, all_rows, 64, Y_UP_ROWS, Y_DOWN_ROWS],
-        [7 * 3 * 224],
-        1, place, u, material, flags_in, below, above,
+        [384, 128, 64, Y_UP_ROWS, Y_UP_ROWS, FLAG_ROWS, all_rows],
+        [7 * 3 * 224, X_UP_ROWS, X_DOWN_ROWS, Y_UP_ROWS, Y_UP_ROWS],
+        1, place, u, material, far, near, flags, incoming, aliases={5: 5, 6: 6},
     )
-    before, after = both_ways(up, down, "gy")
-    first_before, first_after = before, after
+    far, near = swap_pairs(far, near, "gy")
     for step in range(STEPS):
         if step:
-            below, above = both_ways(up, down, "gx")
-            wide, sums, up, down = call(
-                band_next, [384, 64, Y_FLAGS, Y_FLAGS], [7 * 3 * 224], 0, u, below, above, flags, incoming
+            far, near = swap_pairs(far, near, "gx")
+            wide, sums, far, near = call(
+                band_next, [384, 64, Y_MATERIAL, Y_MATERIAL], [7 * 3 * 224, 72, 72, Y_MATERIAL, Y_MATERIAL],
+                1, place, u, far, near, flags, incoming,
             )
-            before, after = both_ways(up, down, "gy")
-        outputs = [112, 48, 48] + ([] if step else [all_rows])
-        theta, up, down, *more = call(
-            functools.partial(strip_theta, step == 0), outputs, [7 * 3 * 224],
-            1, place, wide, flags, incoming, sums, before, after, first_before, first_after,
-        )
-        if not step:
-            incoming = more[0]
-        below, above = both_ways(up, down, "gx")
+            far, near = swap_pairs(far, near, "gy")
+            theta, far, near, before, after = call(
+                functools.partial(strip_theta, False), [112, 48, 48, Y_MATERIAL, Y_MATERIAL], [7 * 3 * 224, 48, 48],
+                1, place, wide, flags, incoming, sums, far, near, first_before, first_after,
+            )
+        else:
+            theta, far, near, before, after, incoming = call(
+                functools.partial(strip_theta, True), [112, 48, 48, Y_UP_ROWS, Y_UP_ROWS, all_rows],
+                [7 * 3 * 224, 48, 48],
+                1, place, wide, flags, incoming, sums, far, near,
+            )
+            first_before, first_after = before, after
+        far, near = swap_pairs(far, near, "gx")
         last = step == STEPS - 1
         u, v, *more = call(
-            functools.partial(advance, last), [192, 192] + ([192] if last else [72, 72]), [7 * 5 * 224, 224],
+            functools.partial(advance, last), [192, 192] + ([192] if last else [72, 72]),
+            [7 * 5 * 224, 224, 48, 48] + ([] if last else [72, 72]),
             4, place, *tables, u, v, wide, before, after, wide_material, first_before, first_after,
-            theta, below, above, flags, incoming,
+            theta, far, near, flags, incoming,
         )
         if last:
             force = more[0]
         else:
-            up, down = more
+            far, near = more
     return u.reshape(shape), v.reshape(shape), force.reshape(shape)
 
 

time: 90.4 us -> 65.7 us (0.73)
  the two profiles are of different devices: /device:TPU:103 before, /device:TPU:102 now
where the time goes in v2:
time: 65.7 us; the launch traced here: 65.4 us
  waiting for transfers between devices  26.3 us (40%)
  Pallas kernels  23.7 us (36%)
  starting transfers between devices  11.3 us (17%)
  local copies, waits for them, and re-layouts  3.34 us (5%)
  between operations  0.78 us (1%)
    ppermute x6, waiting for transfers between devices, swap_pairs(): far = lax.ppermute(far, ('gx', 'gy'), swaps[1])  26.3 us
    pallas_call x8, Pallas kernels, call(): pl.pallas_call(body, out_shape=shapes, in_specs=[SMEM] * scalars + [place...  23.7 us
    ppermute x6, starting transfers between devices, swap_pairs(): far = lax.ppermute(far, ('gx', 'gy'), swaps[1])  7.45 us
    ppermute x6, starting transfers between devices, swap_pairs(): near = lax.ppermute(near, ('gx', 'gy'), swaps[0])  3.86 us
    unnamed x14, local copies, waits for them, and re-layouts  3.23 us
  transfers between devices with their start and end apart: 12, of which 6 were waited for; matrix products, arithmetic and copies ran while one was open for 0% of the time, Pallas kernels for 3%

profile of v2, /device:TPU:102, one launch (start us, length us, event | category | flops | bytes accessed | tf_op | source)
XLA Modules:
  0.0 65.4 jit_solution(108838660929980502)
XLA Ops:
  0.7 0.1 stack.31
  0.8 1.6 %copy-done = s32[61,8,8,128]{3,2,1,0:T(8,128)S(1)} copy-done((s32[61,8,8,128]{3,2,1,0:T(8,128)S(1)}, s32[61,8,8,128]{3,2,1,0:T(8,128)}, u32[]{:S(2)}) %copy-start) | copy-done | bytes 1998872
  2.3 0.9 %copy-done.2 = f32[3,8,8,128]{3,2,1,0:T(8,128)S(1)} copy-done((f32[3,8,8,128]{3,2,1,0:T(8,128)S(1)}, f32[3,8,8,128]{3,2,1,0:T(8,128)}, u32[]{:S(2)}) %copy-start.2) | copy-done | bytes 98328
  3.2 0.8 %copy-done.3 = s32[8,8,128]{2,1,0:T(8,128)S(1)} copy-done((s32[8,8,128]{2,1,0:T(8,128)S(1)}, s32[8,8,128]{2,1,0:T(8,128)}, u32[]{:S(2)}) %copy-start.3) | copy-done | bytes 32792
  4.0 0.9 %shard_map.94 = (f32[656,128]{1,0:T(8,128)S(1)}, f32[656,128]{1,0:T(8,128)S(1)}, f32[192,128]{1,0:T(8,128)S(1)}, f32[64,128]{1,0:T(8,128)S(1)}) custom-call(s32[7]{0:T(128)S(1)} %convert_element_type.3.place, f32[192,128]{1,0:T(8,128)S(1)} %bitcast.18, s32[64,128]{1,0:T(8,128)S(1)} %bitcast.19, s32[61,64,128]{2,1,0:T(8,128)S(1)} %bitcast.15), custom_call_target="tpu_custom_call" | custom-call | bytes 2932764 | tf_op jit(solution)/shard_map/pallas_call | solution.py:446
  4.9 0.9 %collective-permute-start = (f32[656,128]{1,0:T(8,128)S(1)}, f32[656,128]{1,0:T(8,128)S(1)}, u32[]{:S(2)}, u32[]{:S(2)}) collective-permute-start(f32[656,128]{1,0:T(8,128)S(1)} %get-tuple-element.40), channel_id=1, source_target_pairs={{0,1},{32,64},{64,32},{96,128},{128,96},{160,192},{192,160},{224,2... | collective-permute-start | bytes 1007624 | tf_op jit(solution)/shard_map/ppermute | solution.py:477
  5.8 0.9 %collective-permute-start.1 = (f32[656,128]{1,0:T(8,128)S(1)}, f32[656,128]{1,0:T(8,128)S(1)}, u32[]{:S(2)}, u32[]{:S(2)}) collective-permute-start(f32[656,128]{1,0:T(8,128)S(1)} %get-tuple-element.41), channel_id=1, source_target_pairs={{0,32},{32,0},{64,96},{96,64},{128,160},{160,128},{192,224},{224,1... | collective-permute-start | bytes 1007624 | tf_op jit(solution)/shard_map/ppermute | solution.py:478
  6.6 1.7 %shard_map.95 = (f32[4464,128]{1,0:T(8,128)S(1)}, f32[6832,128]{1,0:T(8,128)S(1)}) custom-call(s32[7]{0:T(128)S(1)} %convert_element_type.3.place, s32[3904,128]{1,0:T(8,128)S(1)} %bitcast.16), custom_call_target="tpu_custom_call" | custom-call | flops 1998848 | bytes 7782428 | tf_op jit(solution)/shard_map/pallas_call | solution.py:446
  8.4 3.7 %collective-permute-done.near = f32[656,128]{1,0:T(8,128)S(1)} collective-permute-done((f32[656,128]{1,0:T(8,128)S(1)}, f32[656,128]{1,0:T(8,128)S(1)}, u32[]{:S(2)}, u32[]{:S(2)}) %collective-permute-start) | collective-permute-done | bytes 335904 | tf_op jit(solution)/shard_map/ppermute | solution.py:477
  12.1 3.6 %shard_map.96 = (f32[384,128]{1,0:T(8,128)S(1)}, f32[128,128]{1,0:T(8,128)S(1)}, f32[64,128]{1,0:T(8,128)S(1)}, f32[608,128]{1,0:T(8,128)S(1)}, f32[608,128]{1,0...) custom-call(s32[7]{0:T(128)S(1)} %convert_element_type.3.place, ...), custom_call_target="tpu_custom_call", output_to_operand_aliasing={{5}: (5, {}), {6}: (6, {})} | custom-call | bytes 13287452 | tf_op jit(solution)/shard_map/pallas_call | solution.py:446
  15.7 0.0 copy-start.1
  15.7 0.0 copy-start.4
  15.7 0.0 copy-start.5
  15.7 0.0 copy-start.6
  15.7 3.1 %collective-permute-start.2 = (f32[608,128]{1,0:T(8,128)S(1)}, f32[608,128]{1,0:T(8,128)S(1)}, u32[]{:S(2)}, u32[]{:S(2)}) collective-permute-start(f32[608,128]{1,0:T(8,128)S(1)} %get-tuple-element.48), channel_id=1, source_target_pairs={{0,32},{1,2},{2,1},{3,4},{4,3},{5,6},{6,5},{7,8},{8,7},{9,10},{10,... | collective-permute-start | bytes 933896 | tf_op jit(solution)/shard_map/ppermute | solution.py:477
  18.9 9.2 %collective-permute-done.2.near = f32[608,128]{1,0:T(8,128)S(1)} collective-permute-done((f32[608,128]{1,0:T(8,128)S(1)}, f32[608,128]{1,0:T(8,128)S(1)}, u32[]{:S(2)}, u32[]{:S(2)}) %collective-permute-start.2) | collective-permute-done | bytes 311328 | tf_op jit(solution)/shard_map/ppermute | solution.py:477
  28.1 2.1 %shard_map.97 = (f32[112,128]{1,0:T(8,128)S(1)}, f32[48,128]{1,0:T(8,128)S(1)}, f32[48,128]{1,0:T(8,128)S(1)}, f32[608,128]{1,0:T(8,128)S(1)}, f32[608,128]{1,0:T(8,128)S(1)}, /*index=5*/f32[6832,128]{1,0:T(8,128)S(1)}) custom-call(s32[7]{0:T(128)S(1)} %convert_element_type.3.place, f32[384,128]{1,0:T(8,128)S(1)} %get-tuple-element.44.wide, ...), custom_call_target="tpu_custom_call" | custom-call | bytes 10862620 | tf_op jit(solution)/shard_map/pallas_call | solution.py:446
  30.2 0.1 collective-permute-start.4
  30.3 1.5 %collective-permute-start.5 = (f32[48,128]{1,0:T(8,128)S(1)}, f32[48,128]{1,0:T(8,128)S(1)}, u32[]{:S(2)}, u32[]{:S(2)}) collective-permute-start(f32[48,128]{1,0:T(8,128)S(1)} %get-tuple-element.55), channel_id=1, source_target_pairs={{0,32},{32,0},{64,96},{96,64},{128,160},{160,128},{192,224},{224,1... | collective-permute-start | bytes 73736 | tf_op jit(solution)/shard_map/ppermute | solution.py:478
  31.8 2.3 %collective-permute-done.4.near = f32[48,128]{1,0:T(8,128)S(1)} collective-permute-done((f32[48,128]{1,0:T(8,128)S(1)}, f32[48,128]{1,0:T(8,128)S(1)}, u32[]{:S(2)}, u32[]{:S(2)}) %collective-permute-start.4) | collective-permute-done | bytes 24608 | tf_op jit(solution)/shard_map/ppermute | solution.py:477
  34.1 4.9 %shard_map.98 = (f32[192,128]{1,0:T(8,128)S(1)}, f32[192,128]{1,0:T(8,128)S(1)}, f32[72,128]{1,0:T(8,128)S(1)}, f32[72,128]{1,0:T(8,128)S(1)}) custom-call(s32[7]{0:T(128)S(1)} %convert_element_type.3.place, f32[8]{0:T(128)S(1)} %copy-done.4, f32[8]{0:T(128)S(1)} %copy-done.5, f32[8]{0:T(128)S(1)} %copy-done.6, f32[192,128]{1,0:T(8,128)S(1)} %get-tuple-element.38.u, ...), custom_call_target="tpu_custom_call" | custom-call | bytes 7864444 | tf_op jit(solution)/shard_map/pallas_call | solution.py:446
  39.0 0.1 collective-permute-start.6
  39.1 1.0 %collective-permute-start.7 = (f32[72,128]{1,0:T(8,128)S(1)}, f32[72,128]{1,0:T(8,128)S(1)}, u32[]{:S(2)}, u32[]{:S(2)}) collective-permute-start(f32[72,128]{1,0:T(8,128)S(1)} %get-tuple-element.60), channel_id=1, source_target_pairs={{0,32},{32,0},{64,96},{96,64},{128,160},{160,128},{192,224},{224,1... | collective-permute-start | bytes 110600 | tf_op jit(solution)/shard_map/ppermute | solution.py:478
  40.1 3.0 %collective-permute-done.6.near = f32[72,128]{1,0:T(8,128)S(1)} collective-permute-done((f32[72,128]{1,0:T(8,128)S(1)}, f32[72,128]{1,0:T(8,128)S(1)}, u32[]{:S(2)}, u32[]{:S(2)}) %collective-permute-start.6) | collective-permute-done | bytes 36896 | tf_op jit(solution)/shard_map/ppermute | solution.py:477
  43.0 3.4 %shard_map.99 = (f32[384,128]{1,0:T(8,128)S(1)}, f32[64,128]{1,0:T(8,128)S(1)}, f32[168,128]{1,0:T(8,128)S(1)}, f32[168,128]{1,0:T(8,128)S(1)}) custom-call(s32[7]{0:T(128)S(1)} %convert_element_type.3.place, f32[192,128]{1,0:T(8,128)S(1)} %get-tuple-element.57.u, f32[72,128]{1,0:T(8,128)S(1)} %collective-permute-done.6.near, ...), custom_call_target="tpu_custom_call" | custom-call | bytes 6357020 | tf_op jit(solution)/shard_map/pallas_call | solution.py:446
  46.4 3.1 %collective-permute-start.8 = (f32[168,128]{1,0:T(8,128)S(1)}, f32[168,128]{1,0:T(8,128)S(1)}, u32[]{:S(2)}, u32[]{:S(2)}) collective-permute-start(f32[168,128]{1,0:T(8,128)S(1)} %get-tuple-element.63), channel_id=1, source_target_pairs={{0,32},{1,2},{2,1},{3,4},{4,3},{5,6},{6,5},{7,8},{8,7},{9,10},{10,... | collective-permute-start | bytes 258056 | tf_op jit(solution)/shard_map/ppermute | solution.py:477
  49.6 4.8 %collective-permute-done.8.near = f32[168,128]{1,0:T(8,128)S(1)} collective-permute-done((f32[168,128]{1,0:T(8,128)S(1)}, f32[168,128]{1,0:T(8,128)S(1)}, u32[]{:S(2)}, u32[]{:S(2)}) %collective-permute-start.8) | collective-permute-done | bytes 86048 | tf_op jit(solution)/shard_map/ppermute | solution.py:477
  54.3 1.6 %shard_map.100 = (f32[112,128]{1,0:T(8,128)S(1)}, f32[48,128]{1,0:T(8,128)S(1)}, f32[48,128]{1,0:T(8,128)S(1)}, f32[168,128]{1,0:T(8,128)S(1)}, f32[168,128]{1,0:T(8,128)S(1)}) custom-call(s32[7]{0:T(128)S(1)} %convert_element_type.3.place, f32[384,128]{1,0:T(8,128)S(1)} %get-tuple-element.61.wide, f32[4464,128]{1,0:T(8,128)S(1)} %get-tuple-element.45.flags, ...), custom_call_target="tpu_custom_call" | custom-call | bytes 7086108 | tf_op jit(solution)/shard_map/pallas_call | solution.py:446
  56.0 0.1 collective-permute-start.10
  56.1 0.5 collective-permute-start.11
  56.5 3.3 %collective-permute-done.10.near = f32[48,128]{1,0:T(8,128)S(1)} collective-permute-done((f32[48,128]{1,0:T(8,128)S(1)}, f32[48,128]{1,0:T(8,128)S(1)}, u32[]{:S(2)}, u32[]{:S(2)}) %collective-permute-start.10) | collective-permute-done | bytes 24608 | tf_op jit(solution)/shard_map/ppermute | solution.py:477
  59.9 5.6 %shard_map.101 = (f32[192,128]{1,0:T(8,128)}, f32[192,128]{1,0:T(8,128)}, f32[192,128]{1,0:T(8,128)}) custom-call(s32[7]{0:T(128)S(1)} %convert_element_type.3.place, f32[8]{0:T(128)S(1)} %copy-done.4, f32[8]{0:T(128)S(1)} %copy-done.5, f32[8]{0:T(128)S(1)} %copy-done.6, f32[192,128]{1,0:T(8,128)S(1)} %get-tuple-element.57.u, ...), custom_call_target="tpu_custom_call" | custom-call | bytes 7438460 | tf_op jit(solution)/shard_map/pallas_call | solution.py:446
  (16 shorter events, 0.0 us)
Async XLA Ops:
  0.8 1.6 %copy-start = (s32[61,8,8,128]{3,2,1,0:T(8,128)S(1)}, s32[61,8,8,128]{3,2,1,0:T(8,128)}, u32[]{:S(2)}) copy-start(s32[61,8,8,128]{3,2,1,0:T(8,128)} %param.9) | copy-start | bytes 5996548
  2.3 0.9 %copy-start.2 = (f32[3,8,8,128]{3,2,1,0:T(8,128)S(1)}, f32[3,8,8,128]{3,2,1,0:T(8,128)}, u32[]{:S(2)}) copy-start(f32[3,8,8,128]{3,2,1,0:T(8,128)} %param.7) | copy-start | bytes 294916
  3.2 0.8 %copy-start.3 = (s32[8,8,128]{2,1,0:T(8,128)S(1)}, s32[8,8,128]{2,1,0:T(8,128)}, u32[]{:S(2)}) copy-start(s32[8,8,128]{2,1,0:T(8,128)} %param.10) | copy-start | bytes 98308
  4.9 7.2 %collective-permute-start = (f32[656,128]{1,0:T(8,128)S(1)}, f32[656,128]{1,0:T(8,128)S(1)}, u32[]{:S(2)}, u32[]{:S(2)}) collective-permute-start(f32[656,128]{1,0:T(8,128)S(1)} %get-tuple-element.40), channel_id=1, source_target_pairs={{0,1},{32,64},{64,32},{96,128},{128,96},{160,192},{192,160},{224,2... | collective-permute-start | bytes 1007624 | tf_op jit(solution)/shard_map/ppermute | solution.py:477
  5.8 6.3 %collective-permute-start.1 = (f32[656,128]{1,0:T(8,128)S(1)}, f32[656,128]{1,0:T(8,128)S(1)}, u32[]{:S(2)}, u32[]{:S(2)}) collective-permute-start(f32[656,128]{1,0:T(8,128)S(1)} %get-tuple-element.41), channel_id=1, source_target_pairs={{0,32},{32,0},{64,96},{96,64},{128,160},{160,128},{192,224},{224,1... | collective-permute-start | bytes 1007624 | tf_op jit(solution)/shard_map/ppermute | solution.py:478
  15.7 18.4 %copy-start.1 = (f32[3,8,8,128]{3,2,1,0:T(8,128)S(1)}, f32[3,8,8,128]{3,2,1,0:T(8,128)}, u32[]{:S(2)}) copy-start(f32[3,8,8,128]{3,2,1,0:T(8,128)} %param.8) | copy-start | bytes 294916
  15.7 18.4 %copy-start.4 = (f32[8]{0:T(128)S(1)}, f32[8]{0:T(128)}, u32[]{:S(2)}) copy-start(f32[8]{0:T(128)} %bulk.3) | copy-start | bytes 100
  15.7 18.4 %copy-start.5 = (f32[8]{0:T(128)S(1)}, f32[8]{0:T(128)}, u32[]{:S(2)}) copy-start(f32[8]{0:T(128)} %shear.3) | copy-start | bytes 100
  15.7 18.4 %copy-start.6 = (f32[8]{0:T(128)S(1)}, f32[8]{0:T(128)}, u32[]{:S(2)}) copy-start(f32[8]{0:T(128)} %density.3) | copy-start | bytes 100
  15.7 12.3 %collective-permute-start.2 = (f32[608,128]{1,0:T(8,128)S(1)}, f32[608,128]{1,0:T(8,128)S(1)}, u32[]{:S(2)}, u32[]{:S(2)}) collective-permute-start(f32[608,128]{1,0:T(8,128)S(1)} %get-tuple-element.48), channel_id=1, source_target_pairs={{0,32},{1,2},{2,1},{3,4},{4,3},{5,6},{6,5},{7,8},{8,7},{9,10},{10,... | collective-permute-start | bytes 933896 | tf_op jit(solution)/shard_map/ppermute | solution.py:477
  18.9 9.2 %collective-permute-start.3 = (f32[608,128]{1,0:T(8,128)S(1)}, f32[608,128]{1,0:T(8,128)S(1)}, u32[]{:S(2)}, u32[]{:S(2)}) collective-permute-start(f32[608,128]{1,0:T(8,128)S(1)} %get-tuple-element.49), channel_id=1, source_target_pairs={{0,1},{1,0},{2,3},{3,2},{4,5},{5,4},{6,7},{7,6},{8,9},{9,8},{10,11... | collective-permute-start | bytes 933896 | tf_op jit(solution)/shard_map/ppermute | solution.py:478
  30.2 3.9 %collective-permute-start.4 = (f32[48,128]{1,0:T(8,128)S(1)}, f32[48,128]{1,0:T(8,128)S(1)}, u32[]{:S(2)}, u32[]{:S(2)}) collective-permute-start(f32[48,128]{1,0:T(8,128)S(1)} %get-tuple-element.54), channel_id=1, source_target_pairs={{0,1},{32,64},{64,32},{96,128},{128,96},{160,192},{192,160},{224,2... | collective-permute-start | bytes 73736 | tf_op jit(solution)/shard_map/ppermute | solution.py:477
  30.3 3.8 %collective-permute-start.5 = (f32[48,128]{1,0:T(8,128)S(1)}, f32[48,128]{1,0:T(8,128)S(1)}, u32[]{:S(2)}, u32[]{:S(2)}) collective-permute-start(f32[48,128]{1,0:T(8,128)S(1)} %get-tuple-element.55), channel_id=1, source_target_pairs={{0,32},{32,0},{64,96},{96,64},{128,160},{160,128},{192,224},{224,1... | collective-permute-start | bytes 73736 | tf_op jit(solution)/shard_map/ppermute | solution.py:478
  39.0 4.0 %collective-permute-start.6 = (f32[72,128]{1,0:T(8,128)S(1)}, f32[72,128]{1,0:T(8,128)S(1)}, u32[]{:S(2)}, u32[]{:S(2)}) collective-permute-start(f32[72,128]{1,0:T(8,128)S(1)} %get-tuple-element.59), channel_id=1, source_target_pairs={{0,1},{32,64},{64,32},{96,128},{128,96},{160,192},{192,160},{224,2... | collective-permute-start | bytes 110600 | tf_op jit(solution)/shard_map/ppermute | solution.py:477
  39.1 3.9 %collective-permute-start.7 = (f32[72,128]{1,0:T(8,128)S(1)}, f32[72,128]{1,0:T(8,128)S(1)}, u32[]{:S(2)}, u32[]{:S(2)}) collective-permute-start(f32[72,128]{1,0:T(8,128)S(1)} %get-tuple-element.60), channel_id=1, source_target_pairs={{0,32},{32,0},{64,96},{96,64},{128,160},{160,128},{192,224},{224,1... | collective-permute-start | bytes 110600 | tf_op jit(solution)/shard_map/ppermute | solution.py:478
  46.4 7.9 %collective-permute-start.8 = (f32[168,128]{1,0:T(8,128)S(1)}, f32[168,128]{1,0:T(8,128)S(1)}, u32[]{:S(2)}, u32[]{:S(2)}) collective-permute-start(f32[168,128]{1,0:T(8,128)S(1)} %get-tuple-element.63), channel_id=1, source_target_pairs={{0,32},{1,2},{2,1},{3,4},{4,3},{5,6},{6,5},{7,8},{8,7},{9,10},{10,... | collective-permute-start | bytes 258056 | tf_op jit(solution)/shard_map/ppermute | solution.py:477
  49.6 4.8 %collective-permute-start.9 = (f32[168,128]{1,0:T(8,128)S(1)}, f32[168,128]{1,0:T(8,128)S(1)}, u32[]{:S(2)}, u32[]{:S(2)}) collective-permute-start(f32[168,128]{1,0:T(8,128)S(1)} %get-tuple-element.64), channel_id=1, source_target_pairs={{0,1},{1,0},{2,3},{3,2},{4,5},{5,4},{6,7},{7,6},{8,9},{9,8},{10,11... | collective-permute-start | bytes 258056 | tf_op jit(solution)/shard_map/ppermute | solution.py:478
  56.0 3.9 %collective-permute-start.10 = (f32[48,128]{1,0:T(8,128)S(1)}, f32[48,128]{1,0:T(8,128)S(1)}, u32[]{:S(2)}, u32[]{:S(2)}) collective-permute-start(f32[48,128]{1,0:T(8,128)S(1)} %get-tuple-element.68), channel_id=1, source_target_pairs={{0,1},{32,64},{64,32},{96,128},{128,96},{160,192},{192,160},{224,2... | collective-permute-start | bytes 73736 | tf_op jit(solution)/shard_map/ppermute | solution.py:477
  56.1 3.8 %collective-permute-start.11 = (f32[48,128]{1,0:T(8,128)S(1)}, f32[48,128]{1,0:T(8,128)S(1)}, u32[]{:S(2)}, u32[]{:S(2)}) collective-permute-start(f32[48,128]{1,0:T(8,128)S(1)} %get-tuple-element.69), channel_id=1, source_target_pairs={{0,32},{32,0},{64,96},{96,64},{128,160},{160,128},{192,224},{224,1... | collective-permute-start | bytes 73736 | tf_op jit(solution)/shard_map/ppermute | solution.py:478

commit v3 on v2

--- a/solution.py
+++ b/solution.py
@@ -55,7 +55,18 @@
     elif _b < 0:
         Y_DOWN_FLAG[_k] = _down
         _down += -_b * (8 + _a)
-Y_UP_ROWS, Y_DOWN_ROWS = -(-_up // 8) * 8, -(-_down // 8) * 8
+Y_ROWS = -(-max(_up, _down) // 8) * 8
+
+EARLY, CORNER = {}, {}
+for _sign in (1, -1):
+    _early, _corner = 0, Y_FLAGS
+    for _k, (_a, _b, _c) in enumerate(OFFSETS):
+        if _b * _sign > 0:
+            EARLY[_k], CORNER[_k] = _early, _corner
+            _early += abs(_b) * 8
+            _corner += abs(_b) * _a
+EARLY_ROWS = max(EARLY[k] + 8 * abs(OFFSETS[k][1]) for k in EARLY)
+CORNER_ROWS = -(-max(CORNER[k] + abs(OFFSETS[k][1]) * OFFSETS[k][0] for k in CORNER) // 8) * 8
 
 
 def rows(start, count=8):
@@ -74,6 +85,13 @@
     return value if shift % 128 == 0 else pltpu.roll(value, shift % 128, 1)
 
 
+def position():
+    gx, gy = lax.axis_index("gx"), lax.axis_index("gy")
+    last_x, last_y = lax.axis_size("gx") - 1, lax.axis_size("gy") - 1
+    flags = [gx == last_x, gy == 0, gy == last_y, gy < 0, gx % 2 == 0, gx == 0, gy % 2 == 0]
+    return [jnp.where(flag, 1, 0) for flag in flags]
+
+
 def place_messages(even, up, down, far, near):
     near[...] = jnp.where(even, up[...], down[...])
     far[...] = jnp.where(even, down[...], up[...])
@@ -101,7 +119,8 @@
     take_messages(place[6] == 1, place[1] == 1, place[2] == 1, *blocks)
 
 
-def pack_first(place, u_in, material_in, intact_in, near, far, u, material, material_copy, ones, twos, threes, up, down, done):
+def pack_first(u_in, material_in, intact_in, near, far, u, material_copy, ones, twos, threes, up, down, done):
+    place = position()
     parts = [
         pltpu.make_async_copy(u_in, u, done.at[0]),
         pltpu.make_async_copy(material_in, material_copy, done.at[1]),
@@ -117,7 +136,6 @@
     for n in range(3):
         up[24 * n : 24 * n + 24, :] = u[64 * n + 40 : 64 * n + 64, :]
         down[24 * n : 24 * n + 24, :] = u[64 * n : 64 * n + 24, :]
-    material[...] = material_copy[...].astype(F32)
     up[72:96, :] = material_copy[40:64, :].astype(F32)
     down[72:96, :] = material_copy[0:24, :].astype(F32)
     at = 96
@@ -217,7 +235,13 @@
     return jnp.where(inside, 1.0, 0.0).astype(F32)
 
 
-def prepare_flags(place, intact, flags, incoming):
+def prepare_flags(
+    u_in, material_in, intact, flags, incoming, u, material, near, far, up, down
+):
+    u[...] = u_in[...]
+    material[...] = material_in[...].astype(F32)
+    place = position()
+    zero = place[3]
     last_x = jnp.where(place[0] == 1, 0.0, 1.0)
     for b in range(-3, 4):
         for c in range(-3, 4):
@@ -239,12 +263,20 @@
         return carry
 
     lax.fori_loop(0, 8, turn, 0)
+    for k, at in EARLY.items():
+        a, b, c = OFFSETS[k]
+        for n in range(abs(b)):
+            column = 8 - b + n if b > 0 else n
+            tile = flags[rows(zero + FLAG_BASE[k] + column * (8 + a) + a), :]
+            (up if b > 0 else down)[at + 8 * n : at + 8 * n + 8, :] = tile
+    place_along_y(place, up, down, near, far)
 
 
 def band_first(
-    place, u, material, near, far, own_flags, own_incoming,
+    u, material, near, far, own_flags, own_incoming,
     wide, wide_material, sums, near_y, far_y, flags, incoming, shifts, below, above, up, down,
 ):
+    place = position()
     zero = place[3]
     take_along_x(place, near, far, below, above)
     for k, base in X_FLAG.items():
@@ -262,17 +294,18 @@
     pack_y(wide, sums, up, down)
     up[Y_MATERIAL : Y_MATERIAL + 48, :] = wide_material[80:128, :]
     down[Y_MATERIAL : Y_MATERIAL + 48, :] = wide_material[0:48, :]
-    for k, (a, b, c) in enumerate(OFFSETS):
-        if b > 0:
-            copy_rows(up, zero + Y_UP_FLAG[k], flags, zero + FLAG_BASE[k] + (8 - b) * (8 + a), b * (8 + a))
-        elif b < 0:
-            copy_rows(down, zero + Y_DOWN_FLAG[k], flags, zero + FLAG_BASE[k], -b * (8 + a))
+    for k, at in CORNER.items():
+        a, b, c = OFFSETS[k]
+        for n in range(abs(b) if a else 0):
+            column = 8 - b + n if b > 0 else n
+            copy_rows(up if b > 0 else down, zero + at + a * n, flags, zero + FLAG_BASE[k] + column * (8 + a), a)
     place_along_y(place, up, down, near_y, far_y)
 
 
 def band_next(
-    place, u, near, far, flags, incoming, wide, sums, near_y, far_y, shifts, below, above, up, down
+    u, near, far, flags, incoming, wide, sums, near_y, far_y, shifts, below, above, up, down
 ):
+    place = position()
     take_along_x(place, near, far, below, above)
     for n in range(3):
         widen(wide, 128 * n, u, 64 * n, below, above, 24 * n)
@@ -290,14 +323,30 @@
     return after[rows(48 * field + 16 * (column - 8) + 8 * half), :]
 
 
-def strip_theta(first, place, wide, flags, incoming, sums, near, far, *rest):
+def strip_theta(first, wide, flags, incoming, sums, near, far, *rest):
+    place = position()
     if not first:
         before_flags, after_flags, *rest = rest
+    else:
+        early_near, early_far, *rest = rest
     theta, near_x, far_x, before, after, *rest = rest
-    take_along_y(place, near, far, before, after)
+    zero = place[3]
     if first:
-        all_incoming, shifts, up, down = rest
+        all_incoming, shifts, up, down, early_before, early_after, late_before, late_after = rest
+        take_along_y(place, early_near, early_far, early_before, early_after)
+        take_along_y(place, near, far, late_before, late_after)
         before_flags, after_flags = before, after
+        before[0:Y_FLAGS, :] = late_before[0:Y_FLAGS, :]
+        after[0:Y_FLAGS, :] = late_after[0:Y_FLAGS, :]
+        for k, at in EARLY.items():
+            a, b, c = OFFSETS[k]
+            target, to = (before, Y_UP_FLAG[k]) if b > 0 else (after, Y_DOWN_FLAG[k])
+            early, late = (early_before, late_before) if b > 0 else (early_after, late_after)
+            for n in range(abs(b)):
+                block = zero + to + n * (8 + a)
+                if a:
+                    copy_rows(target, block, late, zero + CORNER[k] + a * n, a)
+                copy_rows(target, block + a, early, at + 8 * n, 8)
         own_incoming, incoming = incoming, all_incoming
 
         def keep(k, carry):
@@ -305,7 +354,6 @@
             return carry
 
         lax.fori_loop(0, len(OFFSETS), keep, 0)
-        zero = place[3]
         for k, (a, b, c) in enumerate(OFFSETS):
             for n in range(abs(b)):
                 if b > 0:
@@ -315,8 +363,8 @@
                     tile = after_flags[rows(zero + Y_DOWN_FLAG[k] + n * (8 + a)), :]
                     incoming[rows((k * 14 + 11 + n) * 8), :] = roll(tile, c)
     else:
+        take_along_y(place, near, far, before, after)
         shifts, up, down = rest
-        zero = place[3]
     for column in (-3, -2, -1, 0, 1, 2, 5, 6, 7, 8, 9, 10):
         for n in range(3):
             for half in range(2):
@@ -360,24 +408,25 @@
 
 
 def pick(numbers, values):
-    result = jnp.full(numbers.shape, values[CLASSES - 1], F32)
+    result = jnp.broadcast_to(values[CLASSES - 1 : CLASSES, :], numbers.shape)
     for n in range(CLASSES - 1):
-        result = jnp.where(numbers == float(n), values[n], result)
+        result = jnp.where(numbers == float(n), values[n : n + 1, :], result)
     return result
 
 
-def advance(last, place, bulk, shear, density, u, v, wide, before, after, wide_material, before_material, after_material,
+def advance(last, table, u, v, wide, before, after, wide_material, before_material, after_material,
             theta, near, far, flags, incoming, *rest):
     if last:
         new_u, new_v, force, shifts, wide_theta, below, above = rest
     else:
         new_u, new_v, near_x, far_x, shifts, wide_theta, below, above, up, down = rest
         force = None
+    place = position()
     zero = place[3]
     take_along_x(place, near, far, below, above)
-    twist = [shear[n] * (15.0 / VOLUME) for n in range(CLASSES)]
-    press = [(bulk[n] * 3.0 - shear[n] * 5.0) * (3.0 / (VOLUME * VOLUME)) for n in range(CLASSES)]
-    inertia = [density[n] for n in range(CLASSES)]
+    bulk, shear, inertia = table[0:8, :], table[8:16, :], table[16:24, :]
+    twist = shear * (15.0 / VOLUME)
+    press = (bulk * 3.0 - shear * 5.0) * (3.0 / (VOLUME * VOLUME))
     for column in range(-3, 11):
         at = 16 * (column + 3)
         wide_theta[rows(zero + at + 3), :] = theta[8 * (column + 3) : 8 * (column + 3) + 8, :]
@@ -436,17 +485,16 @@
 
 
 VMEM = pl.BlockSpec(memory_space=pltpu.VMEM)
-SMEM = pl.BlockSpec(memory_space=pltpu.SMEM)
 IN_HBM = pl.BlockSpec(memory_space=pltpu.HBM)
 
 
-def call(body, outputs, scratch, scalars, *arguments, flops=0, aliases={}, place=VMEM, limit=24):
+def call(body, outputs, scratch, *arguments, flops=0, aliases={}, place=VMEM, limit=24):
     shapes = [jax.ShapeDtypeStruct((n, 128), F32) for n in outputs]
     traffic = 512 * sum(outputs) + sum(4 * x.size for x in arguments)
     return pl.pallas_call(
         body,
         out_shape=shapes,
-        in_specs=[SMEM] * scalars + [place] * (len(arguments) - scalars),
+        in_specs=[place] * len(arguments),
         out_specs=[VMEM] * len(shapes),
         scratch_shapes=[pltpu.VMEM((n, 128), F32) if isinstance(n, int) else n for n in scratch],
         input_output_aliases=aliases,
@@ -484,28 +532,29 @@
     bonds = len(OFFSETS)
     u, v = displacement.reshape(192, 128), velocity.reshape(192, 128)
     material = material.reshape(64, 128)
-    gx, gy = lax.axis_index("gx"), lax.axis_index("gy")
-    place = jnp.stack(
-        [gx == lax.axis_size("gx") - 1, gy == 0, gy == lax.axis_size("gy") - 1, gy < 0, gx % 2 == 0, gx == 0, gy % 2 == 0]
-    ).astype(jnp.int32)
-    tables = (bulk_modulus, shear_modulus, density)
+    table = jnp.broadcast_to(jnp.concatenate([bulk_modulus, shear_modulus, density])[:, None], (3 * CLASSES, 128))
     all_rows = bonds * 14 * 8
     counts = [sum(offset[0] == a for offset in OFFSETS) for a in (1, 2, 3)]
     blocks = [pltpu.VMEM((count, 8 * a, 128), jnp.int32) for a, count in zip((1, 2, 3), counts)]
-    far, near, u, material = call(
-        pack_first, [X_UP_ROWS, X_UP_ROWS, 192, 64],
-        [pltpu.VMEM((64, 128), jnp.int32), *blocks, X_UP_ROWS, X_UP_ROWS, pltpu.SemaphoreType.DMA((5,))],
-        1, place, u, material, intact.reshape(bonds, 64, 128), place=IN_HBM,
+    far, near = call(
+        pack_first, [X_UP_ROWS, X_UP_ROWS],
+        [
+            pltpu.VMEM((192, 128), F32), pltpu.VMEM((64, 128), jnp.int32), *blocks, X_UP_ROWS, X_UP_ROWS,
+            pltpu.SemaphoreType.DMA((5,)),
+        ],
+        u, material, intact.reshape(bonds, 64, 128), place=IN_HBM, limit=59,
     )
-    flags, incoming = call(
-        prepare_flags, [FLAG_ROWS, all_rows], [], 1, place, intact.reshape(bonds * 64, 128), flops=bonds * 8192 * 4
+    flags, incoming, u, material, early_far, early_near = call(
+        prepare_flags, [FLAG_ROWS, all_rows, 192, 64, EARLY_ROWS, EARLY_ROWS], [EARLY_ROWS, EARLY_ROWS],
+        u, material, intact.reshape(bonds * 64, 128), flops=bonds * 8192 * 4,
     )
     far, near = swap_pairs(far, near, "gx")
+    early_far, early_near = swap_pairs(early_far, early_near, "gy")
     wide, wide_material, sums, far, near, flags, incoming = call(
         band_first,
-        [384, 128, 64, Y_UP_ROWS, Y_UP_ROWS, FLAG_ROWS, all_rows],
-        [7 * 3 * 224, X_UP_ROWS, X_DOWN_ROWS, Y_UP_ROWS, Y_UP_ROWS],
-        1, place, u, material, far, near, flags, incoming, aliases={5: 5, 6: 6},
+        [384, 128, 64, CORNER_ROWS, CORNER_ROWS, FLAG_ROWS, all_rows],
+        [7 * 3 * 224, X_UP_ROWS, X_DOWN_ROWS, CORNER_ROWS, CORNER_ROWS],
+        u, material, far, near, flags, incoming, aliases={4: 5, 5: 6},
     )
     far, near = swap_pairs(far, near, "gy")
     for step in range(STEPS):
@@ -513,18 +562,18 @@
             far, near = swap_pairs(far, near, "gx")
             wide, sums, far, near = call(
                 band_next, [384, 64, Y_MATERIAL, Y_MATERIAL], [7 * 3 * 224, 72, 72, Y_MATERIAL, Y_MATERIAL],
-                1, place, u, far, near, flags, incoming,
+                u, far, near, flags, incoming,
             )
             far, near = swap_pairs(far, near, "gy")
             theta, far, near, before, after = call(
                 functools.partial(strip_theta, False), [112, 48, 48, Y_MATERIAL, Y_MATERIAL], [7 * 3 * 224, 48, 48],
-                1, place, wide, flags, incoming, sums, far, near, first_before, first_after,
+                wide, flags, incoming, sums, far, near, first_before, first_after,
             )
         else:
             theta, far, near, before, after, incoming = call(
-                functools.partial(strip_theta, True), [112, 48, 48, Y_UP_ROWS, Y_UP_ROWS, all_rows],
-                [7 * 3 * 224, 48, 48],
-                1, place, wide, flags, incoming, sums, far, near,
+                functools.partial(strip_theta, True), [112, 48, 48, Y_ROWS, Y_ROWS, all_rows],
+                [7 * 3 * 224, 48, 48, EARLY_ROWS, EARLY_ROWS, CORNER_ROWS, CORNER_ROWS],
+                wide, flags, incoming, sums, far, near, early_far, early_near,
             )
             first_before, first_after = before, after
         far, near = swap_pairs(far, near, "gx")
@@ -532,7 +581,7 @@
         u, v, *more = call(
             functools.partial(advance, last), [192, 192] + ([192] if last else [72, 72]),
             [7 * 5 * 224, 224, 48, 48] + ([] if last else [72, 72]),
-            4, place, *tables, u, v, wide, before, after, wide_material, first_before, first_after,
+            table, u, v, wide, before, after, wide_material, first_before, first_after,
             theta, far, near, flags, incoming,
         )
         if last:

time: 65.7 us -> 56.9 us (0.87)
  waiting for transfers between devices: 26.3 us -> 20.1 us
  Pallas kernels: 23.7 us -> 20.7 us
  starting transfers between devices: 11.3 us -> 13.3 us
  local copies, waits for them, and re-layouts: 3.34 us -> 1.75 us
    ppermute x6 -> x7, waiting for transfers between devices: 26.3 us -> 20.1 us  [swap_pairs(): far = lax.ppermute(far, ('gx', 'gy'), swaps[1])]
    pallas_call x8, Pallas kernels: 23.7 us -> 20.7 us  [call(): pl.pallas_call(body, out_shape=shapes, in_specs=[place] * len(arguments),...]
    ppermute x6 -> x7, starting transfers between devices: 7.45 us -> 9.98 us  [swap_pairs(): far = lax.ppermute(far, ('gx', 'gy'), swaps[1])]
    unnamed x14, local copies, waits for them, and re-layouts: 3.23 us -> 1.68 us
    ppermute x6 -> x7, starting transfers between devices: 3.86 us -> 3.33 us  [swap_pairs(): near = lax.ppermute(near, ('gx', 'gy'), swaps[0])]
  transfers between devices with their start and end apart: 12 -> 14, of which waited for: 6 -> 6; matrix products, arithmetic and copies ran while one was open for 0% -> 0% of each run, Pallas kernels for 3% -> 7%
where the time goes in v3:
time: 56.9 us; the launch traced here: 56.7 us
  Pallas kernels  20.7 us (36%)
  waiting for transfers between devices  20.1 us (35%)
  starting transfers between devices  13.3 us (23%)
  local copies, waits for them, and re-layouts  1.75 us (3%)
  between operations  0.74 us (1%)
    pallas_call x8, Pallas kernels, call(): pl.pallas_call(body, out_shape=shapes, in_specs=[place] * len(arguments),...  20.7 us
    ppermute x7, waiting for transfers between devices, swap_pairs(): far = lax.ppermute(far, ('gx', 'gy'), swaps[1])  20.1 us
    ppermute x7, starting transfers between devices, swap_pairs(): far = lax.ppermute(far, ('gx', 'gy'), swaps[1])  9.98 us
    ppermute x7, starting transfers between devices, swap_pairs(): near = lax.ppermute(near, ('gx', 'gy'), swaps[0])  3.33 us
    unnamed x14, local copies, waits for them, and re-layouts  1.68 us
  transfers between devices with their start and end apart: 14, of which 6 were waited for; matrix products, arithmetic and copies ran while one was open for 0% of the time, Pallas kernels for 7%

profile of v3, /device:TPU:102, one launch (start us, length us, event | category | flops | bytes accessed | tf_op | source)
XLA Modules:
  0.0 56.7 jit_solution(2492857478173979764)
XLA Ops:
  0.6 2.1 %shard_map.95 = (f32[656,128]{1,0:T(8,128)}, f32[656,128]{1,0:T(8,128)}) custom-call(f32[192,128]{1,0:T(8,128)} %bitcast.10, s32[64,128]{1,0:T(8,128)} %bitcast.12, s32[61,64,128]{2,1,0:T(8,128)} %bitcast.8), custom_call_target="tpu_custom_call" | custom-call | bytes 2801664 | tf_op jit(solution)/shard_map/pallas_call | solution.py:494
  2.8 0.9 %collective-permute-start = (f32[656,128]{1,0:T(8,128)}, f32[656,128]{1,0:T(8,128)S(1)}, u32[]{:S(2)}, u32[]{:S(2)}) collective-permute-start(f32[656,128]{1,0:T(8,128)} %get-tuple-element.42), channel_id=1, source_target_pairs={{0,1},{32,64},{64,32},{96,128},{128,96},{160,192},{192,160},{224,2... | collective-permute-start | bytes 1007624 | tf_op jit(solution)/shard_map/ppermute | solution.py:525
  3.7 0.9 %collective-permute-start.1 = (f32[656,128]{1,0:T(8,128)}, f32[656,128]{1,0:T(8,128)S(1)}, u32[]{:S(2)}, u32[]{:S(2)}) collective-permute-start(f32[656,128]{1,0:T(8,128)} %get-tuple-element.43), channel_id=1, source_target_pairs={{0,32},{32,0},{64,96},{96,64},{128,160},{160,128},{192,224},{224,1... | collective-permute-start | bytes 1007624 | tf_op jit(solution)/shard_map/ppermute | solution.py:526
  4.6 0.9 %copy-done.1 = f32[3,8,8,128]{3,2,1,0:T(8,128)S(1)} copy-done((f32[3,8,8,128]{3,2,1,0:T(8,128)S(1)}, f32[3,8,8,128]{3,2,1,0:T(8,128)}, u32[]{:S(2)}) %copy-start.1) | copy-done | bytes 98328
  5.5 0.8 %copy-done.2 = s32[8,8,128]{2,1,0:T(8,128)S(1)} copy-done((s32[8,8,128]{2,1,0:T(8,128)S(1)}, s32[8,8,128]{2,1,0:T(8,128)}, u32[]{:S(2)}) %copy-start.2) | copy-done | bytes 32792
  6.2 1.2 %shard_map.94 = (f32[4464,128]{1,0:T(8,128)S(1)}, f32[6832,128]{1,0:T(8,128)S(1)}, f32[192,128]{1,0:T(8,128)S(1)}, f32[64,128]{1,0:T(8,128)S(1)}, f32[352,128]{1,0:T(8,128)S(1)}, /*index=5*/f32[352,128]{1,0:T(8,128)S(1)}) custom-call(f32[192,128]{1,0:T(8,128)S(1)} %bitcast.11, s32[64,128]{1,0:T(8,128)S(1)} %bitcast.13, s32[3904,128]{1,0:T(8,128)S(1)} %bitcast.9), custom_call_target="tpu_custom_call" | custom-call | flops 1998848 | bytes 8404992 | tf_op jit(solution)/shard_map/pallas_call | solution.py:494
  7.5 3.1 %collective-permute-start.4 = (f32[352,128]{1,0:T(8,128)S(1)}, f32[352,128]{1,0:T(8,128)S(1)}, u32[]{:S(2)}, u32[]{:S(2)}) collective-permute-start(f32[352,128]{1,0:T(8,128)S(1)} %get-tuple-element.52), channel_id=1, source_target_pairs={{0,32},{1,2},{2,1},{3,4},{4,3},{5,6},{6,5},{7,8},{8,7},{9,10},{10,... | collective-permute-start | bytes 540680 | tf_op jit(solution)/shard_map/ppermute | solution.py:525
  10.6 3.0 %shard_map.96 = (f32[384,128]{1,0:T(8,128)S(1)}, f32[128,128]{1,0:T(8,128)S(1)}, f32[64,128]{1,0:T(8,128)S(1)}, f32[256,128]{1,0:T(8,128)S(1)}, f32[256,128]{1,0...) custom-call(f32[192,128]{1,0:T(8,128)S(1)} %get-tuple-element.40.u, ...), custom_call_target="tpu_custom_call", output_to_operand_aliasing={{5}: (4, {}), {6}: (5, {})} | custom-call | bytes 12926976 | tf_op jit(solution)/shard_map/pallas_call | solution.py:494
  13.6 0.0 copy-start.5
  13.6 0.0 copy-start.6
  13.6 0.0 copy-start.3
  13.6 3.1 %collective-permute-start.2 = (f32[256,128]{1,0:T(8,128)S(1)}, f32[256,128]{1,0:T(8,128)S(1)}, u32[]{:S(2)}, u32[]{:S(2)}) collective-permute-start(f32[256,128]{1,0:T(8,128)S(1)} %get-tuple-element.50), channel_id=1, source_target_pairs={{0,32},{1,2},{2,1},{3,4},{4,3},{5,6},{6,5},{7,8},{8,7},{9,10},{10,... | collective-permute-start | bytes 393224 | tf_op jit(solution)/shard_map/ppermute | solution.py:525
  16.7 0.6 %collective-permute-done.4.rest_0_ = f32[352,128]{1,0:T(8,128)S(1)} collective-permute-done((f32[352,128]{1,0:T(8,128)S(1)}, f32[352,128]{1,0:T(8,128)S(1)}, u32[]{:S(2)}, u32[]{:S(2)}) %collective-permute-start.4) | collective-permute-done | bytes 180256 | tf_op jit(solution)/shard_map/ppermute | solution.py:525
  17.3 5.2 %collective-permute-done.2.near = f32[256,128]{1,0:T(8,128)S(1)} collective-permute-done((f32[256,128]{1,0:T(8,128)S(1)}, f32[256,128]{1,0:T(8,128)S(1)}, u32[]{:S(2)}, u32[]{:S(2)}) %collective-permute-start.2) | collective-permute-done | bytes 131104 | tf_op jit(solution)/shard_map/ppermute | solution.py:525
  22.5 1.3 %shard_map.97 = (f32[112,128]{1,0:T(8,128)S(1)}, f32[48,128]{1,0:T(8,128)S(1)}, f32[48,128]{1,0:T(8,128)S(1)}, f32[608,128]{1,0:T(8,128)S(1)}, f32[608,128]{1,0:T(8,128)S(1)}, /*index=5*/f32[6832,128]{1,0:T(8,128)S(1)}) custom-call(f32[384,128]{1,0:T(8,128)S(1)} %get-tuple-element.46.wide, f32[4464,128]{1,0:T(8,128)S(1)} %get-tuple-element.47.flags, ...), custom_call_target="tpu_custom_call" | custom-call | bytes 10862592 | tf_op jit(solution)/shard_map/pallas_call | solution.py:494
  23.8 0.1 collective-permute-start.6
  23.9 1.4 %collective-permute-start.7 = (f32[48,128]{1,0:T(8,128)S(1)}, f32[48,128]{1,0:T(8,128)S(1)}, u32[]{:S(2)}, u32[]{:S(2)}) collective-permute-start(f32[48,128]{1,0:T(8,128)S(1)} %get-tuple-element.59), channel_id=1, source_target_pairs={{0,32},{32,0},{64,96},{96,64},{128,160},{160,128},{192,224},{224,1... | collective-permute-start | bytes 73736 | tf_op jit(solution)/shard_map/ppermute | solution.py:526
  25.2 0.1 pad_maximum_fusion
  25.3 2.4 %collective-permute-done.6.near = f32[48,128]{1,0:T(8,128)S(1)} collective-permute-done((f32[48,128]{1,0:T(8,128)S(1)}, f32[48,128]{1,0:T(8,128)S(1)}, u32[]{:S(2)}, u32[]{:S(2)}) %collective-permute-start.6) | collective-permute-done | bytes 24608 | tf_op jit(solution)/shard_map/ppermute | solution.py:525
  27.7 0.1 broadcast_in_dim.2.table
  27.8 4.3 %shard_map.98 = (f32[192,128]{1,0:T(8,128)S(1)}, f32[192,128]{1,0:T(8,128)S(1)}, f32[72,128]{1,0:T(8,128)S(1)}, f32[72,128]{1,0:T(8,128)S(1)}) custom-call(f32[24,128]{1,0:T(8,128)S(1)} %broadcast_in_dim.2.table, f32[192,128]{1,0:T(8,128)S(1)} %get-tuple-element.40.u, f32[192,128]{1,0:T(8,128)S(1)} %bitcast.14, f32[384,128]{1,0:T(8,128)S(1)} %get-tuple-element.46.wide, ...), custom_call_target="tpu_custom_call" | custom-call | bytes 7876608 | tf_op jit(solution)/shard_map/pallas_call | solution.py:494
  32.1 0.1 collective-permute-start.8
  32.2 0.8 %collective-permute-start.9 = (f32[72,128]{1,0:T(8,128)S(1)}, f32[72,128]{1,0:T(8,128)S(1)}, u32[]{:S(2)}, u32[]{:S(2)}) collective-permute-start(f32[72,128]{1,0:T(8,128)S(1)} %get-tuple-element.64), channel_id=1, source_target_pairs={{0,32},{32,0},{64,96},{96,64},{128,160},{160,128},{192,224},{224,1... | collective-permute-start | bytes 110600 | tf_op jit(solution)/shard_map/ppermute | solution.py:526
  33.0 3.1 %collective-permute-done.8.near = f32[72,128]{1,0:T(8,128)S(1)} collective-permute-done((f32[72,128]{1,0:T(8,128)S(1)}, f32[72,128]{1,0:T(8,128)S(1)}, u32[]{:S(2)}, u32[]{:S(2)}) %collective-permute-start.8) | collective-permute-done | bytes 36896 | tf_op jit(solution)/shard_map/ppermute | solution.py:525
  36.1 2.8 %shard_map.99 = (f32[384,128]{1,0:T(8,128)S(1)}, f32[64,128]{1,0:T(8,128)S(1)}, f32[168,128]{1,0:T(8,128)S(1)}, f32[168,128]{1,0:T(8,128)S(1)}) custom-call(f32[192,128]{1,0:T(8,128)S(1)} %get-tuple-element.61.u, f32[72,128]{1,0:T(8,128)S(1)} %collective-permute-done.8.near, f32[72,128]{1,0:T(8,128)S(1)} %collective-permute-done.9.far, ...), custom_call_target="tpu_custom_call" | custom-call | bytes 6356992 | tf_op jit(solution)/shard_map/pallas_call | solution.py:494
  39.0 2.6 %collective-permute-start.10 = (f32[168,128]{1,0:T(8,128)S(1)}, f32[168,128]{1,0:T(8,128)S(1)}, u32[]{:S(2)}, u32[]{:S(2)}) collective-permute-start(f32[168,128]{1,0:T(8,128)S(1)} %get-tuple-element.67), channel_id=1, source_target_pairs={{0,32},{1,2},{2,1},{3,4},{4,3},{5,6},{6,5},{7,8},{8,7},{9,10},{10,... | collective-permute-start | bytes 258056 | tf_op jit(solution)/shard_map/ppermute | solution.py:525
  41.6 5.3 %collective-permute-done.10.near = f32[168,128]{1,0:T(8,128)S(1)} collective-permute-done((f32[168,128]{1,0:T(8,128)S(1)}, f32[168,128]{1,0:T(8,128)S(1)}, u32[]{:S(2)}, u32[]{:S(2)}) %collective-permute-start.10) | collective-permute-done | bytes 86048 | tf_op jit(solution)/shard_map/ppermute | solution.py:525
  46.9 0.8 %shard_map.100 = (f32[112,128]{1,0:T(8,128)S(1)}, f32[48,128]{1,0:T(8,128)S(1)}, f32[48,128]{1,0:T(8,128)S(1)}, f32[168,128]{1,0:T(8,128)S(1)}, f32[168,128]{1,0:T(8,128)S(1)}) custom-call(f32[384,128]{1,0:T(8,128)S(1)} %get-tuple-element.65.wide, f32[4464,128]{1,0:T(8,128)S(1)} %get-tuple-element.47.flags, f32[6832,128]{1,0:T(8,128)S(1)} %get-tuple-element.60.incoming, ...), custom_call_target="tpu_custom_call" | custom-call | bytes 7086080 | tf_op jit(solution)/shard_map/pallas_call | solution.py:494
  47.7 0.1 collective-permute-start.12
  47.8 0.3 collective-permute-start.13
  48.1 3.5 %collective-permute-done.12.near = f32[48,128]{1,0:T(8,128)S(1)} collective-permute-done((f32[48,128]{1,0:T(8,128)S(1)}, f32[48,128]{1,0:T(8,128)S(1)}, u32[]{:S(2)}, u32[]{:S(2)}) %collective-permute-start.12) | collective-permute-done | bytes 24608 | tf_op jit(solution)/shard_map/ppermute | solution.py:525
  51.6 5.0 %shard_map.101 = (f32[192,128]{1,0:T(8,128)}, f32[192,128]{1,0:T(8,128)}, f32[192,128]{1,0:T(8,128)}) custom-call(f32[24,128]{1,0:T(8,128)S(1)} %broadcast_in_dim.2.table, f32[192,128]{1,0:T(8,128)S(1)} %get-tuple-element.61.u, f32[192,128]{1,0:T(8,128)S(1)} %get-tuple-element.62.v, f32[384,128]{1,0:T(8,128)S(1)} %get-tuple-element.65.wide, ...), custom_call_target="tpu_custom_call" | custom-call | bytes 7450624 | tf_op jit(solution)/shard_map/pallas_call | solution.py:494
  (20 shorter events, 0.0 us)
Async XLA Ops:
  0.6 3.9 %copy-start = (s32[61,8,8,128]{3,2,1,0:T(8,128)S(1)}, s32[61,8,8,128]{3,2,1,0:T(8,128)}, u32[]{:S(2)}) copy-start(s32[61,8,8,128]{3,2,1,0:T(8,128)} %param.9) | copy-start | bytes 5996548
  2.8 7.8 %collective-permute-start = (f32[656,128]{1,0:T(8,128)}, f32[656,128]{1,0:T(8,128)S(1)}, u32[]{:S(2)}, u32[]{:S(2)}) collective-permute-start(f32[656,128]{1,0:T(8,128)} %get-tuple-element.42), channel_id=1, source_target_pairs={{0,1},{32,64},{64,32},{96,128},{128,96},{160,192},{192,160},{224,2... | collective-permute-start | bytes 1007624 | tf_op jit(solution)/shard_map/ppermute | solution.py:525
  3.7 6.9 %collective-permute-start.1 = (f32[656,128]{1,0:T(8,128)}, f32[656,128]{1,0:T(8,128)S(1)}, u32[]{:S(2)}, u32[]{:S(2)}) collective-permute-start(f32[656,128]{1,0:T(8,128)} %get-tuple-element.43), channel_id=1, source_target_pairs={{0,32},{32,0},{64,96},{96,64},{128,160},{160,128},{192,224},{224,1... | collective-permute-start | bytes 1007624 | tf_op jit(solution)/shard_map/ppermute | solution.py:526
  4.6 0.9 %copy-start.1 = (f32[3,8,8,128]{3,2,1,0:T(8,128)S(1)}, f32[3,8,8,128]{3,2,1,0:T(8,128)}, u32[]{:S(2)}) copy-start(f32[3,8,8,128]{3,2,1,0:T(8,128)} %param.7) | copy-start | bytes 294916
  5.5 0.8 %copy-start.2 = (s32[8,8,128]{2,1,0:T(8,128)S(1)}, s32[8,8,128]{2,1,0:T(8,128)}, u32[]{:S(2)}) copy-start(s32[8,8,128]{2,1,0:T(8,128)} %param.10) | copy-start | bytes 98308
  7.5 9.9 %collective-permute-start.4 = (f32[352,128]{1,0:T(8,128)S(1)}, f32[352,128]{1,0:T(8,128)S(1)}, u32[]{:S(2)}, u32[]{:S(2)}) collective-permute-start(f32[352,128]{1,0:T(8,128)S(1)} %get-tuple-element.52), channel_id=1, source_target_pairs={{0,32},{1,2},{2,1},{3,4},{4,3},{5,6},{6,5},{7,8},{8,7},{9,10},{10,... | collective-permute-start | bytes 540680 | tf_op jit(solution)/shard_map/ppermute | solution.py:525
  10.6 6.7 %collective-permute-start.5 = (f32[352,128]{1,0:T(8,128)S(1)}, f32[352,128]{1,0:T(8,128)S(1)}, u32[]{:S(2)}, u32[]{:S(2)}) collective-permute-start(f32[352,128]{1,0:T(8,128)S(1)} %get-tuple-element.53), channel_id=1, source_target_pairs={{0,1},{1,0},{2,3},{3,2},{4,5},{5,4},{6,7},{7,6},{8,9},{9,8},{10,11... | collective-permute-start | bytes 540680 | tf_op jit(solution)/shard_map/ppermute | solution.py:526
  13.6 11.6 %copy-start.4 = (f32[8]{0:T(128)S(1)}, f32[8]{0:T(128)}, u32[]{:S(2)}) copy-start(f32[8]{0:T(128)} %param.13) | copy-start | bytes 100
  13.6 11.6 %copy-start.5 = (f32[8]{0:T(128)S(1)}, f32[8]{0:T(128)}, u32[]{:S(2)}) copy-start(f32[8]{0:T(128)} %param.12) | copy-start | bytes 100
  13.6 11.6 %copy-start.6 = (f32[8]{0:T(128)S(1)}, f32[8]{0:T(128)}, u32[]{:S(2)}) copy-start(f32[8]{0:T(128)} %param.11) | copy-start | bytes 100
  13.6 14.1 %copy-start.3 = (f32[3,8,8,128]{3,2,1,0:T(8,128)S(1)}, f32[3,8,8,128]{3,2,1,0:T(8,128)}, u32[]{:S(2)}) copy-start(f32[3,8,8,128]{3,2,1,0:T(8,128)} %param.8) | copy-start | bytes 294916
  13.6 8.8 %collective-permute-start.2 = (f32[256,128]{1,0:T(8,128)S(1)}, f32[256,128]{1,0:T(8,128)S(1)}, u32[]{:S(2)}, u32[]{:S(2)}) collective-permute-start(f32[256,128]{1,0:T(8,128)S(1)} %get-tuple-element.50), channel_id=1, source_target_pairs={{0,32},{1,2},{2,1},{3,4},{4,3},{5,6},{6,5},{7,8},{8,7},{9,10},{10,... | collective-permute-start | bytes 393224 | tf_op jit(solution)/shard_map/ppermute | solution.py:525
  16.7 5.8 %collective-permute-start.3 = (f32[256,128]{1,0:T(8,128)S(1)}, f32[256,128]{1,0:T(8,128)S(1)}, u32[]{:S(2)}, u32[]{:S(2)}) collective-permute-start(f32[256,128]{1,0:T(8,128)S(1)} %get-tuple-element.51), channel_id=1, source_target_pairs={{0,1},{1,0},{2,3},{3,2},{4,5},{5,4},{6,7},{7,6},{8,9},{9,8},{10,11... | collective-permute-start | bytes 393224 | tf_op jit(solution)/shard_map/ppermute | solution.py:526
  23.8 3.9 %collective-permute-start.6 = (f32[48,128]{1,0:T(8,128)S(1)}, f32[48,128]{1,0:T(8,128)S(1)}, u32[]{:S(2)}, u32[]{:S(2)}) collective-permute-start(f32[48,128]{1,0:T(8,128)S(1)} %get-tuple-element.58), channel_id=1, source_target_pairs={{0,1},{32,64},{64,32},{96,128},{128,96},{160,192},{192,160},{224,2... | collective-permute-start | bytes 73736 | tf_op jit(solution)/shard_map/ppermute | solution.py:525
  23.9 3.8 %collective-permute-start.7 = (f32[48,128]{1,0:T(8,128)S(1)}, f32[48,128]{1,0:T(8,128)S(1)}, u32[]{:S(2)}, u32[]{:S(2)}) collective-permute-start(f32[48,128]{1,0:T(8,128)S(1)} %get-tuple-element.59), channel_id=1, source_target_pairs={{0,32},{32,0},{64,96},{96,64},{128,160},{160,128},{192,224},{224,1... | collective-permute-start | bytes 73736 | tf_op jit(solution)/shard_map/ppermute | solution.py:526
  32.1 4.0 %collective-permute-start.8 = (f32[72,128]{1,0:T(8,128)S(1)}, f32[72,128]{1,0:T(8,128)S(1)}, u32[]{:S(2)}, u32[]{:S(2)}) collective-permute-start(f32[72,128]{1,0:T(8,128)S(1)} %get-tuple-element.63), channel_id=1, source_target_pairs={{0,1},{32,64},{64,32},{96,128},{128,96},{160,192},{192,160},{224,2... | collective-permute-start | bytes 110600 | tf_op jit(solution)/shard_map/ppermute | solution.py:525
  32.2 3.9 %collective-permute-start.9 = (f32[72,128]{1,0:T(8,128)S(1)}, f32[72,128]{1,0:T(8,128)S(1)}, u32[]{:S(2)}, u32[]{:S(2)}) collective-permute-start(f32[72,128]{1,0:T(8,128)S(1)} %get-tuple-element.64), channel_id=1, source_target_pairs={{0,32},{32,0},{64,96},{96,64},{128,160},{160,128},{192,224},{224,1... | collective-permute-start | bytes 110600 | tf_op jit(solution)/shard_map/ppermute | solution.py:526
  39.0 7.9 %collective-permute-start.10 = (f32[168,128]{1,0:T(8,128)S(1)}, f32[168,128]{1,0:T(8,128)S(1)}, u32[]{:S(2)}, u32[]{:S(2)}) collective-permute-start(f32[168,128]{1,0:T(8,128)S(1)} %get-tuple-element.67), channel_id=1, source_target_pairs={{0,32},{1,2},{2,1},{3,4},{4,3},{5,6},{6,5},{7,8},{8,7},{9,10},{10,... | collective-permute-start | bytes 258056 | tf_op jit(solution)/shard_map/ppermute | solution.py:525
  41.6 5.3 %collective-permute-start.11 = (f32[168,128]{1,0:T(8,128)S(1)}, f32[168,128]{1,0:T(8,128)S(1)}, u32[]{:S(2)}, u32[]{:S(2)}) collective-permute-start(f32[168,128]{1,0:T(8,128)S(1)} %get-tuple-element.68), channel_id=1, source_target_pairs={{0,1},{1,0},{2,3},{3,2},{4,5},{5,4},{6,7},{7,6},{8,9},{9,8},{10,11... | collective-permute-start | bytes 258056 | tf_op jit(solution)/shard_map/ppermute | solution.py:526
  47.7 3.9 %collective-permute-start.12 = (f32[48,128]{1,0:T(8,128)S(1)}, f32[48,128]{1,0:T(8,128)S(1)}, u32[]{:S(2)}, u32[]{:S(2)}) collective-permute-start(f32[48,128]{1,0:T(8,128)S(1)} %get-tuple-element.72), channel_id=1, source_target_pairs={{0,1},{32,64},{64,32},{96,128},{128,96},{160,192},{192,160},{224,2... | collective-permute-start | bytes 73736 | tf_op jit(solution)/shard_map/ppermute | solution.py:525
  47.8 3.8 %collective-permute-start.13 = (f32[48,128]{1,0:T(8,128)S(1)}, f32[48,128]{1,0:T(8,128)S(1)}, u32[]{:S(2)}, u32[]{:S(2)}) collective-permute-start(f32[48,128]{1,0:T(8,128)S(1)} %get-tuple-element.73), channel_id=1, source_target_pairs={{0,32},{32,0},{64,96},{96,64},{128,160},{160,128},{192,224},{224,1... | collective-permute-start | bytes 73736 | tf_op jit(solution)/shard_map/ppermute | solution.py:526

commit v4 on v3

--- a/solution.py
+++ b/solution.py
@@ -323,16 +323,19 @@
     return after[rows(48 * field + 16 * (column - 8) + 8 * half), :]
 
 
-def strip_theta(first, wide, flags, incoming, sums, near, far, *rest):
+def strip_theta(first, wide, flags, incoming, sums, own_shifts, near, far, *rest):
     place = position()
     if not first:
         before_flags, after_flags, *rest = rest
     else:
         early_near, early_far, *rest = rest
-    theta, near_x, far_x, before, after, *rest = rest
+    if first:
+        theta, near_x, far_x, before, after, shifts, *rest = rest
+    else:
+        theta, near_x, far_x, shifts, before, after, *rest = rest
     zero = place[3]
     if first:
-        all_incoming, shifts, up, down, early_before, early_after, late_before, late_after = rest
+        all_incoming, up, down, early_before, early_after, late_before, late_after = rest
         take_along_y(place, early_near, early_far, early_before, early_after)
         take_along_y(place, near, far, late_before, late_after)
         before_flags, after_flags = before, after
@@ -364,8 +367,8 @@
                     incoming[rows((k * 14 + 11 + n) * 8), :] = roll(tile, c)
     else:
         take_along_y(place, near, far, before, after)
-        shifts, up, down = rest
-    for column in (-3, -2, -1, 0, 1, 2, 5, 6, 7, 8, 9, 10):
+        up, down = rest
+    for column in (-3, -2, -1, 8, 9, 10):
         for n in range(3):
             for half in range(2):
                 tile = wide_tile(wide, before, after, n, column, half)
@@ -414,12 +417,12 @@
     return result
 
 
-def advance(last, table, u, v, wide, before, after, wide_material, before_material, after_material,
+def advance(last, table, u, v, shifts, wide_material, before_material, after_material,
             theta, near, far, flags, incoming, *rest):
     if last:
-        new_u, new_v, force, shifts, wide_theta, below, above = rest
+        new_u, new_v, force, loads, wide_theta, below, above = rest
     else:
-        new_u, new_v, near_x, far_x, shifts, wide_theta, below, above, up, down = rest
+        new_u, new_v, near_x, far_x, loads, wide_theta, below, above, up, down = rest
         force = None
     place = position()
     zero = place[3]
@@ -434,9 +437,6 @@
         wide_theta[rows(zero + at + 11, 3), :] = above[rows(zero + 3 * (column + 3), 3), :]
         wide_theta[rows(zero + at + 14, 2), :] = jnp.zeros((2, 128), F32)
         for half in range(2):
-            for n in range(3):
-                tile = wide_tile(wide, before, after, n, column, half)
-                store_shifts(shifts, n, 5, column, half, tile, n == 2)
             if column < 0:
                 number = before_material[rows(Y_MATERIAL + 16 * (column + 3) + 8 * half), :]
             elif column < 8:
@@ -445,20 +445,21 @@
                 number = after_material[rows(Y_MATERIAL + 16 * (column - 8) + 8 * half), :]
             twisting = pick(number, twist)
             pressing = pick(number, press) * wide_theta[rows(at + 8 * half), :] - twisting
-            store_shifts(shifts, 3, 5, column, half, pressing, False)
-            store_shifts(shifts, 4, 5, column, half, twisting, False)
+            store_shifts(loads, 0, 2, column, half, pressing, False)
+            store_shifts(loads, 1, 2, column, half, twisting, False)
 
     def column_force(y, carry):
-        own = [shifts[rows(shifted_row(n, 5, 0, y) + 3), :] for n in range(5)]
+        own = [shifts[rows(shifted_row(n, 3, 0, y) + 3), :] for n in range(3)]
+        own += [loads[rows(shifted_row(n, 2, 0, y) + 3), :] for n in range(2)]
         own_x = {a: own[0] - float(a) for a in range(-3, 4)}
         total = [jnp.zeros((8, 128), F32) for _ in range(3)]
         for b in range(-3, 4):
             own_y = own[1] - float(b)
             for a, c in directed(b):
-                *vector, square = pair_geometry(shifts, 5, y + b, a, c, own_x[a], own_y, own[2])
+                *vector, square = pair_geometry(shifts, 3, y + b, a, c, own_x[a], own_y, own[2])
                 inverse = lax.rsqrt(square)
-                pressing = shifts[rows(shifted_row(3, 5, c, y + b) + 3 + a), :] + own[3]
-                twisting = shifts[rows(shifted_row(4, 5, c, y + b) + 3 + a), :] + own[4]
+                pressing = loads[rows(shifted_row(0, 2, c, y + b) + 3 + a), :] + own[3]
+                twisting = loads[rows(shifted_row(1, 2, c, y + b) + 3 + a), :] + own[4]
                 if (a, b, c) > (0, 0, 0):
                     flag = flags[rows(FLAG_BASE[INDEX[a, b, c]] + y * (8 + a) + a), :]
                 else:
@@ -550,38 +551,41 @@
     )
     far, near = swap_pairs(far, near, "gx")
     early_far, early_near = swap_pairs(early_far, early_near, "gy")
-    wide, wide_material, sums, far, near, flags, incoming = call(
+    wide, wide_material, sums, far, near, flags, incoming, shifts = call(
         band_first,
-        [384, 128, 64, CORNER_ROWS, CORNER_ROWS, FLAG_ROWS, all_rows],
-        [7 * 3 * 224, X_UP_ROWS, X_DOWN_ROWS, CORNER_ROWS, CORNER_ROWS],
+        [384, 128, 64, CORNER_ROWS, CORNER_ROWS, FLAG_ROWS, all_rows, 7 * 3 * 224],
+        [X_UP_ROWS, X_DOWN_ROWS, CORNER_ROWS, CORNER_ROWS],
         u, material, far, near, flags, incoming, aliases={4: 5, 5: 6},
     )
     far, near = swap_pairs(far, near, "gy")
     for step in range(STEPS):
         if step:
             far, near = swap_pairs(far, near, "gx")
-            wide, sums, far, near = call(
-                band_next, [384, 64, Y_MATERIAL, Y_MATERIAL], [7 * 3 * 224, 72, 72, Y_MATERIAL, Y_MATERIAL],
+            wide, sums, far, near, shifts = call(
+                band_next, [384, 64, Y_MATERIAL, Y_MATERIAL, 7 * 3 * 224], [72, 72, Y_MATERIAL, Y_MATERIAL],
                 u, far, near, flags, incoming,
             )
             far, near = swap_pairs(far, near, "gy")
-            theta, far, near, before, after = call(
-                functools.partial(strip_theta, False), [112, 48, 48, Y_MATERIAL, Y_MATERIAL], [7 * 3 * 224, 48, 48],
-                wide, flags, incoming, sums, far, near, first_before, first_after,
+            theta, far, near, shifts = call(
+                functools.partial(strip_theta, False), [112, 48, 48, 7 * 3 * 224],
+                [Y_MATERIAL, Y_MATERIAL, 48, 48],
+                wide, flags, incoming, sums, shifts, far, near, first_before, first_after,
+                aliases={4: 3},
             )
         else:
-            theta, far, near, before, after, incoming = call(
-                functools.partial(strip_theta, True), [112, 48, 48, Y_ROWS, Y_ROWS, all_rows],
-                [7 * 3 * 224, 48, 48, EARLY_ROWS, EARLY_ROWS, CORNER_ROWS, CORNER_ROWS],
-                wide, flags, incoming, sums, far, near, early_far, early_near,
+            theta, far, near, before, after, shifts, incoming = call(
+                functools.partial(strip_theta, True), [112, 48, 48, Y_ROWS, Y_ROWS, 7 * 3 * 224, all_rows],
+                [48, 48, EARLY_ROWS, EARLY_ROWS, CORNER_ROWS, CORNER_ROWS],
+                wide, flags, incoming, sums, shifts, far, near, early_far, early_near,
+                aliases={4: 5},
             )
             first_before, first_after = before, after
         far, near = swap_pairs(far, near, "gx")
         last = step == STEPS - 1
         u, v, *more = call(
             functools.partial(advance, last), [192, 192] + ([192] if last else [72, 72]),
-            [7 * 5 * 224, 224, 48, 48] + ([] if last else [72, 72]),
-            table, u, v, wide, before, after, wide_material, first_before, first_after,
+            [7 * 2 * 224, 224, 48, 48] + ([] if last else [72, 72]),
+            table, u, v, shifts, wide_material, first_before, first_after,
             theta, far, near, flags, incoming,
         )
         if last:

time: 56.9 us -> 55.9 us (0.982)
  Pallas kernels: 20.7 us -> 19.7 us
    pallas_call x8, Pallas kernels: 20.7 us -> 19.7 us  [call(): pl.pallas_call(body, out_shape=shapes, in_specs=[place] * len(arguments),...]
  transfers between devices with their start and end apart: 14 -> 14, of which waited for: 6 -> 6; matrix products, arithmetic and copies ran while one was open for 0% -> 0% of each run, Pallas kernels for 7% -> 8%
where the time goes in v4:
time: 55.9 us; the launch traced here: 55.7 us
  waiting for transfers between devices  20.1 us (36%)
  Pallas kernels  19.7 us (35%)
  starting transfers between devices  13.3 us (24%)
  local copies, waits for them, and re-layouts  1.74 us (3%)
  between operations  0.72 us (1%)
    ppermute x7, waiting for transfers between devices, swap_pairs(): far = lax.ppermute(far, ('gx', 'gy'), swaps[1])  20.1 us
    pallas_call x8, Pallas kernels, call(): pl.pallas_call(body, out_shape=shapes, in_specs=[place] * len(arguments),...  19.7 us
    ppermute x7, starting transfers between devices, swap_pairs(): far = lax.ppermute(far, ('gx', 'gy'), swaps[1])  9.96 us
    ppermute x7, starting transfers between devices, swap_pairs(): near = lax.ppermute(near, ('gx', 'gy'), swaps[0])  3.33 us
    unnamed x14, local copies, waits for them, and re-layouts  1.67 us
  transfers between devices with their start and end apart: 14, of which 6 were waited for; matrix products, arithmetic and copies ran while one was open for 0% of the time, Pallas kernels for 8%

profile of v4, /device:TPU:102, one launch (start us, length us, event | category | flops | bytes accessed | tf_op | source)
XLA Modules:
  0.0 55.7 jit_solution(11376197238279655617)
XLA Ops:
  0.6 2.1 %shard_map.95 = (f32[656,128]{1,0:T(8,128)}, f32[656,128]{1,0:T(8,128)}) custom-call(f32[192,128]{1,0:T(8,128)} %bitcast.10, s32[64,128]{1,0:T(8,128)} %bitcast.12, s32[61,64,128]{2,1,0:T(8,128)} %bitcast.8), custom_call_target="tpu_custom_call" | custom-call | bytes 2801664 | tf_op jit(solution)/shard_map/pallas_call | solution.py:495
  2.8 0.9 %collective-permute-start = (f32[656,128]{1,0:T(8,128)}, f32[656,128]{1,0:T(8,128)S(1)}, u32[]{:S(2)}, u32[]{:S(2)}) collective-permute-start(f32[656,128]{1,0:T(8,128)} %get-tuple-element.44), channel_id=1, source_target_pairs={{0,1},{32,64},{64,32},{96,128},{128,96},{160,192},{192,160},{224,2... | collective-permute-start | bytes 1007624 | tf_op jit(solution)/shard_map/ppermute | solution.py:526
  3.7 0.9 %collective-permute-start.1 = (f32[656,128]{1,0:T(8,128)}, f32[656,128]{1,0:T(8,128)S(1)}, u32[]{:S(2)}, u32[]{:S(2)}) collective-permute-start(f32[656,128]{1,0:T(8,128)} %get-tuple-element.45), channel_id=1, source_target_pairs={{0,32},{32,0},{64,96},{96,64},{128,160},{160,128},{192,224},{224,1... | collective-permute-start | bytes 1007624 | tf_op jit(solution)/shard_map/ppermute | solution.py:527
  4.6 0.9 %copy-done.1 = f32[3,8,8,128]{3,2,1,0:T(8,128)S(1)} copy-done((f32[3,8,8,128]{3,2,1,0:T(8,128)S(1)}, f32[3,8,8,128]{3,2,1,0:T(8,128)}, u32[]{:S(2)}) %copy-start.1) | copy-done | bytes 98328
  5.5 0.8 %copy-done.2 = s32[8,8,128]{2,1,0:T(8,128)S(1)} copy-done((s32[8,8,128]{2,1,0:T(8,128)S(1)}, s32[8,8,128]{2,1,0:T(8,128)}, u32[]{:S(2)}) %copy-start.2) | copy-done | bytes 32792
  6.2 1.2 %shard_map.94 = (f32[4464,128]{1,0:T(8,128)S(1)}, f32[6832,128]{1,0:T(8,128)S(1)}, f32[192,128]{1,0:T(8,128)S(1)}, f32[64,128]{1,0:T(8,128)S(1)}, f32[352,128]{1,0:T(8,128)S(1)}, /*index=5*/f32[352,128]{1,0:T(8,128)S(1)}) custom-call(f32[192,128]{1,0:T(8,128)S(1)} %bitcast.11, s32[64,128]{1,0:T(8,128)S(1)} %bitcast.13, s32[3904,128]{1,0:T(8,128)S(1)} %bitcast.9), custom_call_target="tpu_custom_call" | custom-call | flops 1998848 | bytes 8404992 | tf_op jit(solution)/shard_map/pallas_call | solution.py:495
  7.5 3.1 %collective-permute-start.4 = (f32[352,128]{1,0:T(8,128)S(1)}, f32[352,128]{1,0:T(8,128)S(1)}, u32[]{:S(2)}, u32[]{:S(2)}) collective-permute-start(f32[352,128]{1,0:T(8,128)S(1)} %get-tuple-element.55), channel_id=1, source_target_pairs={{0,32},{1,2},{2,1},{3,4},{4,3},{5,6},{6,5},{7,8},{8,7},{9,10},{10,... | collective-permute-start | bytes 540680 | tf_op jit(solution)/shard_map/ppermute | solution.py:526
  10.6 0.0 collective-permute-done.near
  10.6 0.0 collective-permute-done.1.far
  10.6 3.0 %shard_map.96 = (f32[384,128]{1,0:T(8,128)S(1)}, f32[128,128]{1,0:T(8,128)S(1)}, f32[64,128]{1,0:T(8,128)S(1)}, f32[256,128]{1,0:T(8,128)S(1)}, f32[256,128]{1,0...) custom-call(f32[192,128]{1,0:T(8,128)S(1)} %get-tuple-element.42.u, ...), custom_call_target="tpu_custom_call", output_to_operand_aliasing={{5}: (4, {}), {6}: (5, {})} | custom-call | bytes 15335424 | tf_op jit(solution)/shard_map/pallas_call | solution.py:495
  13.6 3.1 %collective-permute-start.2 = (f32[256,128]{1,0:T(8,128)S(1)}, f32[256,128]{1,0:T(8,128)S(1)}, u32[]{:S(2)}, u32[]{:S(2)}) collective-permute-start(f32[256,128]{1,0:T(8,128)S(1)} %get-tuple-element.53), channel_id=1, source_target_pairs={{0,32},{1,2},{2,1},{3,4},{4,3},{5,6},{6,5},{7,8},{8,7},{9,10},{10,... | collective-permute-start | bytes 393224 | tf_op jit(solution)/shard_map/ppermute | solution.py:526
  16.7 0.7 %collective-permute-done.4.rest_0_ = f32[352,128]{1,0:T(8,128)S(1)} collective-permute-done((f32[352,128]{1,0:T(8,128)S(1)}, f32[352,128]{1,0:T(8,128)S(1)}, u32[]{:S(2)}, u32[]{:S(2)}) %collective-permute-start.4) | collective-permute-done | bytes 180256 | tf_op jit(solution)/shard_map/ppermute | solution.py:526
  17.3 5.1 %collective-permute-done.2.near = f32[256,128]{1,0:T(8,128)S(1)} collective-permute-done((f32[256,128]{1,0:T(8,128)S(1)}, f32[256,128]{1,0:T(8,128)S(1)}, u32[]{:S(2)}, u32[]{:S(2)}) %collective-permute-start.2) | collective-permute-done | bytes 131104 | tf_op jit(solution)/shard_map/ppermute | solution.py:526
  22.5 0.0 copy-start.3
  22.5 1.3 %shard_map.97 = (f32[112,128]{1,0:T(8,128)S(1)}, f32[48,128]{1,0:T(8,128)S(1)}, f32[48,128]{1,0:T(8,128)S(1)}, f32[608,128]{1,0:T(8,128)S(1)}, f32[608,128]{1,0:...) custom-call(f32[384,128]{1,0:T(8,128)S(1)} %get-tuple-element.48.wide, ...), custom_call_target="tpu_custom_call", output_to_operand_aliasing={{5}: (4, {})} | custom-call | bytes 15679488 | tf_op jit(solution)/shard_map/pallas_call | solution.py:495
  23.7 0.1 collective-permute-start.6
  23.8 1.4 %collective-permute-start.7 = (f32[48,128]{1,0:T(8,128)S(1)}, f32[48,128]{1,0:T(8,128)S(1)}, u32[]{:S(2)}, u32[]{:S(2)}) collective-permute-start(f32[48,128]{1,0:T(8,128)S(1)} %get-tuple-element.63), channel_id=1, source_target_pairs={{0,32},{32,0},{64,96},{96,64},{128,160},{160,128},{192,224},{224,1... | collective-permute-start | bytes 73736 | tf_op jit(solution)/shard_map/ppermute | solution.py:527
  25.2 0.1 pad_maximum_fusion
  25.3 2.4 %collective-permute-done.6.near = f32[48,128]{1,0:T(8,128)S(1)} collective-permute-done((f32[48,128]{1,0:T(8,128)S(1)}, f32[48,128]{1,0:T(8,128)S(1)}, u32[]{:S(2)}, u32[]{:S(2)}) %collective-permute-start.6) | collective-permute-done | bytes 24608 | tf_op jit(solution)/shard_map/ppermute | solution.py:526
  27.6 0.1 broadcast_in_dim.2.table
  27.7 3.8 %shard_map.98 = (f32[192,128]{1,0:T(8,128)S(1)}, f32[192,128]{1,0:T(8,128)S(1)}, f32[72,128]{1,0:T(8,128)S(1)}, f32[72,128]{1,0:T(8,128)S(1)}) custom-call(f32[24,128]{1,0:T(8,128)S(1)} %broadcast_in_dim.2.table, f32[192,128]{1,0:T(8,128)S(1)} %get-tuple-element.42.u, f32[192,128]{1,0:T(8,128)S(1)} %bitcast.14, f32[4704,128]{1,0:T(8,128)S(1)} %get-tuple-element.57.shifts, ...), custom_call_target="tpu_custom_call" | custom-call | bytes 9465856 | tf_op jit(solution)/shard_map/pallas_call | solution.py:495
  31.5 0.1 collective-permute-start.8
  31.6 0.8 %collective-permute-start.9 = (f32[72,128]{1,0:T(8,128)S(1)}, f32[72,128]{1,0:T(8,128)S(1)}, u32[]{:S(2)}, u32[]{:S(2)}) collective-permute-start(f32[72,128]{1,0:T(8,128)S(1)} %get-tuple-element.68), channel_id=1, source_target_pairs={{0,32},{32,0},{64,96},{96,64},{128,160},{160,128},{192,224},{224,1... | collective-permute-start | bytes 110600 | tf_op jit(solution)/shard_map/ppermute | solution.py:527
  32.4 3.1 %collective-permute-done.8.near = f32[72,128]{1,0:T(8,128)S(1)} collective-permute-done((f32[72,128]{1,0:T(8,128)S(1)}, f32[72,128]{1,0:T(8,128)S(1)}, u32[]{:S(2)}, u32[]{:S(2)}) %collective-permute-start.8) | collective-permute-done | bytes 36896 | tf_op jit(solution)/shard_map/ppermute | solution.py:526
  35.6 2.9 %shard_map.99 = (f32[384,128]{1,0:T(8,128)S(1)}, f32[64,128]{1,0:T(8,128)S(1)}, f32[168,128]{1,0:T(8,128)S(1)}, f32[168,128]{1,0:T(8,128)S(1)}, f32[4704,128]{1,0:T(8,128)S(1)}) custom-call(f32[192,128]{1,0:T(8,128)S(1)} %get-tuple-element.65.u, f32[72,128]{1,0:T(8,128)S(1)} %collective-permute-done.8.near, f32[72,128]{1,0:T(8,128)S(1)} %collective-permute-done.9.far, ...), custom_call_target="tpu_custom_call" | custom-call | bytes 8765440 | tf_op jit(solution)/shard_map/pallas_call | solution.py:495
  38.4 2.6 %collective-permute-start.10 = (f32[168,128]{1,0:T(8,128)S(1)}, f32[168,128]{1,0:T(8,128)S(1)}, u32[]{:S(2)}, u32[]{:S(2)}) collective-permute-start(f32[168,128]{1,0:T(8,128)S(1)} %get-tuple-element.72), channel_id=1, source_target_pairs={{0,32},{1,2},{2,1},{3,4},{4,3},{5,6},{6,5},{7,8},{8,7},{9,10},{10,... | collective-permute-start | bytes 258056 | tf_op jit(solution)/shard_map/ppermute | solution.py:526
  41.0 5.3 %collective-permute-done.10.near = f32[168,128]{1,0:T(8,128)S(1)} collective-permute-done((f32[168,128]{1,0:T(8,128)S(1)}, f32[168,128]{1,0:T(8,128)S(1)}, u32[]{:S(2)}, u32[]{:S(2)}) %collective-permute-start.10) | collective-permute-done | bytes 86048 | tf_op jit(solution)/shard_map/ppermute | solution.py:526
  46.3 0.8 %shard_map.100 = (f32[112,128]{1,0:T(8,128)S(1)}, f32[48,128]{1,0:T(8,128)S(1)}, f32[48,128]{1,0:T(8,128)S(1)}, f32[4704,128]{1,0:T(8,128)S(1)}) custom-call(f32[384,128]{1,0:T(8,128)S(1)} %get-tuple-element.69.wide, f32[4464,128]{1,0:T(8,128)S(1)} %get-tuple-element.49.flags, ...), custom_call_target="tpu_custom_call", output_to_operand_aliasing={{3}: (4, {})} | custom-call | bytes 11730944 | tf_op jit(solution)/shard_map/pallas_call | solution.py:495
  47.2 0.1 collective-permute-start.12
  47.2 0.3 collective-permute-start.13
  47.5 3.5 %collective-permute-done.12.near = f32[48,128]{1,0:T(8,128)S(1)} collective-permute-done((f32[48,128]{1,0:T(8,128)S(1)}, f32[48,128]{1,0:T(8,128)S(1)}, u32[]{:S(2)}, u32[]{:S(2)}) %collective-permute-start.12) | collective-permute-done | bytes 24608 | tf_op jit(solution)/shard_map/ppermute | solution.py:526
  51.1 4.6 %shard_map.101 = (f32[192,128]{1,0:T(8,128)}, f32[192,128]{1,0:T(8,128)}, f32[192,128]{1,0:T(8,128)}) custom-call(f32[24,128]{1,0:T(8,128)S(1)} %broadcast_in_dim.2.table, f32[192,128]{1,0:T(8,128)S(1)} %get-tuple-element.65.u, f32[192,128]{1,0:T(8,128)S(1)} %get-tuple-element.66.v, f32[4704,128]{1,0:T(8,128)S(1)} %get-tuple-element.74.shifts, ...), custom_call_target="tpu_custom_call" | custom-call | bytes 9490432 | tf_op jit(solution)/shard_map/pallas_call | solution.py:495
  (20 shorter events, 0.0 us)
Async XLA Ops:
  0.6 3.9 %copy-start = (s32[61,8,8,128]{3,2,1,0:T(8,128)S(1)}, s32[61,8,8,128]{3,2,1,0:T(8,128)}, u32[]{:S(2)}) copy-start(s32[61,8,8,128]{3,2,1,0:T(8,128)} %param.9) | copy-start | bytes 5996548
  2.8 7.8 %collective-permute-start = (f32[656,128]{1,0:T(8,128)}, f32[656,128]{1,0:T(8,128)S(1)}, u32[]{:S(2)}, u32[]{:S(2)}) collective-permute-start(f32[656,128]{1,0:T(8,128)} %get-tuple-element.44), channel_id=1, source_target_pairs={{0,1},{32,64},{64,32},{96,128},{128,96},{160,192},{192,160},{224,2... | collective-permute-start | bytes 1007624 | tf_op jit(solution)/shard_map/ppermute | solution.py:526
  3.7 6.9 %collective-permute-start.1 = (f32[656,128]{1,0:T(8,128)}, f32[656,128]{1,0:T(8,128)S(1)}, u32[]{:S(2)}, u32[]{:S(2)}) collective-permute-start(f32[656,128]{1,0:T(8,128)} %get-tuple-element.45), channel_id=1, source_target_pairs={{0,32},{32,0},{64,96},{96,64},{128,160},{160,128},{192,224},{224,1... | collective-permute-start | bytes 1007624 | tf_op jit(solution)/shard_map/ppermute | solution.py:527
  4.6 0.9 %copy-start.1 = (f32[3,8,8,128]{3,2,1,0:T(8,128)S(1)}, f32[3,8,8,128]{3,2,1,0:T(8,128)}, u32[]{:S(2)}) copy-start(f32[3,8,8,128]{3,2,1,0:T(8,128)} %param.7) | copy-start | bytes 294916
  5.5 0.8 %copy-start.2 = (s32[8,8,128]{2,1,0:T(8,128)S(1)}, s32[8,8,128]{2,1,0:T(8,128)}, u32[]{:S(2)}) copy-start(s32[8,8,128]{2,1,0:T(8,128)} %param.10) | copy-start | bytes 98308
  7.5 9.9 %collective-permute-start.4 = (f32[352,128]{1,0:T(8,128)S(1)}, f32[352,128]{1,0:T(8,128)S(1)}, u32[]{:S(2)}, u32[]{:S(2)}) collective-permute-start(f32[352,128]{1,0:T(8,128)S(1)} %get-tuple-element.55), channel_id=1, source_target_pairs={{0,32},{1,2},{2,1},{3,4},{4,3},{5,6},{6,5},{7,8},{8,7},{9,10},{10,... | collective-permute-start | bytes 540680 | tf_op jit(solution)/shard_map/ppermute | solution.py:526
  10.6 6.7 %collective-permute-start.5 = (f32[352,128]{1,0:T(8,128)S(1)}, f32[352,128]{1,0:T(8,128)S(1)}, u32[]{:S(2)}, u32[]{:S(2)}) collective-permute-start(f32[352,128]{1,0:T(8,128)S(1)} %get-tuple-element.56), channel_id=1, source_target_pairs={{0,1},{1,0},{2,3},{3,2},{4,5},{5,4},{6,7},{7,6},{8,9},{9,8},{10,11... | collective-permute-start | bytes 540680 | tf_op jit(solution)/shard_map/ppermute | solution.py:527
  13.6 8.8 %collective-permute-start.2 = (f32[256,128]{1,0:T(8,128)S(1)}, f32[256,128]{1,0:T(8,128)S(1)}, u32[]{:S(2)}, u32[]{:S(2)}) collective-permute-start(f32[256,128]{1,0:T(8,128)S(1)} %get-tuple-element.53), channel_id=1, source_target_pairs={{0,32},{1,2},{2,1},{3,4},{4,3},{5,6},{6,5},{7,8},{8,7},{9,10},{10,... | collective-permute-start | bytes 393224 | tf_op jit(solution)/shard_map/ppermute | solution.py:526
  16.7 5.8 %collective-permute-start.3 = (f32[256,128]{1,0:T(8,128)S(1)}, f32[256,128]{1,0:T(8,128)S(1)}, u32[]{:S(2)}, u32[]{:S(2)}) collective-permute-start(f32[256,128]{1,0:T(8,128)S(1)} %get-tuple-element.54), channel_id=1, source_target_pairs={{0,1},{1,0},{2,3},{3,2},{4,5},{5,4},{6,7},{7,6},{8,9},{9,8},{10,11... | collective-permute-start | bytes 393224 | tf_op jit(solution)/shard_map/ppermute | solution.py:527
  22.4 2.8 %copy-start.4 = (f32[8]{0:T(128)S(1)}, f32[8]{0:T(128)}, u32[]{:S(2)}) copy-start(f32[8]{0:T(128)} %param.13) | copy-start | bytes 100
  22.4 2.8 %copy-start.5 = (f32[8]{0:T(128)S(1)}, f32[8]{0:T(128)}, u32[]{:S(2)}) copy-start(f32[8]{0:T(128)} %param.12) | copy-start | bytes 100
  22.4 2.8 %copy-start.6 = (f32[8]{0:T(128)S(1)}, f32[8]{0:T(128)}, u32[]{:S(2)}) copy-start(f32[8]{0:T(128)} %param.11) | copy-start | bytes 100
  22.5 5.3 %copy-start.3 = (f32[3,8,8,128]{3,2,1,0:T(8,128)S(1)}, f32[3,8,8,128]{3,2,1,0:T(8,128)}, u32[]{:S(2)}) copy-start(f32[3,8,8,128]{3,2,1,0:T(8,128)} %param.8) | copy-start | bytes 294916
  23.7 3.9 %collective-permute-start.6 = (f32[48,128]{1,0:T(8,128)S(1)}, f32[48,128]{1,0:T(8,128)S(1)}, u32[]{:S(2)}, u32[]{:S(2)}) collective-permute-start(f32[48,128]{1,0:T(8,128)S(1)} %get-tuple-element.62), channel_id=1, source_target_pairs={{0,1},{32,64},{64,32},{96,128},{128,96},{160,192},{192,160},{224,2... | collective-permute-start | bytes 73736 | tf_op jit(solution)/shard_map/ppermute | solution.py:526
  23.8 3.8 %collective-permute-start.7 = (f32[48,128]{1,0:T(8,128)S(1)}, f32[48,128]{1,0:T(8,128)S(1)}, u32[]{:S(2)}, u32[]{:S(2)}) collective-permute-start(f32[48,128]{1,0:T(8,128)S(1)} %get-tuple-element.63), channel_id=1, source_target_pairs={{0,32},{32,0},{64,96},{96,64},{128,160},{160,128},{192,224},{224,1... | collective-permute-start | bytes 73736 | tf_op jit(solution)/shard_map/ppermute | solution.py:527
  31.5 4.0 %collective-permute-start.8 = (f32[72,128]{1,0:T(8,128)S(1)}, f32[72,128]{1,0:T(8,128)S(1)}, u32[]{:S(2)}, u32[]{:S(2)}) collective-permute-start(f32[72,128]{1,0:T(8,128)S(1)} %get-tuple-element.67), channel_id=1, source_target_pairs={{0,1},{32,64},{64,32},{96,128},{128,96},{160,192},{192,160},{224,2... | collective-permute-start | bytes 110600 | tf_op jit(solution)/shard_map/ppermute | solution.py:526
  31.6 3.9 %collective-permute-start.9 = (f32[72,128]{1,0:T(8,128)S(1)}, f32[72,128]{1,0:T(8,128)S(1)}, u32[]{:S(2)}, u32[]{:S(2)}) collective-permute-start(f32[72,128]{1,0:T(8,128)S(1)} %get-tuple-element.68), channel_id=1, source_target_pairs={{0,32},{32,0},{64,96},{96,64},{128,160},{160,128},{192,224},{224,1... | collective-permute-start | bytes 110600 | tf_op jit(solution)/shard_map/ppermute | solution.py:527
  38.4 7.9 %collective-permute-start.10 = (f32[168,128]{1,0:T(8,128)S(1)}, f32[168,128]{1,0:T(8,128)S(1)}, u32[]{:S(2)}, u32[]{:S(2)}) collective-permute-start(f32[168,128]{1,0:T(8,128)S(1)} %get-tuple-element.72), channel_id=1, source_target_pairs={{0,32},{1,2},{2,1},{3,4},{4,3},{5,6},{6,5},{7,8},{8,7},{9,10},{10,... | collective-permute-start | bytes 258056 | tf_op jit(solution)/shard_map/ppermute | solution.py:526
  41.0 5.3 %collective-permute-start.11 = (f32[168,128]{1,0:T(8,128)S(1)}, f32[168,128]{1,0:T(8,128)S(1)}, u32[]{:S(2)}, u32[]{:S(2)}) collective-permute-start(f32[168,128]{1,0:T(8,128)S(1)} %get-tuple-element.73), channel_id=1, source_target_pairs={{0,1},{1,0},{2,3},{3,2},{4,5},{5,4},{6,7},{7,6},{8,9},{9,8},{10,11... | collective-permute-start | bytes 258056 | tf_op jit(solution)/shard_map/ppermute | solution.py:527
  47.2 3.9 %collective-permute-start.12 = (f32[48,128]{1,0:T(8,128)S(1)}, f32[48,128]{1,0:T(8,128)S(1)}, u32[]{:S(2)}, u32[]{:S(2)}) collective-permute-start(f32[48,128]{1,0:T(8,128)S(1)} %get-tuple-element.76), channel_id=1, source_target_pairs={{0,1},{32,64},{64,32},{96,128},{128,96},{160,192},{192,160},{224,2... | collective-permute-start | bytes 73736 | tf_op jit(solution)/shard_map/ppermute | solution.py:526
  47.2 3.8 %collective-permute-start.13 = (f32[48,128]{1,0:T(8,128)S(1)}, f32[48,128]{1,0:T(8,128)S(1)}, u32[]{:S(2)}, u32[]{:S(2)}) collective-permute-start(f32[48,128]{1,0:T(8,128)S(1)} %get-tuple-element.77), channel_id=1, source_target_pairs={{0,32},{32,0},{64,96},{96,64},{128,160},{160,128},{192,224},{224,1... | collective-permute-start | bytes 73736 | tf_op jit(solution)/shard_map/ppermute | solution.py:527
